TPU v7x, 32 devices: a whole 2x2x4 slice. The times are simulated.
32 devices in a mesh: dp: 4 (over z), cls: 8 (over y, x, core).
Axes of the slice: x: 2, y: 2, z: 4, core: 2. Of those that a mesh axis runs over, the one named last changes fastest.
Arguments:
- embeddings: bfloat16 [2048, 512], P(('dp', 'cls')), may hold values from -6 to 6
- labels: int32 [2048], P('dp'), may hold values from 0 to 16383
- centres: bfloat16 [32768, 512], P('cls'), may hold values from -0.25 to 0.25
- momentum: float32 [32768, 512], P('cls'), may hold values from -3 to 3
- sample_home: int32 [16384, 1], P('cls'), may hold values from 0 to 7; in each aligned block of 2048 rows (0 to 2047, 2048 to 4095, ...) at most 512 rows name the same one
- sample_row: int32 [16384], P('cls'), may hold values from 0 to 4095
Outputs:
- emb_grad: float32 [2048, 512], P(('dp', 'cls'))
- momentum_new: float32 [32768, 512], P('cls')
- centres_new: bfloat16 [32768, 512], P('cls')
Inputs may be any that keep to these rules, and one draw needn't show every extreme that they name: Among the 2048 sampled columns of one class tile (aligned blocks of sample_home), at most 512 name the same home shard, and in every draw some home shard supplies exactly 512 columns of some tile.
All inputs are finite; a program needn't handle non-finite values.
Results may differ from a plain program's by a relative error of at most 0.014.
Values may be sent and summed in bfloat16 or wider, within the bound.
No kernel may reach another device: no remote copies, remote signals or barrier semaphores. Data moves between devices by JAX's collectives and lax.ppermute only.
A program may use at most 128 MiB of HBM per device.

v0:
```python
import jax
import jax.numpy as jnp
from jax import lax
from jax.sharding import PartitionSpec as P

eps = 1e-06
logit_scale = 64.0
margin = 0.35
momentum_rate = 0.9
learn_rate = 0.1
weight_decay = 0.0005


def body(embeddings, labels, centres, momentum, sample_home, sample_row):
    shards = lax.axis_size("cls")
    sampled_here = sample_row.shape[0]
    capacity = 2 * sampled_here // shards
    width = embeddings.shape[1]
    home_rows = centres.shape[0]
    xfloat = embeddings.astype(jnp.float32)
    row_norm = jnp.sqrt(jnp.sum(xfloat * xfloat, axis=1, keepdims=True) + eps)
    unit_centres = xfloat / row_norm
    normalized_embedding = unit_centres.astype(jnp.bfloat16)
    collected_centres = lax.all_gather(normalized_embedding, "cls", axis=0, tiled=True)
    home_shard = sample_home[:, 0]
    shard_ids = jnp.arange(shards, dtype=jnp.int32)
    home_onehot = (home_shard[:, None] == shard_ids[None, :]).astype(jnp.int32)
    slot_rank = jnp.sum(jnp.cumsum(home_onehot, axis=0) * home_onehot, axis=1) - 1
    request = jnp.zeros((shards, capacity), jnp.int32).at[home_shard, slot_rank].set(sample_row)
    incoming = lax.all_to_all(request, "cls", split_axis=0, concat_axis=0, tiled=True)
    replies = centres[incoming]
    arrived = lax.all_to_all(replies, "cls", split_axis=0, concat_axis=0, tiled=True)
    fetched = arrived[home_shard, slot_rank]
    wfloat = fetched.astype(jnp.float32)
    col_norm = jnp.sqrt(jnp.sum(wfloat * wfloat, axis=1, keepdims=True) + eps)
    wunit = wfloat / col_norm
    what = wunit.astype(jnp.bfloat16)
    cosine = lax.dot_general(
        collected_centres, what, (((1,), (1,)), ((), ())), preferred_element_type=jnp.float32
    )
    tile_index = lax.axis_index("cls")
    local_label = labels - tile_index * sampled_here
    column_ids = jnp.arange(sampled_here, dtype=jnp.int32)
    target = (local_label[:, None] == column_ids[None, :]).astype(jnp.float32)
    exp_logit = jnp.exp(logit_scale * (cosine - margin * target))
    denominator = lax.psum(jnp.sum(exp_logit, axis=1), "cls")
    grad_logit = (logit_scale * (exp_logit / denominator[:, None] - target)).astype(jnp.bfloat16)
    dunit = lax.psum_scatter(
        jnp.dot(grad_logit, what, preferred_element_type=jnp.float32).astype(jnp.bfloat16),
        "cls",
        scatter_dimension=0,
        tiled=True,
    ).astype(jnp.float32)
    emb_grad = (
        dunit - unit_centres * jnp.sum(unit_centres * dunit, axis=1, keepdims=True)
    ) / row_norm
    dwhat = lax.dot_general(
        grad_logit, collected_centres, (((0,), (0,)), ((), ())), preferred_element_type=jnp.float32
    )
    dfetched = (dwhat - wunit * jnp.sum(wunit * dwhat, axis=1, keepdims=True)) / col_norm
    summed = lax.psum(dfetched.astype(jnp.bfloat16), "dp").astype(jnp.float32)
    packed_buffer = (
        jnp.zeros((shards, capacity, width), jnp.float32).at[home_shard, slot_rank].set(summed)
    )
    returned = lax.all_to_all(
        packed_buffer.astype(jnp.bfloat16), "cls", split_axis=0, concat_axis=0, tiled=True
    ).astype(packed_buffer.dtype)
    centre_grad = (
        jnp.zeros((home_rows, width), jnp.float32)
        .at[incoming.reshape(-1)]
        .add(returned.reshape(-1, width))
    )
    centre_float = centres.astype(jnp.float32)
    momentum_new = momentum_rate * momentum + centre_grad + weight_decay * centre_float
    centres_new = (centre_float - learn_rate * momentum_new).astype(jnp.bfloat16)
    return (emb_grad, momentum_new, centres_new)


def solution(mesh):
    placed = (
        P(("dp", "cls"), None),
        P("dp"),
        P("cls", None),
        P("cls", None),
        P("cls", None),
        P("cls"),
    )
    return jax.shard_map(
        body,
        mesh=mesh,
        in_specs=placed,
        out_specs=(P(("dp", "cls"), None), P("cls", None), P("cls", None)),
        check_vma=False,
    )
```

profile of v0, /device:TPU:1, one launch (start us, length us, event | category | flops | bytes accessed | tf_op | source)
XLA Modules:
  0.0 392.5 jit_solution(12657059488806649129)
XLA Ops:
  8.0 0.7 fusion.13
  8.7 2.3 reduce-window.6
  11.0 0.3 slice_reduce_fusion
  11.3 0.2 reduce-window.9
  11.4 0.1 add_bitcast_fusion
  11.5 0.7 fusion.12
  12.3 0.7 shift-left_or_fusion
  13.0 0.8 and_reduce_fusion
  13.8 0.7 multiply_reduce_fusion.1
  14.5 8.2 %scatter_custom_fusion.1 = s32[4096]{0:T(1024)S(1)} fusion(s32[2048]{0:T(1024)S(1)} %broadcast_select_fusion, s32[2048]{0:T(1024)} %param.11, s32[]{:T(128)} %constant.16.clone.1), kind=kCustom, calls=%fused_computation.47 | custom fusion | bytes 16896
  22.8 9.0 %all_to_all.22 = s32[8,1,512]{2,1,0:T(1,128)S(1)} all-to-all(s32[8,1,512]{2,1,0:T(1,128)S(1)} %bitcast.42), channel_id=1, replica_groups=mesh['dp'=4,'cls'=8] {'cls'}, dimensions={0} | all-to-all | bytes 32768 | tf_op jit(solution)/shard_map/all_to_all | solution.py:30
  31.8 20.2 %gather_fusion = bf16[4096,512]{1,0:T(8,128)(2,1)} fusion(bf16[4096,512]{1,0:T(8,128)(2,1)} %param.8, s32[4096]{0:T(1024)S(1)} %broadcast_clamp_fusion), kind=kCustom, calls=%fused_computation | custom fusion | bytes 8404992 | tf_op jit(solution)/shard_map/gather | solution.py:31
  52.0 0.0 copy-start.2
  52.0 0.0 copy-start.3
  52.0 5.3 %all-to-all-start.1 = ((bf16[8,512,512]{2,1,0:T(8,128)(2,1)}), bf16[8,512,512]{2,1,0:T(8,128)(2,1)}, u32[]{:S(2)}, u32[]{:S(2)}) async-start(bf16[8,512,512]{2,1,0:T(8,128)(2,1)} %bitcast.38), calls=%async_computation.1 | async-start | bytes 8388608 | tf_op jit(solution)/shard_map/all_to_all | solution.py:32
  57.3 0.0 all-reduce.2.cloned.1.call-start
  57.3 0.0 copy-done.2
  57.3 0.1 fusion.8
  57.4 0.1 fusion.16
  57.6 53.1 %all_gather.3 = bf16[512,512]{1,0:T(8,128)(2,1)S(1)} all-gather(bf16[64,512]{1,0:T(8,128)(2,1)S(1)} %fusion.16), channel_id=1, replica_groups=mesh['dp'=4,'cls'=8] {'cls'}, dimensions={0}, use_global_device_ids=true | all-gather | bytes 589824 | tf_op jit(solution)/shard_map/all_gather | solution.py:24
  110.7 0.0 copy-done.3
  110.7 0.0 all-to-all-done.1
  110.7 37.2 %gather_fusion.1 = bf16[2048,512]{1,0:T(8,128)(2,1)} fusion(bf16[8,512,512]{2,1,0:T(8,128)(2,1)} %all-to-all-done.1, s32[2048]{0:T(1024)S(1)} %bitcast.36), kind=kCustom, calls=%fused_computation.1 | custom fusion | bytes 4210688 | tf_op jit(solution)/shard_map/gather | solution.py:33
  147.9 2.9 copy.10
  150.8 0.5 fusion.4
  151.2 3.8 fusion.19
  155.1 11.6 %psum.14 = f32[512]{0:T(512)S(1)} all-reduce(f32[512]{0:T(512)S(1)} %get-tuple-element.8), channel_id=1, replica_groups=mesh['dp'=4,'cls'=8] {'cls'}, use_global_device_ids=true, to_apply=%region_7.8 | all-reduce | flops 512 | bytes 4096 | tf_op jit(solution)/shard_map/psum | solution.py:46
  166.7 3.1 multiply_convert_fusion
  169.8 0.0 copy-start
  169.8 1.5 multiply_reduce_fusion
  171.4 0.0 copy-done
  171.4 2.3 divide_convert_fusion
  173.6 0.0 all-reduce.2.cloned.1.call-update
  173.7 86.7 %all-reduce.2.cloned.1.call-done = bf16[2048,512]{0,1:T(8,128)(2,1)} async-done(((bf16[2048,512]{0,1:T(8,128)(2,1)}), bf16[2048,512]{0,1:T(8,128)(2,1)}) %all-reduce.2.cloned.1.call-update) | async-done | bytes 2097168 | tf_op jit(solution)/shard_map/psum | solution.py:61
  260.3 4.1 %copy.11 = f32[2048,512]{1,0:T(8,128)} copy(bf16[2048,512]{0,1:T(8,128)(2,1)} %all-reduce.2.cloned.1.call-done) | data formatting | bytes 6291456 | tf_op jit(solution)/shard_map/convert_element_type | solution.py:61
  264.4 13.5 %scatter_custom_fusion.2 = f32[4096,512]{1,0:T(8,128)} fusion(s32[2048]{0:T(1024)S(1)} %broadcast_select_fusion, f32[2048,512]{1,0:T(8,128)} %copy.11, f32[]{:T(128)} %constant.14.clone.1), kind=kCustom, calls=%fused_computation.14 | custom fusion | bytes 8389120
  278.0 5.9 %convert_element_type.59 = bf16[4096,512]{1,0:T(8,128)(2,1)} convert(f32[4096,512]{1,0:T(8,128)} %scatter_custom_fusion.2) | non-fusion elementwise | flops 2097152 | bytes 12582912 | tf_op jit(solution)/shard_map/convert_element_type | solution.py:66
  283.9 5.4 %all-to-all-start.2 = ((bf16[8,512,512]{2,1,0:T(8,128)(2,1)}), bf16[8,512,512]{2,1,0:T(8,128)(2,1)}, u32[]{:S(2)}, u32[]{:S(2)}) async-start(bf16[8,512,512]{2,1,0:T(8,128)(2,1)} %bitcast.37), calls=%async_computation.3 | async-start | bytes 8388608 | tf_op jit(solution)/shard_map/all_to_all | solution.py:65
  289.3 0.0 reduce-scatter.2.cloned.1.call-start
  289.3 0.0 copy-start.1
  289.4 9.6 %fusion = f32[4096,512]{1,0:T(8,128)} fusion(bf16[4096,512]{1,0:T(8,128)(2,1)} %param.8, f32[4096,512]{1,0:T(8,128)} %param.9), kind=kLoop, calls=%fused_computation.7 | loop fusion | flops 8388608 | bytes 20971520 | tf_op jit(solution)/shard_map/add.2
  299.0 0.0 copy-done.1
  299.0 2.1 convolution_convert_fusion
  301.1 0.0 reduce-scatter.2.cloned.1.call-update
  301.1 37.6 %reduce-scatter.2.cloned.1.call-done = bf16[64,512]{1,0:T(8,128)(2,1)} async-done(((bf16[512,512]{1,0:T(8,128)(2,1)}), bf16[64,512]{1,0:T(8,128)(2,1)}) %reduce-scatter.2.cloned.1.call-update) | async-done | bytes 65552 | tf_op jit(solution)/shard_map/reduce_scatter | solution.py:48
  338.7 1.0 fusion.9
  339.8 1.6 fusion.10
  341.4 0.0 all-to-all-done.2
  341.4 35.5 %scatter_custom_fusion = f32[4096,512]{1,0:T(8,128)} fusion(f32[4096,512]{1,0:T(8,128)} %fusion, s32[4096]{0:T(1024)S(1)} %bitcast.47, bf16[4096,512]{1,0:T(8,128)(2,1)} %bitcast.14), kind=kCustom, calls=%fused_computation.9 | custom fusion | flops 4194304 | bytes 12582912 | tf_op jit(solution)/shard_map/scatter-add | solution.py:71
  376.9 8.1 %fusion.1 = bf16[4096,512]{1,0:T(8,128)(2,1)} fusion(bf16[4096,512]{1,0:T(8,128)(2,1)} %param.8, f32[4096,512]{1,0:T(8,128)} %scatter_custom_fusion), kind=kLoop, calls=%fused_computation.8 | loop fusion | flops 8388608 | bytes 16777216 | tf_op jit(solution)/shard_map/convert_element_type | solution.py:75
  (8 shorter events, 0.1 us)
Async XLA Ops:
  52.0 5.3 %copy-start.2 = (bf16[64,512]{1,0:T(8,128)(2,1)S(1)}, bf16[64,512]{1,0:T(8,128)(2,1)}, u32[]{:S(2)}) copy-start(bf16[64,512]{1,0:T(8,128)(2,1)} %param.6) | copy-start | bytes 196612
  52.0 58.6 %copy-start.3 = (s32[512]{0:T(512)S(1)}, s32[512]{0:T(512)}, u32[]{:S(2)}) copy-start(s32[512]{0:T(512)} %param.7) | copy-start | bytes 6148
  52.0 58.6 %all-to-all-start.1 = ((bf16[8,512,512]{2,1,0:T(8,128)(2,1)}), bf16[8,512,512]{2,1,0:T(8,128)(2,1)}, u32[]{:S(2)}, u32[]{:S(2)}) async-start(bf16[8,512,512]{2,1,0:T(8,128)(2,1)} %bitcast.38), calls=%async_computation.1 | async-start | bytes 8388608 | tf_op jit(solution)/shard_map/all_to_all | solution.py:32
  57.3 203.0 %all-reduce.2.cloned.1.call-start = ((), (), s32[]{:S(2)}) async-start(), calls=%async_computation.5 | async-start | bytes 4194304 | tf_op jit(solution)/shard_map/psum | solution.py:61
  169.8 1.5 copy-start
  283.9 57.5 %all-to-all-start.2 = ((bf16[8,512,512]{2,1,0:T(8,128)(2,1)}), bf16[8,512,512]{2,1,0:T(8,128)(2,1)}, u32[]{:S(2)}, u32[]{:S(2)}) async-start(bf16[8,512,512]{2,1,0:T(8,128)(2,1)} %bitcast.37), calls=%async_computation.3 | async-start | bytes 8388608 | tf_op jit(solution)/shard_map/all_to_all | solution.py:65
  289.3 49.4 %reduce-scatter.2.cloned.1.call-start = ((), (), s32[]{:S(2)}) async-start(), calls=%async_computation.4 | async-start | bytes 589824 | tf_op jit(solution)/shard_map/reduce_scatter | solution.py:48
  289.3 9.6 %copy-start.1 = (bf16[512,2048]{1,0:T(8,128)(2,1)S(1)}, bf16[512,2048]{1,0:T(8,128)(2,1)}, u32[]{:S(2)}) copy-start(bf16[512,2048]{1,0:T(8,128)(2,1)} %copy-done) | copy-start | bytes 6291460
Sparse Core Ops, SparseCore 0:
  173.8 86.5 all-reduce.1
Sparse Core Ops, SparseCore 1:
  301.2 37.5 reduce-scatter.1
where the time goes:
time: 394 us; the launch traced here: 392 us
  waiting for transfers between devices  124 us (31%)
  local copies, waits for them, and re-layouts  86.5 us (22%)
  other arithmetic  74.2 us (19%)
  blocking collectives  73.8 us (19%)
  between operations  15.6 us (4%)
  starting transfers between devices  10.7 us (3%)
  matrix products  7.44 us (2%)
    psum x1, waiting for transfers between devices, body(): summed = lax.psum(dfetched.astype(jnp.bfloat16), 'dp').astype(jnp.float32)  86.7 us
    all_gather x1, blocking collectives, body(): lax.all_gather(normalized_embedding, 'cls', axis=0, tiled=True)  53.1 us
    gather x2, local copies, waits for them, and re-layouts, body(): fetched = arrived[home_shard, slot_rank]  40.1 us
    reduce_scatter x1, waiting for transfers between devices, body(): lax.psum_scatter(jnp.dot(grad_logit, what, preferred_element_type=jnp.flo...  37.6 us
    scatter-add x1, other arithmetic, body(): centre_grad = jnp.zeros((home_rows, width), jnp.float32).at[incoming.resh...  35.5 us
    unnamed x10, local copies, waits for them, and re-layouts  21.8 us
    gather x1, local copies, waits for them, and re-layouts, body(): replies = centres[incoming]  20.2 us
    another operation x3, other arithmetic  12.1 us
  transfers between devices with their start and end apart: 4, of which 2 were waited for; matrix products, arithmetic and copies ran while one was open for 4% of the time, Pallas kernels for 0%

commit v1 on v0

v1 whole, which is shorter than its diff:
```python
import math

import jax
import jax.numpy as jnp
from jax import lax
from jax.experimental import pallas as pl
from jax.experimental.pallas import tpu as pltpu
from jax.sharding import PartitionSpec as P

eps = 1e-06
logit_scale = 64.0
margin = 0.35
momentum_rate = 0.9
learn_rate = 0.1
weight_decay = 0.0005

LANES = 128
VMEM_LIMIT = 48 * 1024 * 1024
bf16 = jnp.bfloat16
f32 = jnp.float32


def dot(a, b, ca, cb):
    return lax.dot_general(a, b, (((ca,), (cb,)), ((), ())), preferred_element_type=f32)


def swap(x, axis_name, m):
    n = lax.axis_size(axis_name)
    return lax.ppermute(x, axis_name, [(i, i ^ m) for i in range(n)])


def params():
    return pltpu.CompilerParams(vmem_limit_bytes=VMEM_LIMIT)


def norm_kernel(c_ref, o_ref):
    c = c_ref[...].astype(f32)
    inv = 1.0 / jnp.sqrt(jnp.sum(c * c, axis=1, keepdims=True) + eps)
    o_ref[...] = (c * inv).astype(bf16)


def normalize(centres, tile):
    rows, width = centres.shape
    return pl.pallas_call(
        norm_kernel,
        grid=(rows // tile,),
        in_specs=[pl.BlockSpec((tile, width), lambda i: (i, 0))],
        out_specs=pl.BlockSpec((tile, width), lambda i: (i, 0)),
        out_shape=jax.ShapeDtypeStruct((rows, width), bf16),
        compiler_params=params(),
        cost_estimate=pl.CostEstimate(flops=4 * rows * width, bytes_accessed=4 * rows * width, transcendentals=rows),
        name="norm",
    )(centres)


def prep_kernel(home_rows, shard_ref, tiles_ref, table_ref, lab_ref, cnt_ref, cls_ref):
    s = shard_ref[0]
    tiles, here = tiles_ref.shape
    base = s * home_rows
    blocks = home_rows // LANES
    total = jnp.zeros((LANES, blocks), f32)
    for t in range(tiles):
        h = tiles_ref[t : t + 1, :] - base
        hi = lax.shift_right_arithmetic(h, 7)
        lo = lax.bitwise_and(h, LANES - 1)
        a = (lax.broadcasted_iota(jnp.int32, (blocks, here), 0) == hi).astype(f32).astype(bf16)
        b = (lax.broadcasted_iota(jnp.int32, (LANES, here), 0) == lo).astype(f32).astype(bf16)
        total = total + dot(b, a, 1, 1)
    for k in range(blocks):
        cnt_ref[k * LANES : (k + 1) * LANES, :] = jnp.broadcast_to(total[:, k : k + 1], (LANES, LANES))
    table = table_ref[...]
    n_hi = table.shape[0]
    p0 = lax.bitwise_and(table, 255).astype(f32).astype(bf16)
    p1 = lax.bitwise_and(lax.shift_right_logical(table, 8), 255).astype(f32).astype(bf16)
    p2 = lax.shift_right_logical(table, 16).astype(f32).astype(bf16)
    chunks, _, rows = lab_ref.shape
    for j in range(chunks):
        lab = lab_ref[j]
        hi = lax.shift_right_logical(lab, 7)
        lo = lax.bitwise_and(lab, LANES - 1)
        oh = (lax.broadcasted_iota(jnp.int32, (n_hi, rows), 0) == hi).astype(f32).astype(bf16)
        g = dot(p0, oh, 0, 0) + 256.0 * dot(p1, oh, 0, 0) + 65536.0 * dot(p2, oh, 0, 0)
        pick = jnp.where(lax.broadcasted_iota(jnp.int32, (LANES, rows), 0) == lo, g, 0.0)
        cls_ref[j] = jnp.sum(pick, axis=0, keepdims=True).astype(jnp.int32) - base


def prepare(shard, tiles, labels, home_rows):
    vm = pl.BlockSpec(memory_space=pltpu.VMEM)
    table = tiles.reshape(-1, LANES)
    return pl.pallas_call(
        lambda *refs: prep_kernel(home_rows, *refs),
        in_specs=[pl.BlockSpec(memory_space=pltpu.SMEM), vm, vm, vm],
        out_specs=(vm, vm),
        out_shape=(
            jax.ShapeDtypeStruct((home_rows, LANES), f32),
            jax.ShapeDtypeStruct(labels.shape, jnp.int32),
        ),
        compiler_params=params(),
        cost_estimate=pl.CostEstimate(
            flops=2 * tiles.size * 64 * LANES, bytes_accessed=8 * tiles.size + 512 * home_rows, transcendentals=0
        ),
        name="prep",
    )(shard, tiles, table, labels)


def logits_kernel(group, rows_here, x0_ref, x1_ref, what_ref, cnt_ref, lab_ref, w_ref, den_ref, xs_ref, ut0_ref, ut1_ref, u_acc, t_acc, d_acc):
    i = pl.program_id(0)
    tile = what_ref.shape[0]
    rows = xs_ref.shape[0]
    own = 2 * rows_here

    @pl.when(i == 0)
    def _():
        for z in range(group):
            for r, ref in ((0, x0_ref), (1, x1_ref)):
                at = (2 * z + r) * rows_here
                xs_ref[at : at + rows_here, :] = ref[z]
        u_acc[...] = jnp.zeros_like(u_acc)
        t_acc[...] = jnp.zeros_like(t_acc)
        d_acc[...] = jnp.zeros_like(d_acc)

    what = what_ref[...]
    cos = dot(what, xs_ref[...], 1, 1)
    e = jnp.exp2(cos * (logit_scale * math.log2(math.e)))
    ids = lax.broadcasted_iota(jnp.int32, (tile, LANES), 0) + i * tile
    cnt = cnt_ref[...]
    cnt_t = cnt + (math.exp(-logit_scale * margin) - 1.0)
    lab = lab_ref[0]
    den = d_acc[...]
    for k in range(rows // LANES):
        cols = slice(k * LANES, (k + 1) * LANES)
        hit = ids == lab[:, cols]
        w = e[:, cols] * jnp.where(hit, cnt_t, cnt)
        d_acc[:, cols] = den[:, cols] + jnp.sum(w.reshape(tile // 8, 8, LANES), axis=0)
        wb = w.astype(bf16)
        w_ref[:, cols] = wb
        if k < own // LANES:
            u_acc[cols, :] += dot(wb, what, 0, 0)
            t_acc[cols, :] += dot(hit.astype(f32).astype(bf16), what, 0, 0)

    @pl.when(i == pl.num_programs(0) - 1)
    def _():
        den_ref[...] = jnp.sum(d_acc[...], axis=0, keepdims=True)
        for r, ref in ((0, ut0_ref), (1, ut1_ref)):
            ref[:rows_here, :] = u_acc[r * rows_here : (r + 1) * rows_here, :].astype(bf16)
            ref[rows_here:, :] = t_acc[r * rows_here : (r + 1) * rows_here, :].astype(bf16)


def logits(x0, x1, what, cnt, lab, j, tile):
    group, rows_here, width = x0.shape
    classes = what.shape[0]
    rows = 2 * group * rows_here
    own = 2 * rows_here
    whole = lambda *shape: pl.BlockSpec(shape, lambda i: (0,) * len(shape))
    return pl.pallas_call(
        lambda *refs: logits_kernel(group, rows_here, *refs),
        grid=(classes // tile,),
        in_specs=[
            whole(group, rows_here, width),
            whole(group, rows_here, width),
            pl.BlockSpec((tile, width), lambda i: (i, 0)),
            pl.BlockSpec((tile, LANES), lambda i: (i, 0)),
            pl.BlockSpec((1, 1, rows), lambda i: (j, 0, 0)),
        ],
        out_specs=(
            pl.BlockSpec((tile, rows), lambda i: (i, 0)),
            whole(1, rows),
            whole(rows, width),
            whole(own, width),
            whole(own, width),
        ),
        out_shape=(
            jax.ShapeDtypeStruct((classes, rows), bf16),
            jax.ShapeDtypeStruct((1, rows), f32),
            jax.ShapeDtypeStruct((rows, width), bf16),
            jax.ShapeDtypeStruct((own, width), bf16),
            jax.ShapeDtypeStruct((own, width), bf16),
        ),
        scratch_shapes=[
            pltpu.VMEM((own, width), f32),
            pltpu.VMEM((own, width), f32),
            pltpu.VMEM((8, rows), f32),
        ],
        compiler_params=params(),
        cost_estimate=pl.CostEstimate(
            flops=2 * rows * classes * width * 3 // 2,
            bytes_accessed=2 * rows * classes + 2 * classes * width,
            transcendentals=rows * classes,
        ),
        name="logits",
    )(x0, x1, what, cnt, lab)


def update_kernel(chunks, rate_ref, lab_ref, c_ref, m_ref, *refs):
    w_refs, x_refs, (mo_ref, co_ref) = refs[:chunks], refs[chunks : 2 * chunks], refs[2 * chunks :]
    tile = c_ref.shape[0]
    i = pl.program_id(0)
    rows = x_refs[0].shape[0]
    ids = lax.broadcasted_iota(jnp.int32, (tile, rows), 0) + i * tile
    dw = jnp.zeros(c_ref.shape, f32)
    for j in range(chunks):
        g = w_refs[j][...].astype(f32) * rate_ref[j] - jnp.where(ids == lab_ref[j], logit_scale, 0.0)
        dw = dw + dot(g.astype(bf16), x_refs[j][...], 1, 0)
    c = c_ref[...].astype(f32)
    inv = 1.0 / jnp.sqrt(jnp.sum(c * c, axis=1, keepdims=True) + eps)
    unit = c * inv
    grad = (dw - unit * jnp.sum(unit * dw, axis=1, keepdims=True)) * inv
    m = momentum_rate * m_ref[...] + grad + weight_decay * c
    mo_ref[...] = m
    co_ref[...] = (c - learn_rate * m).astype(bf16)


def update(rate, lab, centres, momentum, ws, xs, tile):
    chunks = len(ws)
    classes, width = centres.shape
    rows = xs[0].shape[0]
    whole = lambda *shape: pl.BlockSpec(shape, lambda i: (0,) * len(shape))
    block = pl.BlockSpec((tile, width), lambda i: (i, 0))
    return pl.pallas_call(
        lambda *refs: update_kernel(chunks, *refs),
        grid=(classes // tile,),
        in_specs=[whole(chunks, 1, rows), whole(chunks, 1, rows), block, block]
        + [pl.BlockSpec((tile, rows), lambda i: (i, 0))] * chunks
        + [whole(rows, width)] * chunks,
        out_specs=(block, block),
        out_shape=(
            jax.ShapeDtypeStruct((classes, width), f32),
            jax.ShapeDtypeStruct((classes, width), bf16),
        ),
        compiler_params=params(),
        cost_estimate=pl.CostEstimate(
            flops=2 * rows * chunks * classes * width,
            bytes_accessed=2 * rows * chunks * classes + 12 * classes * width,
            transcendentals=0,
        ),
        name="update",
    )(rate, lab, centres, momentum, *ws, *xs)


def body(embeddings, labels, centres, momentum, sample_home, sample_row):
    shards = lax.axis_size("cls")
    group = lax.axis_size("dp")
    chips = shards // 2
    home_rows, width = centres.shape
    rows_here = embeddings.shape[0]
    here = sample_row.shape[0]
    shard = lax.axis_index("cls")
    chunk_rows = 2 * group * rows_here

    ids = (sample_home[:, 0] * home_rows + sample_row)[None, :]
    step = 1
    while step < shards:
        ids = jnp.concatenate([ids, swap(ids, "cls", step)], axis=0)
        step *= 2

    labs = jnp.stack([labels] + [swap(labels, "dp", m) for m in range(1, group)])
    labs = (lax.bitwise_xor(labs // here, shard) * here + labs % here).reshape(group, shards, rows_here)
    bit = 1
    while bit < shards:
        labs = labs.reshape(group, shards // (2 * bit), 2, bit, rows_here)
        labs = jnp.where(lax.bitwise_and(shard, bit) != 0, labs[:, :, ::-1], labs)
        bit *= 2
    labs = labs.reshape(group, chips, 2, rows_here).transpose(1, 0, 2, 3).reshape(chips, 1, chunk_rows)

    what = normalize(centres, min(1024, home_rows))
    cnt, lab = prepare(shard.astype(jnp.int32).reshape(1), ids, labs, home_rows)

    xfloat = embeddings.astype(f32)
    row_norm = jnp.sqrt(jnp.sum(xfloat * xfloat, axis=1, keepdims=True) + eps)
    unit = xfloat / row_norm
    xhat = unit.astype(bf16)
    mine = jnp.stack([xhat] + [swap(xhat, "dp", m) for m in range(1, group)])
    mine_of = [mine] + [swap(mine, "cls", 2 * q) for q in range(1, chips)]
    other_of = [swap(x, "cls", 1) for x in mine_of]

    tile = min(1024, home_rows)
    parts = [logits(mine_of[q], other_of[q], what, cnt, lab, q, tile) for q in range(chips)]
    ws = [p[0] for p in parts]
    xs = [p[2] for p in parts]

    den = jnp.concatenate([p[1] for p in parts], axis=0)
    theirs = swap(den, "cls", 1).reshape(chips, group, 2, rows_here)[:, :, ::-1]
    den = den + theirs.reshape(chips, chunk_rows)
    got = [swap(den, "cls", 2 * q) for q in range(1, chips)]
    for q in range(1, chips):
        den = den + jnp.concatenate([got[q - 1][j ^ q][None] for j in range(chips)], axis=0)
    rate = (logit_scale / den).reshape(chips, 1, chunk_rows)

    momentum_new, centres_new = update(rate, lab, centres, momentum, ws, xs, min(512, home_rows))

    away = swap(jnp.stack([p[4] for p in parts]), "cls", 1)
    pair = [(p[3].astype(f32) + away[q].astype(f32)) for q, p in enumerate(parts)]
    total = pair[0]
    for q in range(1, chips):
        total = total + swap(pair[q].astype(bf16), "cls", 2 * q).astype(f32)
    scale = rate[0, 0, :rows_here][:, None]
    dunit = total[:rows_here] * scale - logit_scale * total[rows_here:]
    emb_grad = (dunit - unit * jnp.sum(unit * dunit, axis=1, keepdims=True)) / row_norm
    return (emb_grad, momentum_new, centres_new)


def solution(mesh):
    placed = (
        P(("dp", "cls"), None),
        P("dp"),
        P("cls", None),
        P("cls", None),
        P("cls", None),
        P("cls"),
    )
    return jax.shard_map(
        body,
        mesh=mesh,
        in_specs=placed,
        out_specs=(P(("dp", "cls"), None), P("cls", None), P("cls", None)),
        check_vma=False,
    )
```

time: 394 us -> 119 us (0.30)
  waiting for transfers between devices: 124 us -> 12.3 us
  local copies, waits for them, and re-layouts: 86.5 us -> 3.57 us
  blocking collectives: 73.8 us -> 0 us
  other arithmetic: 74.2 us -> 8.52 us
  Pallas kernels: 0 us -> 59.3 us
  starting transfers between devices: 10.7 us -> 32.1 us
  between operations: 15.6 us -> 0.84 us
  matrix products: 7.44 us -> 0 us
    psum x1 -> x0, waiting for transfers between devices: 86.7 us -> none  [body(): summed = lax.psum(dfetched.astype(jnp.bfloat16), 'dp').astype(jnp.float32)]
    gather x3 -> x0, local copies, waits for them, and re-layouts: 60.3 us -> none  [the longest x2 40.1 us: body(): fetched = arrived[home_shard, slot_rank]]
    pallas_call x0 -> x7, Pallas kernels: none -> 59.3 us  [the longest x4 32.8 us: logits(): pl.pallas_call(lambda *refs: logits_kernel(group, rows_here, *refs), grid...]
    all_gather x1 -> x0, blocking collectives: 53.1 us -> none  [body(): lax.all_gather(normalized_embedding, 'cls', axis=0, tiled=True)]
    reduce_scatter x1 -> x0, waiting for transfers between devices: 37.6 us -> none  [body(): lax.psum_scatter(jnp.dot(grad_logit, what, preferred_element_type=jnp.flo...]
    scatter-add x1 -> x0, other arithmetic: 35.5 us -> none  [body(): centre_grad = jnp.zeros((home_rows, width), jnp.float32).at[incoming.resh...]
    ppermute x0 -> x24, starting transfers between devices: none -> 32.1 us  [swap(): return lax.ppermute(x, axis_name, [(i, i ^ m) for i in range(n)])]
    unnamed x10 -> x9, local copies, waits for them, and re-layouts: 21.8 us -> 2.04 us
  transfers between devices with their start and end apart: 4 -> 24, of which waited for: 2 -> 7; matrix products, arithmetic and copies ran while one was open for 4% -> 4% of each run, Pallas kernels for 0% -> 44%
where the time goes in v1:
time: 119 us; the launch traced here: 117 us
  Pallas kernels  59.3 us (50%)
  starting transfers between devices  32.1 us (27%)
  waiting for transfers between devices  12.3 us (10%)
  other arithmetic  8.52 us (7%)
  local copies, waits for them, and re-layouts  3.57 us (3%)
    pallas_call x4, Pallas kernels, logits(): pl.pallas_call(lambda *refs: logits_kernel(group, rows_here, *refs), grid...  32.8 us
    ppermute x24, starting transfers between devices, swap(): return lax.ppermute(x, axis_name, [(i, i ^ m) for i in range(n)])  32.1 us
    pallas_call x1, Pallas kernels, update(): pl.pallas_call(lambda *refs: update_kernel(chunks, *refs), grid=(classes...  19.9 us
    ppermute x24, waiting for transfers between devices, swap(): return lax.ppermute(x, axis_name, [(i, i ^ m) for i in range(n)])  12.3 us
    pallas_call x1, Pallas kernels, normalize(): pl.pallas_call(norm_kernel, grid=(rows // tile,), in_specs=[pl.BlockSpec(...  4.04 us
    pallas_call x1, Pallas kernels, prepare(): pl.pallas_call(lambda *refs: prep_kernel(home_rows, *refs), in_specs=[pl....  2.58 us
  transfers between devices with their start and end apart: 24, of which 7 were waited for; matrix products, arithmetic and copies ran while one was open for 4% of the time, Pallas kernels for 44%

profile of v1, /device:TPU:1, one launch (start us, length us, event | category | flops | bytes accessed | tf_op | source)
XLA Modules:
  0.0 116.6 jit_solution(9658289341685311626)
XLA Ops:
  0.6 1.0 fusion.6
  1.6 0.9 fusion.13
  2.5 4.2 %collective-permute-start.2 = (bf16[64,512]{1,0:T(8,128)(2,1)S(1)}, bf16[64,512]{1,0:T(8,128)(2,1)S(1)}, u32[]{:S(2)}, u32[]{:S(2)}) collective-permute-start(bf16[64,512]{1,0:T(8,128)(2,1)S(1)} %fusion.13), channel_id=1, source_target_pairs={{0,24},{8,16},{16,8},{24,0},{1,25},{9,17},{17,9},{25,1},{2,26},{10... | collective-permute-start | bytes 196616 | tf_op jit(solution)/shard_map/ppermute | solution.py:29
  6.7 0.4 collective-permute-start
  7.1 1.1 collective-permute-start.7
  8.2 2.4 %collective-permute-start.8 = (s32[512]{0:T(512)}, s32[512]{0:T(512)S(1)}, u32[]{:S(2)}, u32[]{:S(2)}) collective-permute-start(s32[512]{0:T(512)} %param.7), channel_id=1, source_target_pairs={{0,16},{8,24},{16,0},{24,8},{1,17},{9,25},{17,1},{25,9},{2,18},{10... | collective-permute-start | bytes 6152 | tf_op jit(solution)/shard_map/ppermute | solution.py:29
  10.6 0.9 fusion.14
  11.5 0.8 stack.50
  12.3 0.7 broadcast_multiply_fusion
  13.0 0.7 add.110
  13.7 4.0 %norm.1.refs_2_ = bf16[4096,512]{1,0:T(8,128)(2,1)S(1)} custom-call(bf16[4096,512]{1,0:T(8,128)(2,1)} %refs_2_.1), custom_call_target="tpu_custom_call" | custom-call | flops 8388608 | bytes 8388608 | tf_op jit(solution)/shard_map/norm/pallas_call | solution.py:44
  17.7 0.0 copy-start
  17.8 2.0 %copy-done = bf16[4096,512]{1,0:T(8,128)(2,1)} copy-done((bf16[4096,512]{1,0:T(8,128)(2,1)}, bf16[4096,512]{1,0:T(8,128)(2,1)S(1)}, u32[]{:S(2)}) %copy-start) | copy-done | bytes 4194328
  19.8 0.1 collective-permute-start.9
  19.8 0.1 stack.51
  19.9 0.0 collective-permute-done.8
  19.9 2.1 %collective-permute-start.4 = (s32[1,2048]{1,0:T(1,128)S(1)}, s32[1,2048]{1,0:T(1,128)S(1)}, u32[]{:S(2)}, u32[]{:S(2)}) collective-permute-start(s32[1,2048]{1,0:T(1,128)S(1)} %bitcast.69), channel_id=1, source_target_pairs={{0,1},{1,0},{2,3},{3,2},{4,5},{5,4},{6,7},{7,6},{8,9},{9,8},{10,11... | collective-permute-start | bytes 24584 | tf_op jit(solution)/shard_map/ppermute | solution.py:29
  22.0 0.1 stack.52
  22.1 1.9 %collective-permute-done.9 = s32[512]{0:T(512)S(1)} collective-permute-done((s32[512]{0:T(512)S(1)}, s32[512]{0:T(512)S(1)}, u32[]{:S(2)}, u32[]{:S(2)}) %collective-permute-start.9) | collective-permute-done | bytes 2080 | tf_op jit(solution)/shard_map/ppermute | solution.py:29
  24.0 0.1 stack.53
  24.1 0.1 fusion.8
  24.2 0.1 broadcast_select_fusion
  24.3 0.0 collective-permute-done.4
  24.3 1.3 %collective-permute-start.5 = (s32[2,2048]{1,0:T(2,128)S(1)}, s32[2,2048]{1,0:T(2,128)S(1)}, u32[]{:S(2)}, u32[]{:S(2)}) collective-permute-start(s32[2,2048]{1,0:T(2,128)S(1)} %pad_add_fusion.2), channel_id=1, source_target_pairs={{0,2},{1,3},{2,0},{3,1},{4,6},{5,7},{6,4},{7,5},{8,10},{9,11},{10,... | collective-permute-start | bytes 49160 | tf_op jit(solution)/shard_map/ppermute | solution.py:29
  25.6 1.4 %collective-permute-done.5 = s32[2,2048]{1,0:T(2,128)S(1)} collective-permute-done((s32[2,2048]{1,0:T(2,128)S(1)}, s32[2,2048]{1,0:T(2,128)S(1)}, u32[]{:S(2)}, u32[]{:S(2)}) %collective-permute-start.5) | collective-permute-done | bytes 16416 | tf_op jit(solution)/shard_map/ppermute | solution.py:29
  27.0 1.3 %collective-permute-start.6 = (s32[4,2048]{1,0:T(4,128)S(1)}, s32[4,2048]{1,0:T(4,128)S(1)}, u32[]{:S(2)}, u32[]{:S(2)}) collective-permute-start(s32[4,2048]{1,0:T(4,128)S(1)} %pad_add_fusion.1), channel_id=1, source_target_pairs={{0,4},{1,5},{2,6},{3,7},{4,0},{5,1},{6,2},{7,3},{8,12},{9,13},{10,... | collective-permute-start | bytes 98312 | tf_op jit(solution)/shard_map/ppermute | solution.py:29
  28.3 0.0 collective-permute-done.1
  28.3 0.0 collective-permute-done
  28.4 1.3 %collective-permute-start.10 = (bf16[4,64,512]{2,1,0:T(8,128)(2,1)S(1)}, bf16[4,64,512]{2,1,0:T(8,128)(2,1)S(1)}, u32[]{:S(2)}, u32[]{:S(2)}) collective-permute-start(bf16[4,64,512]{2,1,0:T(8,128)(2,1)S(1)} %pad_maximum_fusion.1.refs_0_), channel_id=1, source_target_pairs={{0,2},{1,3},{2,0},{3,1},{4,6},{5,7},{6,4},{7,5},{8,10},{9,11},{10,... | collective-permute-start | bytes 786440 | tf_op jit(solution)/shard_map/ppermute | solution.py:29
  29.6 0.2 collective-permute-start.14
  29.8 1.2 %collective-permute-start.12 = (bf16[4,64,512]{2,1,0:T(8,128)(2,1)S(1)}, bf16[4,64,512]{2,1,0:T(8,128)(2,1)S(1)}, u32[]{:S(2)}, u32[]{:S(2)}) collective-permute-start(bf16[4,64,512]{2,1,0:T(8,128)(2,1)S(1)} %pad_maximum_fusion.1.refs_0_), channel_id=1, source_target_pairs={{0,4},{1,5},{2,6},{3,7},{4,0},{5,1},{6,2},{7,3},{8,12},{9,13},{10,... | collective-permute-start | bytes 786440 | tf_op jit(solution)/shard_map/ppermute | solution.py:29
  31.1 5.7 %collective-permute-start.3 = (bf16[4,64,512]{2,1,0:T(8,128)(2,1)S(1)}, bf16[4,64,512]{2,1,0:T(8,128)(2,1)S(1)}, u32[]{:S(2)}, u32[]{:S(2)}) collective-permute-start(bf16[4,64,512]{2,1,0:T(8,128)(2,1)S(1)} %pad_maximum_fusion.1.refs_0_), channel_id=1, source_target_pairs={{0,1},{1,0},{2,3},{3,2},{4,5},{5,4},{6,7},{7,6},{8,9},{9,8},{10,11... | collective-permute-start | bytes 786440 | tf_op jit(solution)/shard_map/ppermute | solution.py:29
  36.8 0.1 reshape.581.refs_3_
  36.9 2.6 %prep.1 = (f32[4096,128]{1,0:T(8,128)S(1)}, s32[4,1,512]{2,1,0:T(1,128)S(1)}) custom-call(s32[1]{0:T(128)} %bitcast.4.refs_0_, s32[8,2048]{1,0:T(8,128)S(1)} %pad_add_fusion.refs_1_, s32[128,128]{1,0:T(8,128)S(1)} %reshape.577.refs_2_, s32[4,1,512]{2,1,0:T(1,128)S(1)} %reshape.581.refs_3_), custom_call_target="tpu_custom_call" | custom-call | flops 268435456 | bytes 2228224 | tf_op jit(solution)/shard_map/prep/pallas_call | solution.py:90
  39.5 1.3 %collective-permute-start.11 = (bf16[4,64,512]{2,1,0:T(8,128)(2,1)S(1)}, bf16[4,64,512]{2,1,0:T(8,128)(2,1)S(1)}, u32[]{:S(2)}, u32[]{:S(2)}) collective-permute-start(bf16[4,64,512]{2,1,0:T(8,128)(2,1)S(1)} %collective-permute-done.10.refs_0_), channel_id=1, source_target_pairs={{0,1},{1,0},{2,3},{3,2},{4,5},{5,4},{6,7},{7,6},{8,9},{9,8},{10,11... | collective-permute-start | bytes 786440 | tf_op jit(solution)/shard_map/ppermute | solution.py:29
  40.8 2.3 %collective-permute-start.15 = (bf16[4,64,512]{2,1,0:T(8,128)(2,1)S(1)}, bf16[4,64,512]{2,1,0:T(8,128)(2,1)S(1)}, u32[]{:S(2)}, u32[]{:S(2)}) collective-permute-start(bf16[4,64,512]{2,1,0:T(8,128)(2,1)S(1)} %collective-permute-done.14.refs_0_), channel_id=1, source_target_pairs={{0,1},{1,0},{2,3},{3,2},{4,5},{5,4},{6,7},{7,6},{8,9},{9,8},{10,11... | collective-permute-start | bytes 786440 | tf_op jit(solution)/shard_map/ppermute | solution.py:29
  43.0 1.5 %collective-permute-start.13 = (bf16[4,64,512]{2,1,0:T(8,128)(2,1)S(1)}, bf16[4,64,512]{2,1,0:T(8,128)(2,1)S(1)}, u32[]{:S(2)}, u32[]{:S(2)}) collective-permute-start(bf16[4,64,512]{2,1,0:T(8,128)(2,1)S(1)} %collective-permute-done.12.refs_0_), channel_id=1, source_target_pairs={{0,1},{1,0},{2,3},{3,2},{4,5},{5,4},{6,7},{7,6},{8,9},{9,8},{10,11... | collective-permute-start | bytes 786440 | tf_op jit(solution)/shard_map/ppermute | solution.py:29
  44.5 8.2 %logits.4 = (bf16[4096,512]{1,0:T(8,128)(2,1)}, f32[1,512]{1,0:T(1,128)S(1)}, bf16[512,512]{1,0:T(8,128)(2,1)S(1)}, bf16[128,512]{1,0:T(8,128)(2,1)S(1)}, bf16[128,512]{1,0:T(8,128)(2,1)S(1)}) custom-call(bf16[4,64,512]{2,1,0:T(8,128)(2,1)S(1)} %pad_maximum_fusion.1.refs_0_, bf16[4,64,512]{2,1,0:T(8,128)(2,1)S(1)} %collective-permute-done.3.refs_1_, ...), custom_call_target="tpu_custom_call" | custom-call | flops 3221225472 | bytes 8388608 | tf_op jit(solution)/shard_map/logits/pallas_call | solution.py:155
  52.7 8.1 %logits.5 = (bf16[4096,512]{1,0:T(8,128)(2,1)}, f32[1,512]{1,0:T(1,128)S(1)}, bf16[512,512]{1,0:T(8,128)(2,1)S(1)}, bf16[128,512]{1,0:T(8,128)(2,1)S(1)}, bf16[128,512]{1,0:T(8,128)(2,1)S(1)}) custom-call(bf16[4,64,512]{2,1,0:T(8,128)(2,1)S(1)} %collective-permute-done.10.refs_0_, bf16[4,64,512]{2,1,0:T(8,128)(2,1)S(1)} %collective-permute-done.11.refs_1_, ...), custom_call_target="tpu_custom_call" | custom-call | flops 3221225472 | bytes 8388608 | tf_op jit(solution)/shard_map/logits/pallas_call | solution.py:155
  60.9 8.3 %logits.7 = (bf16[4096,512]{1,0:T(8,128)(2,1)}, f32[1,512]{1,0:T(1,128)S(1)}, bf16[512,512]{1,0:T(8,128)(2,1)S(1)}, bf16[128,512]{1,0:T(8,128)(2,1)S(1)}, bf16[128,512]{1,0:T(8,128)(2,1)S(1)}) custom-call(bf16[4,64,512]{2,1,0:T(8,128)(2,1)S(1)} %collective-permute-done.14.refs_0_, bf16[4,64,512]{2,1,0:T(8,128)(2,1)S(1)} %collective-permute-done.15.refs_1_, ...), custom_call_target="tpu_custom_call" | custom-call | flops 3221225472 | bytes 8388608 | tf_op jit(solution)/shard_map/logits/pallas_call | solution.py:155
  69.1 8.2 %logits.6 = (bf16[4096,512]{1,0:T(8,128)(2,1)}, f32[1,512]{1,0:T(1,128)S(1)}, bf16[512,512]{1,0:T(8,128)(2,1)S(1)}, bf16[128,512]{1,0:T(8,128)(2,1)S(1)}, bf16[128,512]{1,0:T(8,128)(2,1)S(1)}) custom-call(bf16[4,64,512]{2,1,0:T(8,128)(2,1)S(1)} %collective-permute-done.12.refs_0_, bf16[4,64,512]{2,1,0:T(8,128)(2,1)S(1)} %collective-permute-done.13.refs_1_, ...), custom_call_target="tpu_custom_call" | custom-call | flops 3221225472 | bytes 8388608 | tf_op jit(solution)/shard_map/logits/pallas_call | solution.py:155
  77.3 0.1 collective-permute-start.20
  77.4 1.2 collective-permute-done.20
  78.6 0.1 reshape.582
  78.7 0.1 reshape.584
  78.8 2.2 %collective-permute-start.23 = (f32[4,512]{1,0:T(4,128)S(1)}, f32[4,512]{1,0:T(4,128)S(1)}, u32[]{:S(2)}, u32[]{:S(2)}) collective-permute-start(f32[4,512]{1,0:T(4,128)S(1)} %fusion.12), channel_id=1, source_target_pairs={{0,6},{1,7},{2,4},{3,5},{4,2},{5,3},{6,0},{7,1},{8,14},{9,15},{10,... | collective-permute-start | bytes 24584 | tf_op jit(solution)/shard_map/ppermute | solution.py:29
  81.1 0.9 pad_maximum_fusion
  81.9 0.4 collective-permute-start.16
  82.4 0.2 collective-permute-start.22
  82.6 0.3 collective-permute-start.21
  82.9 0.1 reshape.583
  83.0 1.9 %collective-permute-done.22 = f32[4,512]{1,0:T(4,128)S(1)} collective-permute-done((f32[4,512]{1,0:T(4,128)S(1)}, f32[4,512]{1,0:T(4,128)S(1)}, u32[]{:S(2)}, u32[]{:S(2)}) %collective-permute-start.22) | collective-permute-done | bytes 8224 | tf_op jit(solution)/shard_map/ppermute | solution.py:29
  84.9 0.2 collective-permute-done.21
  85.2 0.0 copy-start.1
  85.2 19.9 %update.1 = (f32[4096,512]{1,0:T(8,128)}, bf16[4096,512]{1,0:T(8,128)(2,1)}) custom-call(f32[4,1,512]{2,1,0:T(1,128)S(1)} %fusion.11.refs_0_, s32[4,1,512]{2,1,0:T(1,128)S(1)} %get-tuple-element.28.refs_4_.refs_1_, bf16[4096,512]{1,0:T(8,128)(2,1)} %refs_2_.1, f32[4096,512]{1,0:T(8,128)} %refs_3_.1, bf16[4096,512]{1,0:T(8,128)(2,1)} %get-tuple-element.41.refs_4_, ...), custom_call_target="tpu_custom_call" | custom-call | flops 8589934592 | bytes 41943040 | tf_op jit(solution)/shard_map/update/pallas_call | solution.py:219
  105.1 1.1 fusion.2
  106.2 1.3 %collective-permute-start.19 = (bf16[128,512]{1,0:T(8,128)(2,1)S(1)}, bf16[128,512]{1,0:T(8,128)(2,1)S(1)}, u32[]{:S(2)}, u32[]{:S(2)}) collective-permute-start(bf16[128,512]{1,0:T(8,128)(2,1)S(1)} %get-tuple-element.52), channel_id=1, source_target_pairs={{0,6},{1,7},{2,4},{3,5},{4,2},{5,3},{6,0},{7,1},{8,14},{9,15},{10,... | collective-permute-start | bytes 393224 | tf_op jit(solution)/shard_map/ppermute | solution.py:29
  107.5 0.2 collective-permute-start.18
  107.7 1.2 %collective-permute-start.17 = (bf16[128,512]{1,0:T(8,128)(2,1)S(1)}, bf16[128,512]{1,0:T(8,128)(2,1)S(1)}, u32[]{:S(2)}, u32[]{:S(2)}) collective-permute-start(bf16[128,512]{1,0:T(8,128)(2,1)S(1)} %get-tuple-element.51), channel_id=1, source_target_pairs={{0,2},{1,3},{2,0},{3,1},{4,6},{5,7},{6,4},{7,5},{8,10},{9,11},{10,... | collective-permute-start | bytes 393224 | tf_op jit(solution)/shard_map/ppermute | solution.py:29
  108.9 2.2 %collective-permute-done.19 = bf16[128,512]{1,0:T(8,128)(2,1)S(1)} collective-permute-done((bf16[128,512]{1,0:T(8,128)(2,1)S(1)}, bf16[128,512]{1,0:T(8,128)(2,1)S(1)}, u32[]{:S(2)}, u32[]{:S(2)}) %collective-permute-start.19) | collective-permute-done | bytes 131104 | tf_op jit(solution)/shard_map/ppermute | solution.py:29
  111.1 3.6 %collective-permute-done.18 = bf16[128,512]{1,0:T(8,128)(2,1)S(1)} collective-permute-done((bf16[128,512]{1,0:T(8,128)(2,1)S(1)}, bf16[128,512]{1,0:T(8,128)(2,1)S(1)}, u32[]{:S(2)}, u32[]{:S(2)}) %collective-permute-start.18) | collective-permute-done | bytes 131104 | tf_op jit(solution)/shard_map/ppermute | solution.py:29
  114.6 1.0 fusion.5
  115.6 0.2 multiply_reduce_fusion
  115.8 0.8 subtract_divide_fusion
  (41 shorter events, 0.4 us)
Async XLA Ops:
  2.5 25.8 %collective-permute-start.2 = (bf16[64,512]{1,0:T(8,128)(2,1)S(1)}, bf16[64,512]{1,0:T(8,128)(2,1)S(1)}, u32[]{:S(2)}, u32[]{:S(2)}) collective-permute-start(bf16[64,512]{1,0:T(8,128)(2,1)S(1)} %fusion.13), channel_id=1, source_target_pairs={{0,24},{8,16},{16,8},{24,0},{1,25},{9,17},{17,9},{25,1},{2,26},{10... | collective-permute-start | bytes 196616 | tf_op jit(solution)/shard_map/ppermute | solution.py:29
  6.7 21.6 %collective-permute-start.1 = (bf16[64,512]{1,0:T(8,128)(2,1)S(1)}, bf16[64,512]{1,0:T(8,128)(2,1)S(1)}, u32[]{:S(2)}, u32[]{:S(2)}) collective-permute-start(bf16[64,512]{1,0:T(8,128)(2,1)S(1)} %fusion.13), channel_id=1, source_target_pairs={{0,16},{8,24},{16,0},{24,8},{1,17},{9,25},{17,1},{25,9},{2,18},{10... | collective-permute-start | bytes 196616 | tf_op jit(solution)/shard_map/ppermute | solution.py:29
  6.7 21.6 %collective-permute-start = (bf16[64,512]{1,0:T(8,128)(2,1)S(1)}, bf16[64,512]{1,0:T(8,128)(2,1)S(1)}, u32[]{:S(2)}, u32[]{:S(2)}) collective-permute-start(bf16[64,512]{1,0:T(8,128)(2,1)S(1)} %fusion.13), channel_id=1, source_target_pairs={{0,8},{8,0},{16,24},{24,16},{1,9},{9,1},{17,25},{25,17},{2,10},{10... | collective-permute-start | bytes 196616 | tf_op jit(solution)/shard_map/ppermute | solution.py:29
  7.1 12.7 %collective-permute-start.7 = (s32[512]{0:T(512)}, s32[512]{0:T(512)S(1)}, u32[]{:S(2)}, u32[]{:S(2)}) collective-permute-start(s32[512]{0:T(512)} %param.7), channel_id=1, source_target_pairs={{0,8},{8,0},{16,24},{24,16},{1,9},{9,1},{17,25},{25,17},{2,10},{10... | collective-permute-start | bytes 6152 | tf_op jit(solution)/shard_map/ppermute | solution.py:29
  8.2 11.7 %collective-permute-start.8 = (s32[512]{0:T(512)}, s32[512]{0:T(512)S(1)}, u32[]{:S(2)}, u32[]{:S(2)}) collective-permute-start(s32[512]{0:T(512)} %param.7), channel_id=1, source_target_pairs={{0,16},{8,24},{16,0},{24,8},{1,17},{9,25},{17,1},{25,9},{2,18},{10... | collective-permute-start | bytes 6152 | tf_op jit(solution)/shard_map/ppermute | solution.py:29
  13.7 6.1 %copy-start.2 = (s32[512]{0:T(512)S(1)}, s32[512]{0:T(512)}, u32[]{:S(2)}) copy-start(s32[512]{0:T(512)} %param.7) | copy-start | bytes 6148
  17.7 2.0 %copy-start = (bf16[4096,512]{1,0:T(8,128)(2,1)}, bf16[4096,512]{1,0:T(8,128)(2,1)S(1)}, u32[]{:S(2)}) copy-start(bf16[4096,512]{1,0:T(8,128)(2,1)S(1)} %norm.1.refs_2_) | copy-start | bytes 12582916
  19.8 4.2 %collective-permute-start.9 = (s32[512]{0:T(512)S(1)}, s32[512]{0:T(512)S(1)}, u32[]{:S(2)}, u32[]{:S(2)}) collective-permute-start(s32[512]{0:T(512)S(1)} %copy-done.2), channel_id=1, source_target_pairs={{0,24},{8,16},{16,8},{24,0},{1,25},{9,17},{17,9},{25,1},{2,26},{10... | collective-permute-start | bytes 6152 | tf_op jit(solution)/shard_map/ppermute | solution.py:29
  19.9 4.4 %collective-permute-start.4 = (s32[1,2048]{1,0:T(1,128)S(1)}, s32[1,2048]{1,0:T(1,128)S(1)}, u32[]{:S(2)}, u32[]{:S(2)}) collective-permute-start(s32[1,2048]{1,0:T(1,128)S(1)} %bitcast.69), channel_id=1, source_target_pairs={{0,1},{1,0},{2,3},{3,2},{4,5},{5,4},{6,7},{7,6},{8,9},{9,8},{10,11... | collective-permute-start | bytes 24584 | tf_op jit(solution)/shard_map/ppermute | solution.py:29
  24.3 2.7 %collective-permute-start.5 = (s32[2,2048]{1,0:T(2,128)S(1)}, s32[2,2048]{1,0:T(2,128)S(1)}, u32[]{:S(2)}, u32[]{:S(2)}) collective-permute-start(s32[2,2048]{1,0:T(2,128)S(1)} %pad_add_fusion.2), channel_id=1, source_target_pairs={{0,2},{1,3},{2,0},{3,1},{4,6},{5,7},{6,4},{7,5},{8,10},{9,11},{10,... | collective-permute-start | bytes 49160 | tf_op jit(solution)/shard_map/ppermute | solution.py:29
  27.0 9.9 %collective-permute-start.6 = (s32[4,2048]{1,0:T(4,128)S(1)}, s32[4,2048]{1,0:T(4,128)S(1)}, u32[]{:S(2)}, u32[]{:S(2)}) collective-permute-start(s32[4,2048]{1,0:T(4,128)S(1)} %pad_add_fusion.1), channel_id=1, source_target_pairs={{0,4},{1,5},{2,6},{3,7},{4,0},{5,1},{6,2},{7,3},{8,12},{9,13},{10,... | collective-permute-start | bytes 98312 | tf_op jit(solution)/shard_map/ppermute | solution.py:29
  28.4 11.1 %collective-permute-start.10 = (bf16[4,64,512]{2,1,0:T(8,128)(2,1)S(1)}, bf16[4,64,512]{2,1,0:T(8,128)(2,1)S(1)}, u32[]{:S(2)}, u32[]{:S(2)}) collective-permute-start(bf16[4,64,512]{2,1,0:T(8,128)(2,1)S(1)} %pad_maximum_fusion.1.refs_0_), channel_id=1, source_target_pairs={{0,2},{1,3},{2,0},{3,1},{4,6},{5,7},{6,4},{7,5},{8,10},{9,11},{10,... | collective-permute-start | bytes 786440 | tf_op jit(solution)/shard_map/ppermute | solution.py:29
  29.6 11.1 %collective-permute-start.14 = (bf16[4,64,512]{2,1,0:T(8,128)(2,1)S(1)}, bf16[4,64,512]{2,1,0:T(8,128)(2,1)S(1)}, u32[]{:S(2)}, u32[]{:S(2)}) collective-permute-start(bf16[4,64,512]{2,1,0:T(8,128)(2,1)S(1)} %pad_maximum_fusion.1.refs_0_), channel_id=1, source_target_pairs={{0,6},{1,7},{2,4},{3,5},{4,2},{5,3},{6,0},{7,1},{8,14},{9,15},{10,... | collective-permute-start | bytes 786440 | tf_op jit(solution)/shard_map/ppermute | solution.py:29
  29.8 13.2 %collective-permute-start.12 = (bf16[4,64,512]{2,1,0:T(8,128)(2,1)S(1)}, bf16[4,64,512]{2,1,0:T(8,128)(2,1)S(1)}, u32[]{:S(2)}, u32[]{:S(2)}) collective-permute-start(bf16[4,64,512]{2,1,0:T(8,128)(2,1)S(1)} %pad_maximum_fusion.1.refs_0_), channel_id=1, source_target_pairs={{0,4},{1,5},{2,6},{3,7},{4,0},{5,1},{6,2},{7,3},{8,12},{9,13},{10,... | collective-permute-start | bytes 786440 | tf_op jit(solution)/shard_map/ppermute | solution.py:29
  31.1 13.5 %collective-permute-start.3 = (bf16[4,64,512]{2,1,0:T(8,128)(2,1)S(1)}, bf16[4,64,512]{2,1,0:T(8,128)(2,1)S(1)}, u32[]{:S(2)}, u32[]{:S(2)}) collective-permute-start(bf16[4,64,512]{2,1,0:T(8,128)(2,1)S(1)} %pad_maximum_fusion.1.refs_0_), channel_id=1, source_target_pairs={{0,1},{1,0},{2,3},{3,2},{4,5},{5,4},{6,7},{7,6},{8,9},{9,8},{10,11... | collective-permute-start | bytes 786440 | tf_op jit(solution)/shard_map/ppermute | solution.py:29
  39.5 13.2 %collective-permute-start.11 = (bf16[4,64,512]{2,1,0:T(8,128)(2,1)S(1)}, bf16[4,64,512]{2,1,0:T(8,128)(2,1)S(1)}, u32[]{:S(2)}, u32[]{:S(2)}) collective-permute-start(bf16[4,64,512]{2,1,0:T(8,128)(2,1)S(1)} %collective-permute-done.10.refs_0_), channel_id=1, source_target_pairs={{0,1},{1,0},{2,3},{3,2},{4,5},{5,4},{6,7},{7,6},{8,9},{9,8},{10,11... | collective-permute-start | bytes 786440 | tf_op jit(solution)/shard_map/ppermute | solution.py:29
  40.8 20.1 %collective-permute-start.15 = (bf16[4,64,512]{2,1,0:T(8,128)(2,1)S(1)}, bf16[4,64,512]{2,1,0:T(8,128)(2,1)S(1)}, u32[]{:S(2)}, u32[]{:S(2)}) collective-permute-start(bf16[4,64,512]{2,1,0:T(8,128)(2,1)S(1)} %collective-permute-done.14.refs_0_), channel_id=1, source_target_pairs={{0,1},{1,0},{2,3},{3,2},{4,5},{5,4},{6,7},{7,6},{8,9},{9,8},{10,11... | collective-permute-start | bytes 786440 | tf_op jit(solution)/shard_map/ppermute | solution.py:29
  43.0 26.1 %collective-permute-start.13 = (bf16[4,64,512]{2,1,0:T(8,128)(2,1)S(1)}, bf16[4,64,512]{2,1,0:T(8,128)(2,1)S(1)}, u32[]{:S(2)}, u32[]{:S(2)}) collective-permute-start(bf16[4,64,512]{2,1,0:T(8,128)(2,1)S(1)} %collective-permute-done.12.refs_0_), channel_id=1, source_target_pairs={{0,1},{1,0},{2,3},{3,2},{4,5},{5,4},{6,7},{7,6},{8,9},{9,8},{10,11... | collective-permute-start | bytes 786440 | tf_op jit(solution)/shard_map/ppermute | solution.py:29
  77.3 1.2 %collective-permute-start.20 = (f32[4,512]{1,0:T(4,128)S(1)}, f32[4,512]{1,0:T(4,128)S(1)}, u32[]{:S(2)}, u32[]{:S(2)}) collective-permute-start(f32[4,512]{1,0:T(4,128)S(1)} %pad_maximum_fusion.2), channel_id=1, source_target_pairs={{0,1},{1,0},{2,3},{3,2},{4,5},{5,4},{6,7},{7,6},{8,9},{9,8},{10,11... | collective-permute-start | bytes 24584 | tf_op jit(solution)/shard_map/ppermute | solution.py:29
  78.8 4.1 %collective-permute-start.23 = (f32[4,512]{1,0:T(4,128)S(1)}, f32[4,512]{1,0:T(4,128)S(1)}, u32[]{:S(2)}, u32[]{:S(2)}) collective-permute-start(f32[4,512]{1,0:T(4,128)S(1)} %fusion.12), channel_id=1, source_target_pairs={{0,6},{1,7},{2,4},{3,5},{4,2},{5,3},{6,0},{7,1},{8,14},{9,15},{10,... | collective-permute-start | bytes 24584 | tf_op jit(solution)/shard_map/ppermute | solution.py:29
  81.9 23.1 %collective-permute-start.16 = (bf16[4,128,512]{2,1,0:T(8,128)(2,1)}, bf16[4,128,512]{2,1,0:T(8,128)(2,1)}, u32[]{:S(2)}, u32[]{:S(2)}) collective-permute-start(bf16[4,128,512]{2,1,0:T(8,128)(2,1)} %pad_maximum_fusion), channel_id=1, source_target_pairs={{0,1},{1,0},{2,3},{3,2},{4,5},{5,4},{6,7},{7,6},{8,9},{9,8},{10,11... | collective-permute-start | bytes 1572872 | tf_op jit(solution)/shard_map/ppermute | solution.py:29
  82.4 2.5 %collective-permute-start.22 = (f32[4,512]{1,0:T(4,128)S(1)}, f32[4,512]{1,0:T(4,128)S(1)}, u32[]{:S(2)}, u32[]{:S(2)}) collective-permute-start(f32[4,512]{1,0:T(4,128)S(1)} %fusion.12), channel_id=1, source_target_pairs={{0,4},{1,5},{2,6},{3,7},{4,0},{5,1},{6,2},{7,3},{8,12},{9,13},{10,... | collective-permute-start | bytes 24584 | tf_op jit(solution)/shard_map/ppermute | solution.py:29
  82.6 2.5 %collective-permute-start.21 = (f32[4,512]{1,0:T(4,128)S(1)}, f32[4,512]{1,0:T(4,128)S(1)}, u32[]{:S(2)}, u32[]{:S(2)}) collective-permute-start(f32[4,512]{1,0:T(4,128)S(1)} %fusion.12), channel_id=1, source_target_pairs={{0,2},{1,3},{2,0},{3,1},{4,6},{5,7},{6,4},{7,5},{8,10},{9,11},{10,... | collective-permute-start | bytes 24584 | tf_op jit(solution)/shard_map/ppermute | solution.py:29
  85.2 30.5 %copy-start.1 = (bf16[64,512]{1,0:T(8,128)(2,1)S(1)}, bf16[64,512]{1,0:T(8,128)(2,1)}, u32[]{:S(2)}) copy-start(bf16[64,512]{1,0:T(8,128)(2,1)} %param.6) | copy-start | bytes 196612
  106.2 4.9 %collective-permute-start.19 = (bf16[128,512]{1,0:T(8,128)(2,1)S(1)}, bf16[128,512]{1,0:T(8,128)(2,1)S(1)}, u32[]{:S(2)}, u32[]{:S(2)}) collective-permute-start(bf16[128,512]{1,0:T(8,128)(2,1)S(1)} %get-tuple-element.52), channel_id=1, source_target_pairs={{0,6},{1,7},{2,4},{3,5},{4,2},{5,3},{6,0},{7,1},{8,14},{9,15},{10,... | collective-permute-start | bytes 393224 | tf_op jit(solution)/shard_map/ppermute | solution.py:29
  107.5 7.2 %collective-permute-start.18 = (bf16[128,512]{1,0:T(8,128)(2,1)S(1)}, bf16[128,512]{1,0:T(8,128)(2,1)S(1)}, u32[]{:S(2)}, u32[]{:S(2)}) collective-permute-start(bf16[128,512]{1,0:T(8,128)(2,1)S(1)} %get-tuple-element.53), channel_id=1, source_target_pairs={{0,4},{1,5},{2,6},{3,7},{4,0},{5,1},{6,2},{7,3},{8,12},{9,13},{10,... | collective-permute-start | bytes 393224 | tf_op jit(solution)/shard_map/ppermute | solution.py:29
  107.7 6.9 %collective-permute-start.17 = (bf16[128,512]{1,0:T(8,128)(2,1)S(1)}, bf16[128,512]{1,0:T(8,128)(2,1)S(1)}, u32[]{:S(2)}, u32[]{:S(2)}) collective-permute-start(bf16[128,512]{1,0:T(8,128)(2,1)S(1)} %get-tuple-element.51), channel_id=1, source_target_pairs={{0,2},{1,3},{2,0},{3,1},{4,6},{5,7},{6,4},{7,5},{8,10},{9,11},{10,... | collective-permute-start | bytes 393224 | tf_op jit(solution)/shard_map/ppermute | solution.py:29

commit v2 on v0

v2 whole, which is shorter than its diff:
```python
import math

import jax
import jax.numpy as jnp
from jax import lax
from jax.experimental import pallas as pl
from jax.experimental.pallas import tpu as pltpu
from jax.sharding import PartitionSpec as P

eps = 1e-06
logit_scale = 64.0
margin = 0.35
momentum_rate = 0.9
learn_rate = 0.1
weight_decay = 0.0005

LANES = 128
sharpness = logit_scale * math.log2(math.e)
HBM = pl.BlockSpec(memory_space=pltpu.HBM)
bf16 = jnp.bfloat16
f32 = jnp.float32


def dot(a, b, ca, cb):
    return lax.dot_general(a, b, (((ca,), (cb,)), ((), ())), preferred_element_type=f32)


def swap(x, axis_name, m):
    n = lax.axis_size(axis_name)
    return lax.ppermute(x, axis_name, [(i, i ^ m) for i in range(n)])


def shift(x, axis_name, m):
    n = lax.axis_size(axis_name)
    return lax.ppermute(x, axis_name, [(i, (i + m) % n) for i in range(n)])


def params(mib):
    return pltpu.CompilerParams(vmem_limit_bytes=mib << 20)


def iota(shape, axis):
    return lax.broadcasted_iota(jnp.int32, shape, axis)


def ones_where(mask):
    return mask.astype(f32).astype(bf16)


def look_up(table, hi, lo, limit):
    n_hi, n = table.shape[0], hi.shape[1]
    oh = ones_where(iota((n_hi, n), 0) == hi)
    got = jnp.zeros((LANES, n), f32)
    for bits in range(0, 8 * pieces_of(limit), 8):
        piece = lax.bitwise_and(lax.shift_right_logical(table, bits), 255).astype(f32).astype(bf16)
        got = got + float(1 << bits) * dot(piece, oh, 0, 0)
    pick = jnp.where(iota((LANES, n), 0) == lo, got, 0.0)
    return jnp.sum(pick, axis=0, keepdims=True).astype(jnp.int32)


def pieces_of(limit):
    return -(-(limit - 1).bit_length() // 8)


def tell_kernel(dims, x_ref, home_ref, row_ref, lab_ref, o_ref):
    home_rows, rows_here, _, classes, sampled = dims
    width = x_ref.shape[1]
    x = x_ref[...].astype(f32)
    scale = sharpness / jnp.sqrt(jnp.sum(x * x, axis=1, keepdims=True) + eps)
    o_ref[:rows_here, :] = (x * scale).astype(bf16)
    per = width // LANES
    lines = []
    for values, limit in ((home_ref[...] * home_rows + row_ref[...], classes), (lab_ref[...], sampled)):
        for k in range(pieces_of(limit)):
            v = lax.bitwise_and(lax.shift_right_logical(values, 8 * k), 255).astype(f32)
            for r in range(v.shape[0] // per):
                lines.append(jnp.concatenate([v[r * per + c : r * per + c + 1, :] for c in range(per)], axis=1))
    lines += [jnp.zeros_like(lines[0])] * (o_ref.shape[0] - rows_here - len(lines))
    o_ref[rows_here:, :] = jnp.concatenate(lines, axis=0).astype(bf16)


def tell(embeddings, home, row, labels, dims):
    _, rows_here, _, classes, sampled = dims
    width = embeddings.shape[1]
    lines = (row.size * pieces_of(classes) + labels.size * pieces_of(sampled)) // width
    args = [embeddings, home.reshape(-1, LANES), row.reshape(-1, LANES), labels.reshape(-1, LANES)]
    args = [pltpu.with_memory_space_constraint(x, pltpu.HBM) for x in args]
    return pl.pallas_call(
        lambda *refs: tell_kernel(dims, *refs),
        out_shape=jax.ShapeDtypeStruct((-(-(rows_here + lines) // 16) * 16, width), bf16),
        compiler_params=params(4),
        name="tell",
    )(*args)


def decode(get, row, count, number):
    total = get(row, row + count).astype(f32)
    for k in range(1, number):
        total = total + float(1 << (8 * k)) * get(row + k * count, row + (k + 1) * count).astype(f32)
    return total


def swap_groups(x, size):
    n = x.shape[1] // size
    return jnp.concatenate([x[:, (g ^ 1) * size : ((g ^ 1) + 1) * size] for g in range(n)], axis=1)


def prep_kernel(dims, shard_ref, mine_ref, away_ref, row_ref, rep_ref, cnt_ref, off_ref, known_ref, table_ref):
    home_rows, rows_here, here, classes, _ = dims
    base = shard_ref[0] * home_rows
    chips, _, width = mine_ref.shape
    blocks = home_rows // LANES
    lines, id_bytes = here // width, pieces_of(classes)
    total = jnp.zeros((LANES, blocks), f32)
    total_t = jnp.zeros((blocks, LANES), f32)
    for tile in range(2 * chips):
        ref = (mine_ref, away_ref)[tile % 2]
        ids = decode(lambda p, q: ref[tile // 2, p:q, :], rows_here, lines, id_bytes).astype(jnp.int32)
        h = ids - base
        for k in range(lines):
            a = ones_where(iota((blocks, width), 0) == lax.shift_right_arithmetic(h[k : k + 1], 7))
            b = ones_where(iota((LANES, width), 0) == lax.bitwise_and(h[k : k + 1], LANES - 1))
            total = total + dot(b, a, 1, 1)
            total_t = total_t + dot(a, b, 1, 1)
            for c in range(width // LANES):
                to = (tile * lines + k) * (width // LANES) + c
                table_ref[to : to + 1, :] = ids[k : k + 1, c * LANES : (c + 1) * LANES]
    have, have_t = ones_where(total > 0), ones_where(total_t > 0)
    before = ones_where(iota((LANES, LANES), 1) < iota((LANES, LANES), 0))
    ahead = ones_where(iota((LANES, LANES), 0) < iota((LANES, LANES), 1))
    ahead_b = ones_where(iota((blocks, blocks), 0) < iota((blocks, blocks), 1))
    before_b = ones_where(iota((blocks, blocks), 1) < iota((blocks, blocks), 0))
    sizes = jnp.broadcast_to(jnp.sum(have.astype(f32), axis=0, keepdims=True), (8, blocks))
    start = dot(sizes.astype(bf16), ahead_b, 1, 0)
    off_ref[...] = jnp.concatenate([start, start + sizes], axis=1).astype(jnp.int32)
    sizes_t = jnp.broadcast_to(jnp.sum(have_t.astype(f32), axis=1, keepdims=True), (blocks, LANES))
    start_t = dot(before_b, sizes_t.astype(bf16), 1, 0)
    pos = jnp.where(total > 0, dot(before, have, 1, 0) + start[:1], -1.0).astype(jnp.int32)
    pos_t = jnp.where(total_t > 0, dot(have_t, ahead, 1, 0) + start_t, -1.0).astype(jnp.int32)
    for k in range(blocks):
        rows = slice(k * LANES, (k + 1) * LANES)
        row_ref[k] = pos_t[k : k + 1, :]
        rep_ref[rows, :] = jnp.broadcast_to(pos[:, k : k + 1], (LANES, LANES))
        cnt_ref[rows, :] = jnp.broadcast_to(total[:, k : k + 1], (LANES, LANES))
    known_ref[...] = jnp.maximum(pos_t, 0)


def labels_kernel(dims, shard_ref, known_ref, table_ref, *refs):
    home_rows, rows_here, here, classes, sampled = dims
    z_refs, at_ref = refs[:-1], refs[-1]
    chips = at_ref.shape[0]
    width = z_refs[0].shape[1]
    shard = shard_ref[0]
    base = shard * home_rows
    lines, id_bytes = here // width, pieces_of(classes)
    known = known_ref[...]
    table = table_ref[...]
    own = 2 * rows_here
    group_rows = 2 * chips * rows_here
    lab_lines, lab_bytes = group_rows // width, pieces_of(sampled)
    per_tile = here // LANES
    for z, ref in enumerate(z_refs):
        first = rows_here + lines * id_bytes
        got = decode(lambda p, q: ref[p:q, :], first, lab_lines, lab_bytes)
        lab = jnp.concatenate([got[k : k + 1] for k in range(lab_lines)], axis=1)
        bit = 1
        while bit < 2 * chips:
            lab = jnp.where(lax.bitwise_and(shard, bit) != 0, swap_groups(lab, bit * rows_here), lab)
            bit *= 2
        lab = lab.astype(jnp.int32)
        tile = lax.bitwise_xor(lax.shift_right_logical(lab, here.bit_length() - 1), shard)
        hi = tile * per_tile + lax.shift_right_logical(lax.bitwise_and(lab, here - 1), 7)
        h = look_up(table, hi, lax.bitwise_and(lab, LANES - 1), classes) - base
        at = look_up(known, lax.shift_right_arithmetic(h, 7), lax.bitwise_and(h, LANES - 1), home_rows)
        at = jnp.where((h >= 0) & (h < home_rows), at, -1)
        for j in range(chips):
            at_ref[j, :, z * own : (z + 1) * own] = at[:, j * own : (j + 1) * own]


def prepare(shard, mine, away, dims):
    home_rows, _, _, _, sampled = dims
    vm = pl.BlockSpec(memory_space=pltpu.VMEM)
    blocks = home_rows // LANES
    i32 = jnp.int32
    return pl.pallas_call(
        lambda *refs: prep_kernel(dims, *refs),
        in_specs=[pl.BlockSpec(memory_space=pltpu.SMEM), vm, vm],
        out_specs=(vm,) * 6,
        out_shape=(
            jax.ShapeDtypeStruct((blocks, 1, LANES), i32),
            jax.ShapeDtypeStruct((home_rows, LANES), i32),
            jax.ShapeDtypeStruct((home_rows, LANES), f32),
            jax.ShapeDtypeStruct((8, 2 * blocks), i32),
            jax.ShapeDtypeStruct((blocks, LANES), i32),
            jax.ShapeDtypeStruct((sampled // LANES, LANES), i32),
        ),
        compiler_params=params(10),
        cost_estimate=pl.CostEstimate(flops=128 * sampled * LANES, bytes_accessed=1024 * home_rows, transcendentals=0),
        name="prep",
    )(shard, mine, away)


def label_places(shard, known, table, told, chips, dims):
    rows_here = dims[1]
    vm = pl.BlockSpec(memory_space=pltpu.VMEM)
    return pl.pallas_call(
        lambda *refs: labels_kernel(dims, *refs),
        in_specs=[pl.BlockSpec(memory_space=pltpu.SMEM)] + [vm] * (2 + len(told)),
        out_specs=vm,
        out_shape=jax.ShapeDtypeStruct((chips, 1, 2 * len(told) * rows_here), jnp.int32),
        compiler_params=params(12),
        cost_estimate=pl.CostEstimate(
            flops=8 * table.size * 2 * chips * len(told) * rows_here, bytes_accessed=8 * table.size, transcendentals=0
        ),
        name="places",
    )(shard, known, table, *told)


WINDOW = LANES + 16


def pack_kernel(off_ref, row_ref, cnt_ref, c_ref, what_ref, raw_ref, num_ref):
    i = pl.program_id(0)

    @pl.when(i == 0)
    def _():
        for ref in (what_ref, raw_ref, num_ref):
            ref[:16, :] = jnp.zeros((16, ref.shape[1]), ref.dtype)

    c = c_ref[...].astype(f32)
    width = c.shape[1]
    unit = (c * (1.0 / jnp.sqrt(jnp.sum(c * c, axis=1, keepdims=True) + eps))).astype(bf16)
    cnt = cnt_ref[...]
    high = jnp.floor(cnt * (1.0 / 256.0))
    low = cnt - 256.0 * high
    here = row_ref.shape[0]
    todo = []
    for k in range(here):
        rows = slice(k * LANES, (k + 1) * LANES)
        base = pl.multiple_of(lax.shift_left(lax.shift_right_logical(off_ref[0, i * here + k], 4), 4), 16)
        pick = ones_where(iota((WINDOW, LANES), 0) + base == row_ref[k])
        right = jnp.concatenate([unit[rows], c_ref[rows, :], low[rows].astype(bf16), high[rows].astype(bf16)], axis=1)
        todo.append((base, dot(pick, right, 1, 0)))
    for base, got in todo:
        num = got[:, 2 * width : 2 * width + LANES] + 256.0 * got[:, 2 * width + LANES :]
        for ref, new in ((what_ref, got[:, :width]), (raw_ref, got[:, width : 2 * width]), (num_ref, num)):
            new = new.astype(ref.dtype)
            ref[pl.ds(base, 16), :] = ref[pl.ds(base, 16), :] + new[:16]
            ref[pl.ds(pl.multiple_of(base + 16, 16), LANES), :] = new[16:]

    @pl.when(i == pl.num_programs(0) - 1)
    def _():
        for ref in (what_ref, raw_ref, num_ref):
            ref[pl.ds(pl.multiple_of(base + WINDOW, 16), 4 * LANES), :] = jnp.zeros((4 * LANES, ref.shape[1]), ref.dtype)


def pack(off, row, cnt, centres, tile):
    classes, width = centres.shape
    per = tile // LANES
    room = classes + 6 * LANES
    whole = lambda n: pl.BlockSpec((room, n), lambda i: (0, 0))
    return pl.pallas_call(
        pack_kernel,
        grid=(classes // tile,),
        in_specs=[
            pl.BlockSpec(memory_space=pltpu.SMEM),
            pl.BlockSpec((per, 1, LANES), lambda i: (i, 0, 0)),
            pl.BlockSpec((tile, LANES), lambda i: (i, 0)),
            pl.BlockSpec((tile, width), lambda i: (i, 0)),
        ],
        out_specs=(whole(width), whole(width), whole(LANES)),
        out_shape=(
            jax.ShapeDtypeStruct((room, width), bf16),
            jax.ShapeDtypeStruct((room, width), bf16),
            jax.ShapeDtypeStruct((room, LANES), f32),
        ),
        compiler_params=params(20),
        cost_estimate=pl.CostEstimate(flops=5 * classes * LANES * width, bytes_accessed=4 * classes * width, transcendentals=0),
        name="pack",
    )(off, row, cnt, centres)


def used_tile(i, steps):
    return (lax.min(i, steps[0] - 1), 0)


def logits_kernel(chunks, tile, off_ref, e0_ref, e1_ref, what_ref, num_ref, at_ref, *refs):
    l0_refs, l1_refs = refs[:chunks], refs[chunks : 2 * chunks]
    w_hbm, den_ref, turn_ref, x_ref, d_acc, cos0, cos1, w_buf, w_sem = refs[2 * chunks :]
    group, rows_here, _ = l0_refs[0].shape
    rows = cos0.shape[1]
    for j in range(chunks):
        for r, (early, late) in enumerate(((e0_ref, l0_refs[j]), (e1_ref, l1_refs[j]))):
            to = j * rows + r * rows_here
            x_ref[to : to + rows_here, :] = early[j, :rows_here, :]
            for z in range(group):
                to = j * rows + (2 * z + 2 + r) * rows_here
                x_ref[to : to + rows_here, :] = late[z]
    d_acc[...] = jnp.zeros_like(d_acc)
    used = off_ref[0, off_ref.shape[1] - 1]
    steps = lax.shift_right_logical(used + tile - 1, tile.bit_length() - 1)
    half = tile // 2

    def put(t):
        slot = lax.bitwise_and(t, 1)
        here = pl.ds(pl.multiple_of(t * tile, tile), tile)
        return pltpu.make_async_copy(w_buf.at[slot], w_hbm.at[here], w_sem.at[slot])

    def product(first, j):
        a = what_ref[pl.ds(pl.multiple_of(first, half), half), :]
        return dot(a, x_ref[pl.ds(pl.multiple_of(j * rows, rows), rows), :], 1, 1)

    def weigh(cos_ref, first, j, slot, to):
        ids = iota((half, LANES), 0) + first
        num = num_ref[pl.ds(pl.multiple_of(first, half), half), :]
        num_t = num + (math.exp(-logit_scale * margin) - 1.0)
        at = at_ref[j]
        for k in range(rows // LANES):
            cols = slice(k * LANES, (k + 1) * LANES)
            w = jnp.exp2(cos_ref[:, cols]) * jnp.where(ids == at[:, cols], num_t, num)
            d_acc[j, :, cols] += jnp.sum(w.reshape(half // 8, 8, LANES), axis=0)
            w_buf[slot, to : to + half, pl.ds(pl.multiple_of(j * rows + k * LANES, LANES), LANES)] = w.astype(bf16)

    cos0[...] = product(0, 0)

    def one(t, carry):
        @pl.when(t >= 2)
        def _():
            put(t - 2).wait()

        slot = lax.bitwise_and(t, 1)

        def chunk(j, carry):
            cos1[...] = product(t * tile + half, j)
            weigh(cos0, t * tile, j, slot, 0)
            last = j == chunks - 1
            cos0[...] = product(jnp.where(last, t + 1, t) * tile, jnp.where(last, 0, j + 1))
            weigh(cos1, t * tile + half, j, slot, half)
            return carry

        lax.fori_loop(0, chunks, chunk, 0)
        put(t).start()
        return carry

    lax.fori_loop(0, steps, one, 0)
    for back in (2, 1):

        @pl.when(steps >= back)
        def _():
            put(steps - back).wait()

    for j in range(chunks):
        den = jnp.sum(d_acc[j], axis=0, keepdims=True)
        den_ref[j] = den
        turn_ref[j] = swap_groups(den, rows_here)


def logits(off, early0, early1, late0, late1, what, num, at, tile, classes):
    chunks = len(late0)
    group, rows_here, width = late0[0].shape
    rows = 2 * (group + 1) * rows_here
    vm = pl.BlockSpec(memory_space=pltpu.VMEM)
    return pl.pallas_call(
        lambda *refs: logits_kernel(chunks, tile, *refs),
        in_specs=[pl.BlockSpec(memory_space=pltpu.SMEM)] + [vm] * (5 + 2 * chunks),
        out_specs=(HBM, vm, vm, vm),
        out_shape=(
            pltpu.HBM((classes, chunks * rows), bf16),
            jax.ShapeDtypeStruct((chunks, 1, rows), f32),
            jax.ShapeDtypeStruct((chunks, 1, rows), f32),
            jax.ShapeDtypeStruct((chunks * rows, width), bf16),
        ),
        scratch_shapes=[
            pltpu.VMEM((chunks, 8, rows), f32),
            pltpu.VMEM((tile // 2, rows), f32),
            pltpu.VMEM((tile // 2, rows), f32),
            pltpu.VMEM((2, tile, chunks * rows), bf16),
            pltpu.SemaphoreType.DMA((2,)),
        ],
        compiler_params=params(8 + 3 * chunks // 2),
        cost_estimate=pl.CostEstimate(
            flops=chunks * rows * classes * width,
            bytes_accessed=chunks * rows * classes + classes * width,
            transcendentals=chunks * rows * classes // 2,
        ),
        name="logits",
    )(off, early0, early1, what, num, at, *late0, *late1)


def own_columns(tile, own, at):
    return pl.BlockSpec((tile, own), lambda i, steps: (lax.min(i, steps[0] - 1), at))


def rows_kernel(chunks, steps_ref, what_ref, at_ref, *refs):
    w_refs, (self_ref, away_ref), acc = refs[:chunks], refs[chunks : chunks + 2], refs[chunks + 2]
    i = pl.program_id(0)
    tile = what_ref.shape[0]
    own = w_refs[0].shape[1]
    half = own // 2

    @pl.when(i == 0)
    def _():
        acc[...] = jnp.zeros_like(acc)

    @pl.when(i < steps_ref[0])
    def _():
        ids = iota((tile, own), 0) + i * tile
        left = [w[...] for w in w_refs] + [ones_where(ids == at_ref[j][:, :own]) for j in range(chunks)]
        acc[...] += dot(jnp.concatenate(left, axis=1), what_ref[...], 0, 0)

    @pl.when(i == pl.num_programs(0) - 1)
    def _():
        for j in range(chunks):
            for part in range(2):
                at = (part * chunks + j) * own
                self_ref[j, part * half : (part + 1) * half, :] = acc[at : at + half, :].astype(bf16)
                away_ref[j, part * half : (part + 1) * half, :] = acc[at + half : at + own, :].astype(bf16)


def row_parts(steps, what, at, w, own, tile):
    chunks, _, rows = at.shape
    width = what.shape[1]
    out = jax.ShapeDtypeStruct((chunks, own, width), bf16)
    whole = pl.BlockSpec((chunks, own, width), lambda i, n: (0, 0, 0))
    return pl.pallas_call(
        lambda *refs: rows_kernel(chunks, *refs),
        grid_spec=pltpu.PrefetchScalarGridSpec(
            num_scalar_prefetch=1,
            grid=(w.shape[0] // tile,),
            in_specs=[
                pl.BlockSpec((tile, width), used_tile),
                pl.BlockSpec(at.shape, lambda i, n: (0, 0, 0)),
            ]
            + [own_columns(tile, own, j * rows // own) for j in range(chunks)],
            out_specs=(whole, whole),
            scratch_shapes=[pltpu.VMEM((2 * chunks * own, width), f32)],
        ),
        out_shape=(out, out),
        compiler_params=params(8 + 3 * chunks),
        cost_estimate=pl.CostEstimate(
            flops=2 * chunks * own * w.shape[0] * width, bytes_accessed=2 * what.size, transcendentals=0
        ),
        name="rows",
    )(steps, what, at, *[w] * chunks)


def update_kernel(chunks, step, tile, off_ref, at_ref, rep_ref, raw_ref, c_hbm, m_hbm, *refs):
    w_hbm, x_ref, d_refs = refs[0], refs[1], refs[2 : 2 + chunks]
    mo_hbm, co_hbm, scale_ref, rate_ref, dw_ref, c_buf, m_buf, c_new, m_new, buf, w_sem, c_sem, m_sem, co_sem, mo_sem = refs[2 + chunks :]
    classes, width = c_buf.shape
    per = tile // LANES
    groups = classes // tile
    blocks = off_ref.shape[1] // 2
    rows = x_ref.shape[0] // chunks
    used = off_ref[0, 2 * blocks - 1]

    def span(g):
        return pl.ds(pl.multiple_of(g * tile, tile), tile)

    def ins(g):
        at = span(g)
        return (
            pltpu.make_async_copy(c_hbm.at[at], c_buf.at[at], c_sem.at[g]),
            pltpu.make_async_copy(m_hbm.at[at], m_buf.at[at], m_sem.at[g]),
        )

    def outs(g):
        at, slot = span(g), lax.bitwise_and(g, 1)
        return (
            pltpu.make_async_copy(c_new.at[slot], co_hbm.at[at], co_sem.at[slot]),
            pltpu.make_async_copy(m_new.at[slot], mo_hbm.at[at], mo_sem.at[slot]),
        )

    def fetch(start):
        slot = lax.bitwise_and(lax.shift_right_logical(start, step.bit_length() - 1), 1)
        at = pl.ds(pl.multiple_of(start, step), step)
        return slot, pltpu.make_async_copy(w_hbm.at[at], buf.at[slot], w_sem.at[slot])

    @pl.when(used > 0)
    def _():
        fetch(0)[1].start()

    for g in range(groups):
        for copy in ins(g):
            copy.start()
    for j in range(chunks):
        den = d_refs[0][j]
        for q in range(1, chunks):
            den = den + d_refs[q][j ^ q]
        rate = logit_scale / den
        rate_ref[j] = rate.astype(bf16)
        if j == 0:
            scale_ref[...] = rate

    def one(done):
        @pl.when(done + step < used)
        def _():
            fetch(done + step)[1].start()

        slot, copy = fetch(done)
        at = pl.ds(pl.multiple_of(done, step), step)
        copy.wait()
        exact = min(step, 256)
        ids = iota((exact, rows), 0).astype(f32).astype(bf16)
        lines = []
        for h in range(0, step, exact):
            parts = []
            for j in range(chunks):
                place = at_ref[j] - (done + h)
                place = jnp.where((place >= 0) & (place < exact), place, -1).astype(f32).astype(bf16)
                g = buf[slot, h : h + exact, j * rows : (j + 1) * rows] * rate_ref[j]
                parts.append(jnp.where(ids == place, g - jnp.asarray(logit_scale, bf16), g))
            lines.append(jnp.concatenate(parts, axis=1))
        dw = dot(jnp.concatenate(lines, axis=0), x_ref[...], 1, 0)
        c = raw_ref[at, :].astype(f32)
        inv = 1.0 / jnp.sqrt(jnp.sum(c * c, axis=1, keepdims=True) + eps)
        along = jnp.sum(c * dw, axis=1, keepdims=True) * (inv * inv)
        dw_ref[at, :] = ((dw - c * along) * (inv * (1.0 / sharpness))).astype(bf16)
        dw_ref[pl.ds(pl.multiple_of(done + step, step), 2 * LANES), :] = jnp.zeros((2 * LANES, width), bf16)
        return done + step

    def group(g, done):
        done = lax.while_loop(lambda d: d < off_ref[0, blocks + (g + 1) * per - 1], one, done)
        for copy in ins(g):
            copy.wait()
        slot = lax.bitwise_and(g, 1)

        @pl.when(g >= 2)
        def _():
            for copy in outs(g - 2):
                copy.wait()

        lane = iota((LANES, LANES), 1)
        for k in range(per):
            base = pl.multiple_of(lax.shift_left(lax.shift_right_logical(off_ref[0, g * per + k], 4), 4), 16)
            mine = pl.ds(pl.multiple_of(g * tile + k * LANES, LANES), LANES)
            to = slice(k * LANES, (k + 1) * LANES)
            place = rep_ref[mine, :] - base
            place = jnp.concatenate([ones_where(place == lane), ones_where(place == lane + LANES)], axis=1)
            dw = dot(place, dw_ref[pl.ds(base, 2 * LANES), :], 1, 0)
            c = c_buf[mine, :].astype(f32)
            m = momentum_rate * m_buf[mine, :] + dw + weight_decay * c
            m_new[slot, to, :] = m
            c_new[slot, to, :] = (c - learn_rate * m).astype(bf16)
        for copy in outs(g):
            copy.start()
        return done

    @pl.when(used == 0)
    def _():
        dw_ref[: 2 * LANES, :] = jnp.zeros((2 * LANES, width), bf16)

    lax.fori_loop(0, groups, group, 0)
    for g in range(max(0, groups - 2), groups):
        for copy in outs(g):
            copy.wait()


def update(off, at, rep, raw, centres, momentum, w, x, dens, tile, step):
    chunks = len(dens)
    classes, width = centres.shape
    rows = x.shape[0] // chunks
    vm = pl.BlockSpec(memory_space=pltpu.VMEM)
    sems = pltpu.SemaphoreType.DMA((classes // tile,))
    return pl.pallas_call(
        lambda *refs: update_kernel(chunks, step, tile, *refs),
        in_specs=[pl.BlockSpec(memory_space=pltpu.SMEM), vm, vm, vm, HBM, HBM, HBM] + [vm] * (1 + chunks),
        out_specs=(HBM, HBM, vm),
        out_shape=(
            jax.ShapeDtypeStruct((classes, width), f32),
            jax.ShapeDtypeStruct((classes, width), bf16),
            jax.ShapeDtypeStruct((1, rows), f32),
        ),
        scratch_shapes=[
            pltpu.VMEM((chunks, 1, rows), bf16),
            pltpu.VMEM((classes + 2 * LANES + step, width), bf16),
            pltpu.VMEM((classes, width), bf16),
            pltpu.VMEM((classes, width), f32),
            pltpu.VMEM((2, tile, width), bf16),
            pltpu.VMEM((2, tile, width), f32),
            pltpu.VMEM((2, step, chunks * rows), bf16),
            pltpu.SemaphoreType.DMA((2,)),
            sems,
            sems,
            pltpu.SemaphoreType.DMA((2,)),
            pltpu.SemaphoreType.DMA((2,)),
        ],
        compiler_params=params(22 + 3 * chunks),
        cost_estimate=pl.CostEstimate(
            flops=rows * chunks * classes * width,
            bytes_accessed=rows * chunks * classes + 12 * classes * width,
            transcendentals=0,
        ),
        name="update",
    )(off, at, rep, raw, centres, momentum, w, x, *dens)


def body(embeddings, labels, centres, momentum, sample_home, sample_row):
    shards = lax.axis_size("cls")
    group = lax.axis_size("dp")
    chips = shards // 2
    home_rows, _ = centres.shape
    rows_here = embeddings.shape[0]
    here = sample_row.shape[0]
    classes, sampled = shards * home_rows, shards * here
    shard = lax.axis_index("cls")

    dims = (home_rows, rows_here, here, classes, sampled)
    told = tell(embeddings, sample_home, sample_row, labels, dims)

    from_z = [shift(told, "dp", m) for m in (1, group - 1)] + [shift(told, "dp", m) for m in range(2, group - 1)]
    early = jnp.stack([told] + [swap(told, "cls", 2 * q) for q in range(1, chips)])
    early_away = swap(early, "cls", 1)
    late0 = jnp.stack([z[:rows_here] for z in from_z])
    late = [late0] + [swap(late0, "cls", 2 * q) for q in range(1, chips)]
    late_away = []
    for x in late:
        late_away.append(swap(x, "cls", 1))

    me = shard.astype(jnp.int32).reshape(1)
    in_hbm = lambda x: pltpu.with_memory_space_constraint(x, pltpu.HBM)
    row, rep, cnt, off, known, table = prepare(me, early, early_away, dims)
    what, raw, num = pack(off, row, cnt, in_hbm(centres), min(1024, home_rows))
    at = label_places(me, known, table, [told] + from_z, chips, dims)
    tile = min(512, home_rows)
    w, own_den, turned, x = logits(off, early, early_away, late, late_away, what, num, at, tile, home_rows)
    w = in_hbm(w)

    den = own_den + swap(turned, "cls", 1)
    dens = [den] + [swap(den, "cls", 2 * q) for q in range(1, chips)]

    steps = lax.max(lax.shift_right_logical(off[0, -1:] + tile - 1, tile.bit_length() - 1), 1)
    self_part, away_part = row_parts(steps, what, at, w, 2 * rows_here, tile)
    pair = self_part.astype(f32) + swap(away_part, "cls", 1).astype(f32)
    sums = [swap(pair[q].astype(bf16), "cls", 2 * q) for q in range(1, chips)]

    momentum_new, centres_new, scale = update(
        off, at, rep, raw, in_hbm(centres), in_hbm(momentum), w, x, dens, min(512, home_rows), 512
    )
    total = pair[0]
    for got in sums:
        total = total + got.astype(f32)
    xfloat = embeddings.astype(f32)
    row_norm = jnp.sqrt(jnp.sum(xfloat * xfloat, axis=1, keepdims=True) + eps)
    unit = xfloat / row_norm
    scale = scale[0, :rows_here][:, None]
    dunit = total[:rows_here] * scale - logit_scale * total[rows_here:]
    emb_grad = (dunit - unit * jnp.sum(unit * dunit, axis=1, keepdims=True)) / row_norm
    return (emb_grad, momentum_new, centres_new)


def solution(mesh):
    placed = (
        P(("dp", "cls"), None),
        P("dp"),
        P("cls", None),
        P("cls", None),
        P("cls", None),
        P("cls"),
    )
    return jax.shard_map(
        body,
        mesh=mesh,
        in_specs=placed,
        out_specs=(P(("dp", "cls"), None), P("cls", None), P("cls", None)),
        check_vma=False,
    )
```

time: 394 us -> 99.7 us (0.25)
  waiting for transfers between devices: 124 us -> 10.7 us
  local copies, waits for them, and re-layouts: 86.5 us -> 0.64 us
  blocking collectives: 73.8 us -> 0 us
  other arithmetic: 74.2 us -> 2.23 us
  Pallas kernels: 0 us -> 55 us
  starting transfers between devices: 10.7 us -> 28.3 us
  between operations: 15.6 us -> 1.55 us
  matrix products: 7.44 us -> 0 us
    psum x1 -> x0, waiting for transfers between devices: 86.7 us -> none  [body(): summed = lax.psum(dfetched.astype(jnp.bfloat16), 'dp').astype(jnp.float32)]
    gather x3 -> x0, local copies, waits for them, and re-layouts: 60.3 us -> none  [the longest x2 40.1 us: body(): fetched = arrived[home_shard, slot_rank]]
    pallas_call x0 -> x7, Pallas kernels: none -> 55 us  [the longest x1 20.2 us: update(): pl.pallas_call(lambda *refs: update_kernel(chunks, step, tile, *refs), in...]
    all_gather x1 -> x0, blocking collectives: 53.1 us -> none  [body(): lax.all_gather(normalized_embedding, 'cls', axis=0, tiled=True)]
    reduce_scatter x1 -> x0, waiting for transfers between devices: 37.6 us -> none  [body(): lax.psum_scatter(jnp.dot(grad_logit, what, preferred_element_type=jnp.flo...]
    scatter-add x1 -> x0, other arithmetic: 35.5 us -> none  [body(): centre_grad = jnp.zeros((home_rows, width), jnp.float32).at[incoming.resh...]
    ppermute x0 -> x22, starting transfers between devices: none -> 28.3 us  [the longest x19 24.4 us: swap(): return lax.ppermute(x, axis_name, [(i, i ^ m) for i in range(n)])]
    unnamed x10 -> x2, local copies, waits for them, and re-layouts: 21.8 us -> 0.01 us
  transfers between devices with their start and end apart: 4 -> 22, of which waited for: 2 -> 5; matrix products, arithmetic and copies ran while one was open for 4% -> 2% of each run, Pallas kernels for 0% -> 38%
where the time goes in v2:
time: 99.7 us; the launch traced here: 98.5 us
  Pallas kernels  55 us (55%)
  starting transfers between devices  28.3 us (28%)
  waiting for transfers between devices  10.7 us (11%)
  other arithmetic  2.23 us (2%)
  between operations  1.55 us (2%)
    ppermute x19, starting transfers between devices, swap(): return lax.ppermute(x, axis_name, [(i, i ^ m) for i in range(n)])  24.4 us
    pallas_call x1, Pallas kernels, update(): pl.pallas_call(lambda *refs: update_kernel(chunks, step, tile, *refs), in...  20.2 us
    pallas_call x1, Pallas kernels, logits(): pl.pallas_call(lambda *refs: logits_kernel(chunks, tile, *refs), in_specs...  16.7 us
    pallas_call x1, Pallas kernels, row_parts(): pl.pallas_call(lambda *refs: rows_kernel(chunks, *refs), grid_spec=pltpu....  6.86 us
    ppermute x19, waiting for transfers between devices, swap(): return lax.ppermute(x, axis_name, [(i, i ^ m) for i in range(n)])  6.41 us
    pallas_call x1, Pallas kernels, pack(): pl.pallas_call(pack_kernel, grid=(classes // tile,), in_specs=[pl.BlockSp...  5.89 us
    ppermute x3, waiting for transfers between devices, shift(): return lax.ppermute(x, axis_name, [(i, (i + m) % n) for i in range(n)])  4.27 us
    ppermute x3, starting transfers between devices, shift(): return lax.ppermute(x, axis_name, [(i, (i + m) % n) for i in range(n)])  3.97 us
  transfers between devices with their start and end apart: 22, of which 5 were waited for; matrix products, arithmetic and copies ran while one was open for 2% of the time, Pallas kernels for 38%

profile of v2, /device:TPU:1, one launch (start us, length us, event | category | flops | bytes accessed | tf_op | source)
XLA Modules:
  0.0 98.5 jit_solution(14062528850651148620)
XLA Ops:
  0.6 1.0 %tell.1.refs_3_ = bf16[80,512]{1,0:T(8,128)(2,1)S(1)} custom-call(bf16[64,512]{1,0:T(8,128)(2,1)} %refs_0_.1, s32[16,128]{1,0:T(8,128)} %bitcast.35, s32[16,128]{1,0:T(8,128)} %bitcast.36, s32[4,128]{1,0:T(4,128)} %bitcast.37), custom_call_target="tpu_custom_call" | custom-call | tf_op jit(solution)/shard_map/tell/pallas_call | solution.py:88
  1.6 3.0 %collective-permute-start.2 = (bf16[80,512]{1,0:T(8,128)(2,1)S(1)}, bf16[80,512]{1,0:T(8,128)(2,1)S(1)}, u32[]{:S(2)}, u32[]{:S(2)}) collective-permute-start(bf16[80,512]{1,0:T(8,128)(2,1)S(1)} %tell.1.refs_3_), channel_id=1, source_target_pairs={{0,6},{1,7},{2,4},{3,5},{4,2},{5,3},{6,0},{7,1},{8,14},{9,15},{10,... | collective-permute-start | bytes 245768 | tf_op jit(solution)/shard_map/ppermute | solution.py:30
  4.7 0.2 collective-permute-start.1
  4.9 0.1 collective-permute-start
  5.0 1.4 %collective-permute-start.4 = (bf16[80,512]{1,0:T(8,128)(2,1)S(1)}, bf16[80,512]{1,0:T(8,128)(2,1)S(1)}, u32[]{:S(2)}, u32[]{:S(2)}) collective-permute-start(bf16[80,512]{1,0:T(8,128)(2,1)S(1)} %tell.1.refs_3_), channel_id=1, source_target_pairs={{0,8},{8,16},{16,24},{24,0},{1,9},{9,17},{17,25},{25,1},{2,10},{10... | collective-permute-start | bytes 245768 | tf_op jit(solution)/shard_map/ppermute | solution.py:35
  6.5 2.0 %collective-permute-start.5 = (bf16[80,512]{1,0:T(8,128)(2,1)S(1)}, bf16[80,512]{1,0:T(8,128)(2,1)S(1)}, u32[]{:S(2)}, u32[]{:S(2)}) collective-permute-start(bf16[80,512]{1,0:T(8,128)(2,1)S(1)} %tell.1.refs_3_), channel_id=1, source_target_pairs={{0,24},{8,0},{16,8},{24,16},{1,25},{9,1},{17,9},{25,17},{2,26},{10... | collective-permute-start | bytes 245768 | tf_op jit(solution)/shard_map/ppermute | solution.py:35
  8.5 0.0 collective-permute-done.2
  8.5 0.5 collective-permute-start.6
  9.0 0.0 collective-permute-done.1
  9.0 0.1 collective-permute-done
  9.1 2.3 %collective-permute-start.3 = (bf16[4,80,512]{2,1,0:T(8,128)(2,1)S(1)}, bf16[4,80,512]{2,1,0:T(8,128)(2,1)S(1)}, u32[]{:S(2)}, u32[]{:S(2)}) collective-permute-start(bf16[4,80,512]{2,1,0:T(8,128)(2,1)S(1)} %pad_maximum_fusion.refs_1_), channel_id=1, source_target_pairs={{0,1},{1,0},{2,3},{3,2},{4,5},{5,4},{6,7},{7,6},{8,9},{9,8},{10,11... | collective-permute-start | bytes 983048 | tf_op jit(solution)/shard_map/ppermute | solution.py:30
  11.4 4.3 %collective-permute-done.6.refs_6_ = bf16[80,512]{1,0:T(8,128)(2,1)S(1)} collective-permute-done((bf16[80,512]{1,0:T(8,128)(2,1)S(1)}, bf16[80,512]{1,0:T(8,128)(2,1)S(1)}, u32[]{:S(2)}, u32[]{:S(2)}) %collective-permute-start.6) | collective-permute-done | bytes 81952 | tf_op jit(solution)/shard_map/ppermute | solution.py:35
  15.7 0.0 collective-permute-done.5.refs_5_
  15.7 0.0 collective-permute-done.4.refs_4_
  15.8 1.4 %collective-permute-start.7 = (bf16[3,64,512]{2,1,0:T(8,128)(2,1)S(1)}, bf16[3,64,512]{2,1,0:T(8,128)(2,1)S(1)}, u32[]{:S(2)}, u32[]{:S(2)}) collective-permute-start(bf16[3,64,512]{2,1,0:T(8,128)(2,1)S(1)} %pad_maximum_fusion.1.refs_6_), channel_id=1, source_target_pairs={{0,2},{1,3},{2,0},{3,1},{4,6},{5,7},{6,4},{7,5},{8,10},{9,11},{10,... | collective-permute-start | bytes 589832 | tf_op jit(solution)/shard_map/ppermute | solution.py:30
  17.2 1.2 %collective-permute-start.8 = (bf16[3,64,512]{2,1,0:T(8,128)(2,1)S(1)}, bf16[3,64,512]{2,1,0:T(8,128)(2,1)S(1)}, u32[]{:S(2)}, u32[]{:S(2)}) collective-permute-start(bf16[3,64,512]{2,1,0:T(8,128)(2,1)S(1)} %pad_maximum_fusion.1.refs_6_), channel_id=1, source_target_pairs={{0,4},{1,5},{2,6},{3,7},{4,0},{5,1},{6,2},{7,3},{8,12},{9,13},{10,... | collective-permute-start | bytes 589832 | tf_op jit(solution)/shard_map/ppermute | solution.py:30
  18.4 0.1 collective-permute-start.9
  18.5 2.6 %collective-permute-start.10 = (bf16[3,64,512]{2,1,0:T(8,128)(2,1)S(1)}, bf16[3,64,512]{2,1,0:T(8,128)(2,1)S(1)}, u32[]{:S(2)}, u32[]{:S(2)}) collective-permute-start(bf16[3,64,512]{2,1,0:T(8,128)(2,1)S(1)} %pad_maximum_fusion.1.refs_6_), channel_id=1, source_target_pairs={{0,1},{1,0},{2,3},{3,2},{4,5},{5,4},{6,7},{7,6},{8,9},{9,8},{10,11... | collective-permute-start | bytes 589832 | tf_op jit(solution)/shard_map/ppermute | solution.py:30
  21.1 0.0 collective-permute-done.7.refs_7_
  21.1 4.0 %collective-permute-start.11 = (bf16[3,64,512]{2,1,0:T(8,128)(2,1)S(1)}, bf16[3,64,512]{2,1,0:T(8,128)(2,1)S(1)}, u32[]{:S(2)}, u32[]{:S(2)}) collective-permute-start(bf16[3,64,512]{2,1,0:T(8,128)(2,1)S(1)} %collective-permute-done.7.refs_7_), channel_id=1, source_target_pairs={{0,1},{1,0},{2,3},{3,2},{4,5},{5,4},{6,7},{7,6},{8,9},{9,8},{10,11... | collective-permute-start | bytes 589832 | tf_op jit(solution)/shard_map/ppermute | solution.py:30
  25.0 0.0 collective-permute-done.8.refs_8_
  25.0 3.8 %collective-permute-start.12 = (bf16[3,64,512]{2,1,0:T(8,128)(2,1)S(1)}, bf16[3,64,512]{2,1,0:T(8,128)(2,1)S(1)}, u32[]{:S(2)}, u32[]{:S(2)}) collective-permute-start(bf16[3,64,512]{2,1,0:T(8,128)(2,1)S(1)} %collective-permute-done.8.refs_8_), channel_id=1, source_target_pairs={{0,1},{1,0},{2,3},{3,2},{4,5},{5,4},{6,7},{7,6},{8,9},{9,8},{10,11... | collective-permute-start | bytes 589832 | tf_op jit(solution)/shard_map/ppermute | solution.py:30
  28.9 0.0 collective-permute-done.9.refs_9_
  28.9 0.0 collective-permute-start.13
  28.9 1.0 fusion.3
  29.9 0.0 collective-permute-done.3.refs_2_
  29.9 3.0 %prep.1 = (s32[32,1,128]{2,1,0:T(1,128)S(1)}, s32[4096,128]{1,0:T(8,128)S(1)}, f32[4096,128]{1,0:T(8,128)S(1)}, s32[8,64]{1,0:T(8,128)S(1)}, s32[32,128]{1,0:T(8,128)S(1)}, /*index=5*/s32[128,128]{1,0:T(8,128)S(1)}) custom-call(s32[1]{0:T(128)} %bitcast.refs_0_, bf16[4,80,512]{2,1,0:T(8,128)(2,1)S(1)} %pad_maximum_fusion.refs_1_, ...), custom_call_target="tpu_custom_call" | custom-call | flops 268435456 | bytes 4194304 | tf_op jit(solution)/shard_map/prep/pallas_call | solution.py:185
  32.8 0.6 slice.36
  34.1 1.5 %places.1.refs_5_.refs_2_.refs_1_ = s32[4,1,512]{2,1,0:T(1,128)S(1)} custom-call(s32[1]{0:T(128)} %bitcast.refs_0_, s32[32,128]{1,0:T(8,128)S(1)} %get-tuple-element.25.refs_1_, s32[128,128]{1,0:T(8,128)S(1)} %get-tuple-element.26.refs_2_, bf16[80,512]{1,0:T(8,128)(2,1)S(1)} %tell.1.refs_3_, bf16[80,512]{1,0:T(8,128)(2,1)S(1)} %collective-permute-done.4.refs_4_, ...), custom_call_target="tpu_custom_call" | custom-call | flops 268435456 | bytes 131072 | tf_op jit(solution)/shard_map/places/pallas_call | solution.py:206
  35.5 5.9 %pack.1 = (bf16[4864,512]{1,0:T(8,128)(2,1)S(1)}, bf16[4864,512]{1,0:T(8,128)(2,1)S(1)}, f32[4864,128]{1,0:T(8,128)S(1)}) custom-call(s32[8,64]{1,0:T(8,128)S(1)} %get-tuple-element.21.off_ref.refs_0_, s32[32,1,128]{2,1,0:T(1,128)S(1)} %get-tuple-element.22.row_ref, f32[4096,128]{1,0:T(8,128)S(1)} %get-tuple-element.23.cnt_ref, bf16[4096,512]{1,0:T(8,128)(2,1)} %refs_4_.1), custom_call_target="tpu_custom_call" | custom-call | flops 1342177280 | bytes 8388608 | tf_op jit(solution)/shard_map/pack/pallas_call | solution.py:262
  41.4 0.0 collective-permute-done.10.refs_10_
  41.4 0.0 collective-permute-done.11.refs_11_
  41.5 0.0 collective-permute-done.12.refs_12_
  41.5 0.0 collective-permute-done.13.refs_13_
  41.5 16.7 %logits.1 = (bf16[4096,2048]{1,0:T(8,128)(2,1)}, f32[4,1,512]{2,1,0:T(1,128)S(1)}, f32[4,1,512]{2,1,0:T(1,128)S(1)}, bf16[2048,512]{1,0:T(8,128)(2,1)S(1)}) custom-call(s32[8,64]{1,0:T(8,128)S(1)} %get-tuple-element.21.off_ref.refs_0_, bf16[4,80,512]{2,1,0:T(8,128)(2,1)S(1)} %pad_maximum_fusion.refs_1_, ...), custom_call_target="tpu_custom_call" | custom-call | flops 4294967296 | bytes 10485760 | tf_op jit(solution)/shard_map/logits/pallas_call | solution.py:363
  58.2 0.1 collective-permute-start.18
  58.3 6.9 %rows.1 = (bf16[4,128,512]{2,1,0:T(8,128)(2,1)S(1)}, bf16[4,128,512]{2,1,0:T(8,128)(2,1)S(1)}) custom-call(s32[1]{0:T(128)} %bitcast.8.refs_0_, bf16[4864,512]{1,0:T(8,128)(2,1)S(1)} %get-tuple-element.24.refs_3_.refs_1_, s32[4,1,512]{2,1,0:T(1,128)S(1)} %places.1.refs_5_.refs_2_.refs_1_, ...), custom_call_target="tpu_custom_call" | custom-call | flops 2147483648 | bytes 4980736 | tf_op jit(solution)/shard_map/rows/pallas_call | solution.py:425
  65.1 0.1 collective-permute-start.14
  65.2 0.0 collective-permute-done.18
  65.2 0.1 collective-permute-start.19
  65.3 0.1 collective-permute-start.20
  65.4 2.6 %collective-permute-start.21 = (f32[4,1,512]{2,1,0:T(1,128)S(1)}, f32[4,1,512]{2,1,0:T(1,128)S(1)}, u32[]{:S(2)}, u32[]{:S(2)}) collective-permute-start(f32[4,1,512]{2,1,0:T(1,128)S(1)} %add.35.refs_8_), channel_id=1, source_target_pairs={{0,6},{1,7},{2,4},{3,5},{4,2},{5,3},{6,0},{7,1},{8,14},{9,15},{10,... | collective-permute-start | bytes 24584 | tf_op jit(solution)/shard_map/ppermute | solution.py:30
  68.0 0.0 collective-permute-done.19.refs_9_
  68.0 0.0 collective-permute-done.20.refs_10_
  68.0 1.0 %collective-permute-done.21.refs_11_ = f32[4,1,512]{2,1,0:T(1,128)S(1)} collective-permute-done((f32[4,1,512]{2,1,0:T(1,128)S(1)}, f32[4,1,512]{2,1,0:T(1,128)S(1)}, u32[]{:S(2)}, u32[]{:S(2)}) %collective-permute-start.21) | collective-permute-done | bytes 8224 | tf_op jit(solution)/shard_map/ppermute | solution.py:30
  69.0 20.2 %update.1 = (f32[4096,512]{1,0:T(8,128)}, bf16[4096,512]{1,0:T(8,128)(2,1)}, f32[1,512]{1,0:T(1,128)S(1)}) custom-call(s32[8,64]{1,0:T(8,128)S(1)} %get-tuple-element.21.off_ref.refs_0_, s32[4,1,512]{2,1,0:T(1,128)S(1)} %places.1.refs_5_.refs_2_.refs_1_, s32[4096,128]{1,0:T(8,128)S(1)} %get-tuple-element.31.refs_2_, ...), custom_call_target="tpu_custom_call" | custom-call | flops 4294967296 | bytes 33554432 | tf_op jit(solution)/shard_map/update/pallas_call | solution.py:565
  89.2 0.0 copy-start
  89.2 0.0 collective-permute-done.14
  89.2 0.2 fusion.5
  89.4 0.1 collective-permute-start.17
  89.5 0.1 collective-permute-start.16
  89.6 2.6 %collective-permute-start.15 = (bf16[128,512]{1,0:T(8,128)(2,1)S(1)}, bf16[128,512]{1,0:T(8,128)(2,1)S(1)}, u32[]{:S(2)}, u32[]{:S(2)}) collective-permute-start(bf16[128,512]{1,0:T(8,128)(2,1)S(1)} %get-tuple-element.41), channel_id=1, source_target_pairs={{0,2},{1,3},{2,0},{3,1},{4,6},{5,7},{6,4},{7,5},{8,10},{9,11},{10,... | collective-permute-start | bytes 393224 | tf_op jit(solution)/shard_map/ppermute | solution.py:30
  92.1 3.1 %collective-permute-done.17 = bf16[128,512]{1,0:T(8,128)(2,1)S(1)} collective-permute-done((bf16[128,512]{1,0:T(8,128)(2,1)S(1)}, bf16[128,512]{1,0:T(8,128)(2,1)S(1)}, u32[]{:S(2)}, u32[]{:S(2)}) %collective-permute-start.17) | collective-permute-done | bytes 131104 | tf_op jit(solution)/shard_map/ppermute | solution.py:30
  95.2 2.2 %collective-permute-done.16 = bf16[128,512]{1,0:T(8,128)(2,1)S(1)} collective-permute-done((bf16[128,512]{1,0:T(8,128)(2,1)S(1)}, bf16[128,512]{1,0:T(8,128)(2,1)S(1)}, u32[]{:S(2)}, u32[]{:S(2)}) %collective-permute-start.16) | collective-permute-done | bytes 131104 | tf_op jit(solution)/shard_map/ppermute | solution.py:30
  97.4 0.0 collective-permute-done.15
  97.4 0.1 fusion.2
  97.5 0.0 copy-done
  97.5 0.2 multiply_reduce_fusion
  97.7 0.8 subtract_divide_fusion
  (9 shorter events, 0.1 us)
Async XLA Ops:
  1.6 6.9 %collective-permute-start.2 = (bf16[80,512]{1,0:T(8,128)(2,1)S(1)}, bf16[80,512]{1,0:T(8,128)(2,1)S(1)}, u32[]{:S(2)}, u32[]{:S(2)}) collective-permute-start(bf16[80,512]{1,0:T(8,128)(2,1)S(1)} %tell.1.refs_3_), channel_id=1, source_target_pairs={{0,6},{1,7},{2,4},{3,5},{4,2},{5,3},{6,0},{7,1},{8,14},{9,15},{10,... | collective-permute-start | bytes 245768 | tf_op jit(solution)/shard_map/ppermute | solution.py:30
  4.7 4.3 %collective-permute-start.1 = (bf16[80,512]{1,0:T(8,128)(2,1)S(1)}, bf16[80,512]{1,0:T(8,128)(2,1)S(1)}, u32[]{:S(2)}, u32[]{:S(2)}) collective-permute-start(bf16[80,512]{1,0:T(8,128)(2,1)S(1)} %tell.1.refs_3_), channel_id=1, source_target_pairs={{0,4},{1,5},{2,6},{3,7},{4,0},{5,1},{6,2},{7,3},{8,12},{9,13},{10,... | collective-permute-start | bytes 245768 | tf_op jit(solution)/shard_map/ppermute | solution.py:30
  4.9 4.2 %collective-permute-start = (bf16[80,512]{1,0:T(8,128)(2,1)S(1)}, bf16[80,512]{1,0:T(8,128)(2,1)S(1)}, u32[]{:S(2)}, u32[]{:S(2)}) collective-permute-start(bf16[80,512]{1,0:T(8,128)(2,1)S(1)} %tell.1.refs_3_), channel_id=1, source_target_pairs={{0,2},{1,3},{2,0},{3,1},{4,6},{5,7},{6,4},{7,5},{8,10},{9,11},{10,... | collective-permute-start | bytes 245768 | tf_op jit(solution)/shard_map/ppermute | solution.py:30
  5.0 10.7 %collective-permute-start.4 = (bf16[80,512]{1,0:T(8,128)(2,1)S(1)}, bf16[80,512]{1,0:T(8,128)(2,1)S(1)}, u32[]{:S(2)}, u32[]{:S(2)}) collective-permute-start(bf16[80,512]{1,0:T(8,128)(2,1)S(1)} %tell.1.refs_3_), channel_id=1, source_target_pairs={{0,8},{8,16},{16,24},{24,0},{1,9},{9,17},{17,25},{25,1},{2,10},{10... | collective-permute-start | bytes 245768 | tf_op jit(solution)/shard_map/ppermute | solution.py:35
  6.5 9.2 %collective-permute-start.5 = (bf16[80,512]{1,0:T(8,128)(2,1)S(1)}, bf16[80,512]{1,0:T(8,128)(2,1)S(1)}, u32[]{:S(2)}, u32[]{:S(2)}) collective-permute-start(bf16[80,512]{1,0:T(8,128)(2,1)S(1)} %tell.1.refs_3_), channel_id=1, source_target_pairs={{0,24},{8,0},{16,8},{24,16},{1,25},{9,1},{17,9},{25,17},{2,26},{10... | collective-permute-start | bytes 245768 | tf_op jit(solution)/shard_map/ppermute | solution.py:35
  8.5 7.2 %collective-permute-start.6 = (bf16[80,512]{1,0:T(8,128)(2,1)S(1)}, bf16[80,512]{1,0:T(8,128)(2,1)S(1)}, u32[]{:S(2)}, u32[]{:S(2)}) collective-permute-start(bf16[80,512]{1,0:T(8,128)(2,1)S(1)} %tell.1.refs_3_), channel_id=1, source_target_pairs={{0,16},{8,24},{16,0},{24,8},{1,17},{9,25},{17,1},{25,9},{2,18},{10... | collective-permute-start | bytes 245768 | tf_op jit(solution)/shard_map/ppermute | solution.py:35
  9.1 20.7 %collective-permute-start.3 = (bf16[4,80,512]{2,1,0:T(8,128)(2,1)S(1)}, bf16[4,80,512]{2,1,0:T(8,128)(2,1)S(1)}, u32[]{:S(2)}, u32[]{:S(2)}) collective-permute-start(bf16[4,80,512]{2,1,0:T(8,128)(2,1)S(1)} %pad_maximum_fusion.refs_1_), channel_id=1, source_target_pairs={{0,1},{1,0},{2,3},{3,2},{4,5},{5,4},{6,7},{7,6},{8,9},{9,8},{10,11... | collective-permute-start | bytes 983048 | tf_op jit(solution)/shard_map/ppermute | solution.py:30
  15.8 5.3 %collective-permute-start.7 = (bf16[3,64,512]{2,1,0:T(8,128)(2,1)S(1)}, bf16[3,64,512]{2,1,0:T(8,128)(2,1)S(1)}, u32[]{:S(2)}, u32[]{:S(2)}) collective-permute-start(bf16[3,64,512]{2,1,0:T(8,128)(2,1)S(1)} %pad_maximum_fusion.1.refs_6_), channel_id=1, source_target_pairs={{0,2},{1,3},{2,0},{3,1},{4,6},{5,7},{6,4},{7,5},{8,10},{9,11},{10,... | collective-permute-start | bytes 589832 | tf_op jit(solution)/shard_map/ppermute | solution.py:30
  17.2 7.9 %collective-permute-start.8 = (bf16[3,64,512]{2,1,0:T(8,128)(2,1)S(1)}, bf16[3,64,512]{2,1,0:T(8,128)(2,1)S(1)}, u32[]{:S(2)}, u32[]{:S(2)}) collective-permute-start(bf16[3,64,512]{2,1,0:T(8,128)(2,1)S(1)} %pad_maximum_fusion.1.refs_6_), channel_id=1, source_target_pairs={{0,4},{1,5},{2,6},{3,7},{4,0},{5,1},{6,2},{7,3},{8,12},{9,13},{10,... | collective-permute-start | bytes 589832 | tf_op jit(solution)/shard_map/ppermute | solution.py:30
  18.4 10.5 %collective-permute-start.9 = (bf16[3,64,512]{2,1,0:T(8,128)(2,1)S(1)}, bf16[3,64,512]{2,1,0:T(8,128)(2,1)S(1)}, u32[]{:S(2)}, u32[]{:S(2)}) collective-permute-start(bf16[3,64,512]{2,1,0:T(8,128)(2,1)S(1)} %pad_maximum_fusion.1.refs_6_), channel_id=1, source_target_pairs={{0,6},{1,7},{2,4},{3,5},{4,2},{5,3},{6,0},{7,1},{8,14},{9,15},{10,... | collective-permute-start | bytes 589832 | tf_op jit(solution)/shard_map/ppermute | solution.py:30
  18.5 23.0 %collective-permute-start.10 = (bf16[3,64,512]{2,1,0:T(8,128)(2,1)S(1)}, bf16[3,64,512]{2,1,0:T(8,128)(2,1)S(1)}, u32[]{:S(2)}, u32[]{:S(2)}) collective-permute-start(bf16[3,64,512]{2,1,0:T(8,128)(2,1)S(1)} %pad_maximum_fusion.1.refs_6_), channel_id=1, source_target_pairs={{0,1},{1,0},{2,3},{3,2},{4,5},{5,4},{6,7},{7,6},{8,9},{9,8},{10,11... | collective-permute-start | bytes 589832 | tf_op jit(solution)/shard_map/ppermute | solution.py:30
  21.1 20.4 %collective-permute-start.11 = (bf16[3,64,512]{2,1,0:T(8,128)(2,1)S(1)}, bf16[3,64,512]{2,1,0:T(8,128)(2,1)S(1)}, u32[]{:S(2)}, u32[]{:S(2)}) collective-permute-start(bf16[3,64,512]{2,1,0:T(8,128)(2,1)S(1)} %collective-permute-done.7.refs_7_), channel_id=1, source_target_pairs={{0,1},{1,0},{2,3},{3,2},{4,5},{5,4},{6,7},{7,6},{8,9},{9,8},{10,11... | collective-permute-start | bytes 589832 | tf_op jit(solution)/shard_map/ppermute | solution.py:30
  25.0 16.4 %collective-permute-start.12 = (bf16[3,64,512]{2,1,0:T(8,128)(2,1)S(1)}, bf16[3,64,512]{2,1,0:T(8,128)(2,1)S(1)}, u32[]{:S(2)}, u32[]{:S(2)}) collective-permute-start(bf16[3,64,512]{2,1,0:T(8,128)(2,1)S(1)} %collective-permute-done.8.refs_8_), channel_id=1, source_target_pairs={{0,1},{1,0},{2,3},{3,2},{4,5},{5,4},{6,7},{7,6},{8,9},{9,8},{10,11... | collective-permute-start | bytes 589832 | tf_op jit(solution)/shard_map/ppermute | solution.py:30
  28.9 12.6 %collective-permute-start.13 = (bf16[3,64,512]{2,1,0:T(8,128)(2,1)S(1)}, bf16[3,64,512]{2,1,0:T(8,128)(2,1)S(1)}, u32[]{:S(2)}, u32[]{:S(2)}) collective-permute-start(bf16[3,64,512]{2,1,0:T(8,128)(2,1)S(1)} %collective-permute-done.9.refs_9_), channel_id=1, source_target_pairs={{0,1},{1,0},{2,3},{3,2},{4,5},{5,4},{6,7},{7,6},{8,9},{9,8},{10,11... | collective-permute-start | bytes 589832 | tf_op jit(solution)/shard_map/ppermute | solution.py:30
  58.2 7.0 %collective-permute-start.18 = (f32[4,1,512]{2,1,0:T(1,128)S(1)}, f32[4,1,512]{2,1,0:T(1,128)S(1)}, u32[]{:S(2)}, u32[]{:S(2)}) collective-permute-start(f32[4,1,512]{2,1,0:T(1,128)S(1)} %get-tuple-element.35), channel_id=1, source_target_pairs={{0,1},{1,0},{2,3},{3,2},{4,5},{5,4},{6,7},{7,6},{8,9},{9,8},{10,11... | collective-permute-start | bytes 24584 | tf_op jit(solution)/shard_map/ppermute | solution.py:30
  65.1 24.1 %collective-permute-start.14 = (bf16[4,128,512]{2,1,0:T(8,128)(2,1)S(1)}, bf16[4,128,512]{2,1,0:T(8,128)(2,1)S(1)}, u32[]{:S(2)}, u32[]{:S(2)}) collective-permute-start(bf16[4,128,512]{2,1,0:T(8,128)(2,1)S(1)} %get-tuple-element.30), channel_id=1, source_target_pairs={{0,1},{1,0},{2,3},{3,2},{4,5},{5,4},{6,7},{7,6},{8,9},{9,8},{10,11... | collective-permute-start | bytes 1572872 | tf_op jit(solution)/shard_map/ppermute | solution.py:30
  65.2 2.7 %collective-permute-start.19 = (f32[4,1,512]{2,1,0:T(1,128)S(1)}, f32[4,1,512]{2,1,0:T(1,128)S(1)}, u32[]{:S(2)}, u32[]{:S(2)}) collective-permute-start(f32[4,1,512]{2,1,0:T(1,128)S(1)} %add.35.refs_8_), channel_id=1, source_target_pairs={{0,2},{1,3},{2,0},{3,1},{4,6},{5,7},{6,4},{7,5},{8,10},{9,11},{10,... | collective-permute-start | bytes 24584 | tf_op jit(solution)/shard_map/ppermute | solution.py:30
  65.3 2.6 %collective-permute-start.20 = (f32[4,1,512]{2,1,0:T(1,128)S(1)}, f32[4,1,512]{2,1,0:T(1,128)S(1)}, u32[]{:S(2)}, u32[]{:S(2)}) collective-permute-start(f32[4,1,512]{2,1,0:T(1,128)S(1)} %add.35.refs_8_), channel_id=1, source_target_pairs={{0,4},{1,5},{2,6},{3,7},{4,0},{5,1},{6,2},{7,3},{8,12},{9,13},{10,... | collective-permute-start | bytes 24584 | tf_op jit(solution)/shard_map/ppermute | solution.py:30
  65.4 3.6 %collective-permute-start.21 = (f32[4,1,512]{2,1,0:T(1,128)S(1)}, f32[4,1,512]{2,1,0:T(1,128)S(1)}, u32[]{:S(2)}, u32[]{:S(2)}) collective-permute-start(f32[4,1,512]{2,1,0:T(1,128)S(1)} %add.35.refs_8_), channel_id=1, source_target_pairs={{0,6},{1,7},{2,4},{3,5},{4,2},{5,3},{6,0},{7,1},{8,14},{9,15},{10,... | collective-permute-start | bytes 24584 | tf_op jit(solution)/shard_map/ppermute | solution.py:30
  89.2 8.3 %copy-start = (bf16[64,512]{1,0:T(8,128)(2,1)S(1)}, bf16[64,512]{1,0:T(8,128)(2,1)}, u32[]{:S(2)}) copy-start(bf16[64,512]{1,0:T(8,128)(2,1)} %refs_0_.1) | copy-start | bytes 196612
  89.4 5.8 %collective-permute-start.17 = (bf16[128,512]{1,0:T(8,128)(2,1)S(1)}, bf16[128,512]{1,0:T(8,128)(2,1)S(1)}, u32[]{:S(2)}, u32[]{:S(2)}) collective-permute-start(bf16[128,512]{1,0:T(8,128)(2,1)S(1)} %get-tuple-element.42), channel_id=1, source_target_pairs={{0,6},{1,7},{2,4},{3,5},{4,2},{5,3},{6,0},{7,1},{8,14},{9,15},{10,... | collective-permute-start | bytes 393224 | tf_op jit(solution)/shard_map/ppermute | solution.py:30
  89.5 7.9 %collective-permute-start.16 = (bf16[128,512]{1,0:T(8,128)(2,1)S(1)}, bf16[128,512]{1,0:T(8,128)(2,1)S(1)}, u32[]{:S(2)}, u32[]{:S(2)}) collective-permute-start(bf16[128,512]{1,0:T(8,128)(2,1)S(1)} %get-tuple-element.43), channel_id=1, source_target_pairs={{0,4},{1,5},{2,6},{3,7},{4,0},{5,1},{6,2},{7,3},{8,12},{9,13},{10,... | collective-permute-start | bytes 393224 | tf_op jit(solution)/shard_map/ppermute | solution.py:30
  89.6 7.9 %collective-permute-start.15 = (bf16[128,512]{1,0:T(8,128)(2,1)S(1)}, bf16[128,512]{1,0:T(8,128)(2,1)S(1)}, u32[]{:S(2)}, u32[]{:S(2)}) collective-permute-start(bf16[128,512]{1,0:T(8,128)(2,1)S(1)} %get-tuple-element.41), channel_id=1, source_target_pairs={{0,2},{1,3},{2,0},{3,1},{4,6},{5,7},{6,4},{7,5},{8,10},{9,11},{10,... | collective-permute-start | bytes 393224 | tf_op jit(solution)/shard_map/ppermute | solution.py:30

commit v3 on v2

--- a/solution.py
+++ b/solution.py
@@ -280,15 +280,19 @@
     )(off, row, cnt, centres)
 
 
-def used_tile(i, steps):
-    return (lax.min(i, steps[0] - 1), 0)
+def tiles_used(off, tile):
+    return lax.shift_right_logical(off[0, off.shape[1] - 1] + tile - 1, tile.bit_length() - 1)
+
+
+def last_used(i, off, tile):
+    return lax.max(lax.min(i, tiles_used(off, tile) - 1), 0)
 
 
 def logits_kernel(chunks, tile, off_ref, e0_ref, e1_ref, what_ref, num_ref, at_ref, *refs):
     l0_refs, l1_refs = refs[:chunks], refs[chunks : 2 * chunks]
-    w_hbm, den_ref, turn_ref, x_ref, d_acc, cos0, cos1, w_buf, w_sem = refs[2 * chunks :]
+    w_hbm, den_ref, turn_ref, x_ref, d_acc, w_buf, w_sem = refs[2 * chunks :]
     group, rows_here, _ = l0_refs[0].shape
-    rows = cos0.shape[1]
+    rows = 2 * (group + 1) * rows_here
     for j in range(chunks):
         for r, (early, late) in enumerate(((e0_ref, l0_refs[j]), (e1_ref, l1_refs[j]))):
             to = j * rows + r * rows_here
@@ -297,52 +301,61 @@
                 to = j * rows + (2 * z + 2 + r) * rows_here
                 x_ref[to : to + rows_here, :] = late[z]
     d_acc[...] = jnp.zeros_like(d_acc)
-    used = off_ref[0, off_ref.shape[1] - 1]
-    steps = lax.shift_right_logical(used + tile - 1, tile.bit_length() - 1)
+    steps = tiles_used(off_ref, tile)
     half = tile // 2
+    cut = rows
 
     def put(t):
         slot = lax.bitwise_and(t, 1)
         here = pl.ds(pl.multiple_of(t * tile, tile), tile)
         return pltpu.make_async_copy(w_buf.at[slot], w_hbm.at[here], w_sem.at[slot])
 
-    def product(first, j):
-        a = what_ref[pl.ds(pl.multiple_of(first, half), half), :]
-        return dot(a, x_ref[pl.ds(pl.multiple_of(j * rows, rows), rows), :], 1, 1)
-
-    def weigh(cos_ref, first, j, slot, to):
-        ids = iota((half, LANES), 0) + first
-        num = num_ref[pl.ds(pl.multiple_of(first, half), half), :]
+    def weigh(first, size, j, slot):
+        here = pl.ds(pl.multiple_of(first, half), size)
+        ids = iota((size, LANES), 0) + first
+        num = num_ref[here, :]
         num_t = num + (math.exp(-logit_scale * margin) - 1.0)
         at = at_ref[j]
-        for k in range(rows // LANES):
-            cols = slice(k * LANES, (k + 1) * LANES)
-            w = jnp.exp2(cos_ref[:, cols]) * jnp.where(ids == at[:, cols], num_t, num)
-            d_acc[j, :, cols] += jnp.sum(w.reshape(half // 8, 8, LANES), axis=0)
-            w_buf[slot, to : to + half, pl.ds(pl.multiple_of(j * rows + k * LANES, LANES), LANES)] = w.astype(bf16)
-
-    cos0[...] = product(0, 0)
-
-    def one(t, carry):
+        for left in range(0, rows, cut):
+            x = x_ref[pl.ds(pl.multiple_of(j * rows + left, cut), cut), :]
+            cos = dot(what_ref[here, :], x, 1, 1)
+            for k in range(0, cut, LANES):
+                cols = slice(left + k, left + k + LANES)
+                w = jnp.exp2(cos[:, k : k + LANES]) * jnp.where(ids == at[:, cols], num_t, num)
+                d_acc[j, :, cols] += jnp.sum(w.reshape(size // 8, 8, LANES), axis=0)
+                w_buf[slot, :size, pl.ds(pl.multiple_of(j * rows + left + k, LANES), LANES)] = w.astype(bf16)
+
+    def one(t, size):
         @pl.when(t >= 2)
         def _():
             put(t - 2).wait()
 
         slot = lax.bitwise_and(t, 1)
+        if size < tile:
+            w_buf[slot, size:, :] = jnp.zeros((tile - size, w_buf.shape[2]), bf16)
+
+        together = math.gcd(chunks, 4)
 
         def chunk(j, carry):
-            cos1[...] = product(t * tile + half, j)
-            weigh(cos0, t * tile, j, slot, 0)
-            last = j == chunks - 1
-            cos0[...] = product(jnp.where(last, t + 1, t) * tile, jnp.where(last, 0, j + 1))
-            weigh(cos1, t * tile + half, j, slot, half)
+            for k in range(together):
+                weigh(t * tile, size, j * together + k, slot)
             return carry
 
-        lax.fori_loop(0, chunks, chunk, 0)
+        lax.fori_loop(0, chunks // together, chunk, 0)
         put(t).start()
+
+    def full(t, carry):
+        one(t, tile)
         return carry
 
-    lax.fori_loop(0, steps, one, 0)
+    used = off_ref[0, off_ref.shape[1] - 1]
+    whole = lax.shift_right_logical(used + half - 1, tile.bit_length() - 1)
+    lax.fori_loop(0, whole, full, 0)
+
+    @pl.when(whole < steps)
+    def _():
+        one(whole, half)
+
     for back in (2, 1):
 
         @pl.when(steps >= back)
@@ -372,8 +385,6 @@
         ),
         scratch_shapes=[
             pltpu.VMEM((chunks, 8, rows), f32),
-            pltpu.VMEM((tile // 2, rows), f32),
-            pltpu.VMEM((tile // 2, rows), f32),
             pltpu.VMEM((2, tile, chunks * rows), bf16),
             pltpu.SemaphoreType.DMA((2,)),
         ],
@@ -388,10 +399,10 @@
 
 
 def own_columns(tile, own, at):
-    return pl.BlockSpec((tile, own), lambda i, steps: (lax.min(i, steps[0] - 1), at))
-
-
-def rows_kernel(chunks, steps_ref, what_ref, at_ref, *refs):
+    return pl.BlockSpec((tile, own), lambda i, off: (last_used(i, off, tile), at))
+
+
+def rows_kernel(chunks, off_ref, what_ref, at_ref, *refs):
     w_refs, (self_ref, away_ref), acc = refs[:chunks], refs[chunks : chunks + 2], refs[chunks + 2]
     i = pl.program_id(0)
     tile = what_ref.shape[0]
@@ -402,11 +413,20 @@
     def _():
         acc[...] = jnp.zeros_like(acc)
 
-    @pl.when(i < steps_ref[0])
-    def _():
-        ids = iota((tile, own), 0) + i * tile
-        left = [w[...] for w in w_refs] + [ones_where(ids == at_ref[j][:, :own]) for j in range(chunks)]
-        acc[...] += dot(jnp.concatenate(left, axis=1), what_ref[...], 0, 0)
+    left = off_ref[0, off_ref.shape[1] - 1] - i * tile
+
+    def add(size):
+        ids = iota((size, own), 0) + i * tile
+        a = [w[:size, :] for w in w_refs] + [ones_where(ids == at_ref[j][:, :own]) for j in range(chunks)]
+        acc[...] += dot(jnp.concatenate(a, axis=1), what_ref[:size, :], 0, 0)
+
+    @pl.when(left > tile // 2)
+    def _():
+        add(tile)
+
+    @pl.when((left > 0) & (left <= tile // 2))
+    def _():
+        add(tile // 2)
 
     @pl.when(i == pl.num_programs(0) - 1)
     def _():
@@ -417,7 +437,7 @@
                 away_ref[j, part * half : (part + 1) * half, :] = acc[at + half : at + own, :].astype(bf16)
 
 
-def row_parts(steps, what, at, w, own, tile):
+def row_parts(off, what, at, w, own, tile):
     chunks, _, rows = at.shape
     width = what.shape[1]
     out = jax.ShapeDtypeStruct((chunks, own, width), bf16)
@@ -428,7 +448,7 @@
             num_scalar_prefetch=1,
             grid=(w.shape[0] // tile,),
             in_specs=[
-                pl.BlockSpec((tile, width), used_tile),
+                pl.BlockSpec((tile, width), lambda i, off: (last_used(i, off, tile), 0)),
                 pl.BlockSpec(at.shape, lambda i, n: (0, 0, 0)),
             ]
             + [own_columns(tile, own, j * rows // own) for j in range(chunks)],
@@ -441,7 +461,7 @@
             flops=2 * chunks * own * w.shape[0] * width, bytes_accessed=2 * what.size, transcendentals=0
         ),
         name="rows",
-    )(steps, what, at, *[w] * chunks)
+    )(off, what, at, *[w] * chunks)
 
 
 def update_kernel(chunks, step, tile, off_ref, at_ref, rep_ref, raw_ref, c_hbm, m_hbm, *refs):
@@ -492,18 +512,13 @@
         if j == 0:
             scale_ref[...] = rate
 
-    def one(done):
-        @pl.when(done + step < used)
-        def _():
-            fetch(done + step)[1].start()
-
-        slot, copy = fetch(done)
-        at = pl.ds(pl.multiple_of(done, step), step)
-        copy.wait()
-        exact = min(step, 256)
+    def work(done, size):
+        slot = lax.bitwise_and(lax.shift_right_logical(done, step.bit_length() - 1), 1)
+        at = pl.ds(pl.multiple_of(done, step), size)
+        exact = min(size, 256)
         ids = iota((exact, rows), 0).astype(f32).astype(bf16)
         lines = []
-        for h in range(0, step, exact):
+        for h in range(0, size, exact):
             parts = []
             for j in range(chunks):
                 place = at_ref[j] - (done + h)
@@ -516,7 +531,23 @@
         inv = 1.0 / jnp.sqrt(jnp.sum(c * c, axis=1, keepdims=True) + eps)
         along = jnp.sum(c * dw, axis=1, keepdims=True) * (inv * inv)
         dw_ref[at, :] = ((dw - c * along) * (inv * (1.0 / sharpness))).astype(bf16)
-        dw_ref[pl.ds(pl.multiple_of(done + step, step), 2 * LANES), :] = jnp.zeros((2 * LANES, width), bf16)
+        dw_ref[pl.ds(pl.multiple_of(done + size, size), 2 * LANES), :] = jnp.zeros((2 * LANES, width), bf16)
+
+    def one(done):
+        @pl.when(done + step < used)
+        def _():
+            fetch(done + step)[1].start()
+
+        fetch(done)[1].wait()
+
+        @pl.when(used - done > step // 2)
+        def _():
+            work(done, step)
+
+        @pl.when(used - done <= step // 2)
+        def _():
+            work(done, step // 2)
+
         return done + step
 
     def group(g, done):
@@ -629,8 +660,7 @@
     den = own_den + swap(turned, "cls", 1)
     dens = [den] + [swap(den, "cls", 2 * q) for q in range(1, chips)]
 
-    steps = lax.max(lax.shift_right_logical(off[0, -1:] + tile - 1, tile.bit_length() - 1), 1)
-    self_part, away_part = row_parts(steps, what, at, w, 2 * rows_here, tile)
+    self_part, away_part = row_parts(off, what, at, w, 2 * rows_here, tile)
     pair = self_part.astype(f32) + swap(away_part, "cls", 1).astype(f32)
     sums = [swap(pair[q].astype(bf16), "cls", 2 * q) for q in range(1, chips)]
 

time: 99.7 us -> 91.9 us (0.922)
  Pallas kernels: 55 us -> 48.4 us
    pallas_call x1, Pallas kernels: 16.7 us -> 10.3 us  [logits(): pl.pallas_call(lambda *refs: logits_kernel(chunks, tile, *refs), in_specs...]
  transfers between devices with their start and end apart: 22 -> 22, of which waited for: 5 -> 5; matrix products, arithmetic and copies ran while one was open for 2% -> 1% of each run, Pallas kernels for 38% -> 41%
where the time goes in v3:
time: 91.9 us; the launch traced here: 90.6 us
  Pallas kernels  48.4 us (53%)
  starting transfers between devices  28.3 us (31%)
  waiting for transfers between devices  10.7 us (12%)
  other arithmetic  2.24 us (2%)
    ppermute x19, starting transfers between devices, swap(): return lax.ppermute(x, axis_name, [(i, i ^ m) for i in range(n)])  24.4 us
    pallas_call x1, Pallas kernels, update(): pl.pallas_call(lambda *refs: update_kernel(chunks, step, tile, *refs), in...  19.6 us
    pallas_call x1, Pallas kernels, logits(): pl.pallas_call(lambda *refs: logits_kernel(chunks, tile, *refs), in_specs...  10.3 us
    pallas_call x1, Pallas kernels, row_parts(): pl.pallas_call(lambda *refs: rows_kernel(chunks, *refs), grid_spec=pltpu....  7.24 us
    ppermute x19, waiting for transfers between devices, swap(): return lax.ppermute(x, axis_name, [(i, i ^ m) for i in range(n)])  6.41 us
    pallas_call x1, Pallas kernels, pack(): pl.pallas_call(pack_kernel, grid=(classes // tile,), in_specs=[pl.BlockSp...  5.89 us
    ppermute x3, waiting for transfers between devices, shift(): return lax.ppermute(x, axis_name, [(i, (i + m) % n) for i in range(n)])  4.27 us
    ppermute x3, starting transfers between devices, shift(): return lax.ppermute(x, axis_name, [(i, (i + m) % n) for i in range(n)])  3.97 us
  transfers between devices with their start and end apart: 22, of which 5 were waited for; matrix products, arithmetic and copies ran while one was open for 1% of the time, Pallas kernels for 41%

profile of v3, /device:TPU:1, one launch (start us, length us, event | category | flops | bytes accessed | tf_op | source)
XLA Modules:
  0.0 90.6 jit_solution(7584502282725276592)
XLA Ops:
  0.6 1.0 %tell.1.refs_3_ = bf16[80,512]{1,0:T(8,128)(2,1)S(1)} custom-call(bf16[64,512]{1,0:T(8,128)(2,1)} %refs_0_.1, s32[16,128]{1,0:T(8,128)} %bitcast.34, s32[16,128]{1,0:T(8,128)} %bitcast.35, s32[4,128]{1,0:T(4,128)} %bitcast.36), custom_call_target="tpu_custom_call" | custom-call | tf_op jit(solution)/shard_map/tell/pallas_call | solution.py:88
  1.6 3.0 %collective-permute-start.2 = (bf16[80,512]{1,0:T(8,128)(2,1)S(1)}, bf16[80,512]{1,0:T(8,128)(2,1)S(1)}, u32[]{:S(2)}, u32[]{:S(2)}) collective-permute-start(bf16[80,512]{1,0:T(8,128)(2,1)S(1)} %tell.1.refs_3_), channel_id=1, source_target_pairs={{0,6},{1,7},{2,4},{3,5},{4,2},{5,3},{6,0},{7,1},{8,14},{9,15},{10,... | collective-permute-start | bytes 245768 | tf_op jit(solution)/shard_map/ppermute | solution.py:30
  4.7 0.2 collective-permute-start.1
  4.9 0.1 collective-permute-start
  5.0 1.4 %collective-permute-start.4 = (bf16[80,512]{1,0:T(8,128)(2,1)S(1)}, bf16[80,512]{1,0:T(8,128)(2,1)S(1)}, u32[]{:S(2)}, u32[]{:S(2)}) collective-permute-start(bf16[80,512]{1,0:T(8,128)(2,1)S(1)} %tell.1.refs_3_), channel_id=1, source_target_pairs={{0,8},{8,16},{16,24},{24,0},{1,9},{9,17},{17,25},{25,1},{2,10},{10... | collective-permute-start | bytes 245768 | tf_op jit(solution)/shard_map/ppermute | solution.py:35
  6.5 2.0 %collective-permute-start.5 = (bf16[80,512]{1,0:T(8,128)(2,1)S(1)}, bf16[80,512]{1,0:T(8,128)(2,1)S(1)}, u32[]{:S(2)}, u32[]{:S(2)}) collective-permute-start(bf16[80,512]{1,0:T(8,128)(2,1)S(1)} %tell.1.refs_3_), channel_id=1, source_target_pairs={{0,24},{8,0},{16,8},{24,16},{1,25},{9,1},{17,9},{25,17},{2,26},{10... | collective-permute-start | bytes 245768 | tf_op jit(solution)/shard_map/ppermute | solution.py:35
  8.5 0.0 collective-permute-done.2
  8.5 0.5 collective-permute-start.6
  9.0 0.0 collective-permute-done.1
  9.0 0.1 collective-permute-done
  9.1 2.3 %collective-permute-start.3 = (bf16[4,80,512]{2,1,0:T(8,128)(2,1)S(1)}, bf16[4,80,512]{2,1,0:T(8,128)(2,1)S(1)}, u32[]{:S(2)}, u32[]{:S(2)}) collective-permute-start(bf16[4,80,512]{2,1,0:T(8,128)(2,1)S(1)} %pad_maximum_fusion.refs_1_), channel_id=1, source_target_pairs={{0,1},{1,0},{2,3},{3,2},{4,5},{5,4},{6,7},{7,6},{8,9},{9,8},{10,11... | collective-permute-start | bytes 983048 | tf_op jit(solution)/shard_map/ppermute | solution.py:30
  11.4 4.3 %collective-permute-done.6.refs_6_ = bf16[80,512]{1,0:T(8,128)(2,1)S(1)} collective-permute-done((bf16[80,512]{1,0:T(8,128)(2,1)S(1)}, bf16[80,512]{1,0:T(8,128)(2,1)S(1)}, u32[]{:S(2)}, u32[]{:S(2)}) %collective-permute-start.6) | collective-permute-done | bytes 81952 | tf_op jit(solution)/shard_map/ppermute | solution.py:35
  15.7 0.0 collective-permute-done.5.refs_5_
  15.7 0.0 collective-permute-done.4.refs_4_
  15.8 1.4 %collective-permute-start.7 = (bf16[3,64,512]{2,1,0:T(8,128)(2,1)S(1)}, bf16[3,64,512]{2,1,0:T(8,128)(2,1)S(1)}, u32[]{:S(2)}, u32[]{:S(2)}) collective-permute-start(bf16[3,64,512]{2,1,0:T(8,128)(2,1)S(1)} %pad_maximum_fusion.1.refs_6_), channel_id=1, source_target_pairs={{0,2},{1,3},{2,0},{3,1},{4,6},{5,7},{6,4},{7,5},{8,10},{9,11},{10,... | collective-permute-start | bytes 589832 | tf_op jit(solution)/shard_map/ppermute | solution.py:30
  17.2 1.2 %collective-permute-start.8 = (bf16[3,64,512]{2,1,0:T(8,128)(2,1)S(1)}, bf16[3,64,512]{2,1,0:T(8,128)(2,1)S(1)}, u32[]{:S(2)}, u32[]{:S(2)}) collective-permute-start(bf16[3,64,512]{2,1,0:T(8,128)(2,1)S(1)} %pad_maximum_fusion.1.refs_6_), channel_id=1, source_target_pairs={{0,4},{1,5},{2,6},{3,7},{4,0},{5,1},{6,2},{7,3},{8,12},{9,13},{10,... | collective-permute-start | bytes 589832 | tf_op jit(solution)/shard_map/ppermute | solution.py:30
  18.4 0.1 collective-permute-start.9
  18.5 2.6 %collective-permute-start.10 = (bf16[3,64,512]{2,1,0:T(8,128)(2,1)S(1)}, bf16[3,64,512]{2,1,0:T(8,128)(2,1)S(1)}, u32[]{:S(2)}, u32[]{:S(2)}) collective-permute-start(bf16[3,64,512]{2,1,0:T(8,128)(2,1)S(1)} %pad_maximum_fusion.1.refs_6_), channel_id=1, source_target_pairs={{0,1},{1,0},{2,3},{3,2},{4,5},{5,4},{6,7},{7,6},{8,9},{9,8},{10,11... | collective-permute-start | bytes 589832 | tf_op jit(solution)/shard_map/ppermute | solution.py:30
  21.1 0.0 collective-permute-done.7.refs_7_
  21.1 4.0 %collective-permute-start.11 = (bf16[3,64,512]{2,1,0:T(8,128)(2,1)S(1)}, bf16[3,64,512]{2,1,0:T(8,128)(2,1)S(1)}, u32[]{:S(2)}, u32[]{:S(2)}) collective-permute-start(bf16[3,64,512]{2,1,0:T(8,128)(2,1)S(1)} %collective-permute-done.7.refs_7_), channel_id=1, source_target_pairs={{0,1},{1,0},{2,3},{3,2},{4,5},{5,4},{6,7},{7,6},{8,9},{9,8},{10,11... | collective-permute-start | bytes 589832 | tf_op jit(solution)/shard_map/ppermute | solution.py:30
  25.0 0.0 collective-permute-done.8.refs_8_
  25.0 3.8 %collective-permute-start.12 = (bf16[3,64,512]{2,1,0:T(8,128)(2,1)S(1)}, bf16[3,64,512]{2,1,0:T(8,128)(2,1)S(1)}, u32[]{:S(2)}, u32[]{:S(2)}) collective-permute-start(bf16[3,64,512]{2,1,0:T(8,128)(2,1)S(1)} %collective-permute-done.8.refs_8_), channel_id=1, source_target_pairs={{0,1},{1,0},{2,3},{3,2},{4,5},{5,4},{6,7},{7,6},{8,9},{9,8},{10,11... | collective-permute-start | bytes 589832 | tf_op jit(solution)/shard_map/ppermute | solution.py:30
  28.9 0.0 collective-permute-done.9.refs_9_
  28.9 0.0 collective-permute-start.13
  28.9 1.0 %fusion.3 = f32[64]{0:T(128)S(1)} fusion(bf16[64,512]{1,0:T(8,128)(2,1)} %refs_0_.1), kind=kLoop, calls=%fused_computation.9 | loop fusion | flops 98240 | bytes 65792 | tf_op jit(solution)/shard_map/reduce_sum | solution.py:674
  29.9 0.0 collective-permute-done.3.refs_2_
  29.9 3.0 %prep.1 = (s32[32,1,128]{2,1,0:T(1,128)S(1)}, s32[4096,128]{1,0:T(8,128)S(1)}, f32[4096,128]{1,0:T(8,128)S(1)}, s32[8,64]{1,0:T(8,128)S(1)}, s32[32,128]{1,0:T(8,128)S(1)}, /*index=5*/s32[128,128]{1,0:T(8,128)S(1)}) custom-call(s32[1]{0:T(128)} %bitcast.refs_0_, bf16[4,80,512]{2,1,0:T(8,128)(2,1)S(1)} %pad_maximum_fusion.refs_1_, ...), custom_call_target="tpu_custom_call" | custom-call | flops 268435456 | bytes 4194304 | tf_op jit(solution)/shard_map/prep/pallas_call | solution.py:185
  32.8 1.5 %places.1.refs_5_.refs_2_.refs_1_ = s32[4,1,512]{2,1,0:T(1,128)S(1)} custom-call(s32[1]{0:T(128)} %bitcast.refs_0_, s32[32,128]{1,0:T(8,128)S(1)} %get-tuple-element.25.refs_1_, s32[128,128]{1,0:T(8,128)S(1)} %get-tuple-element.26.refs_2_, bf16[80,512]{1,0:T(8,128)(2,1)S(1)} %tell.1.refs_3_, bf16[80,512]{1,0:T(8,128)(2,1)S(1)} %collective-permute-done.4.refs_4_, ...), custom_call_target="tpu_custom_call" | custom-call | flops 268435456 | bytes 131072 | tf_op jit(solution)/shard_map/places/pallas_call | solution.py:206
  34.3 5.9 %pack.1 = (bf16[4864,512]{1,0:T(8,128)(2,1)S(1)}, bf16[4864,512]{1,0:T(8,128)(2,1)S(1)}, f32[4864,128]{1,0:T(8,128)S(1)}) custom-call(s32[8,64]{1,0:T(8,128)S(1)} %get-tuple-element.21.off_ref.refs_0_, s32[32,1,128]{2,1,0:T(1,128)S(1)} %get-tuple-element.22.row_ref, f32[4096,128]{1,0:T(8,128)S(1)} %get-tuple-element.23.cnt_ref, bf16[4096,512]{1,0:T(8,128)(2,1)} %refs_4_.1), custom_call_target="tpu_custom_call" | custom-call | flops 1342177280 | bytes 8388608 | tf_op jit(solution)/shard_map/pack/pallas_call | solution.py:262
  40.2 0.0 collective-permute-done.10.refs_10_
  40.2 0.0 collective-permute-done.11.refs_11_
  40.2 0.0 collective-permute-done.12.refs_12_
  40.2 0.0 collective-permute-done.13.refs_13_
  40.2 10.3 %logits.1 = (bf16[4096,2048]{1,0:T(8,128)(2,1)}, f32[4,1,512]{2,1,0:T(1,128)S(1)}, f32[4,1,512]{2,1,0:T(1,128)S(1)}, bf16[2048,512]{1,0:T(8,128)(2,1)S(1)}) custom-call(s32[8,64]{1,0:T(8,128)S(1)} %get-tuple-element.21.off_ref.refs_0_, bf16[4,80,512]{2,1,0:T(8,128)(2,1)S(1)} %pad_maximum_fusion.refs_1_, ...), custom_call_target="tpu_custom_call" | custom-call | flops 4294967296 | bytes 10485760 | tf_op jit(solution)/shard_map/logits/pallas_call | solution.py:376
  50.5 0.1 collective-permute-start.18
  50.6 7.2 %rows.1 = (bf16[4,128,512]{2,1,0:T(8,128)(2,1)S(1)}, bf16[4,128,512]{2,1,0:T(8,128)(2,1)S(1)}) custom-call(s32[8,64]{1,0:T(8,128)S(1)} %get-tuple-element.21.off_ref.refs_0_, bf16[4864,512]{1,0:T(8,128)(2,1)S(1)} %get-tuple-element.24.refs_3_.refs_1_, s32[4,1,512]{2,1,0:T(1,128)S(1)} %places.1.refs_5_.refs_2_.refs_1_, ...), custom_call_target="tpu_custom_call" | custom-call | flops 2147483648 | bytes 4980736 | tf_op jit(solution)/shard_map/rows/pallas_call | solution.py:445
  57.8 0.1 collective-permute-start.14
  57.9 0.0 collective-permute-done.18
  57.9 0.1 collective-permute-start.19
  58.0 0.1 collective-permute-start.20
  58.1 2.6 %collective-permute-start.21 = (f32[4,1,512]{2,1,0:T(1,128)S(1)}, f32[4,1,512]{2,1,0:T(1,128)S(1)}, u32[]{:S(2)}, u32[]{:S(2)}) collective-permute-start(f32[4,1,512]{2,1,0:T(1,128)S(1)} %add.30.refs_8_), channel_id=1, source_target_pairs={{0,6},{1,7},{2,4},{3,5},{4,2},{5,3},{6,0},{7,1},{8,14},{9,15},{10,... | collective-permute-start | bytes 24584 | tf_op jit(solution)/shard_map/ppermute | solution.py:30
  60.7 0.0 collective-permute-done.19.refs_9_
  60.7 0.0 collective-permute-done.20.refs_10_
  60.7 1.0 %collective-permute-done.21.refs_11_ = f32[4,1,512]{2,1,0:T(1,128)S(1)} collective-permute-done((f32[4,1,512]{2,1,0:T(1,128)S(1)}, f32[4,1,512]{2,1,0:T(1,128)S(1)}, u32[]{:S(2)}, u32[]{:S(2)}) %collective-permute-start.21) | collective-permute-done | bytes 8224 | tf_op jit(solution)/shard_map/ppermute | solution.py:30
  61.7 19.6 %update.1 = (f32[4096,512]{1,0:T(8,128)}, bf16[4096,512]{1,0:T(8,128)(2,1)}, f32[1,512]{1,0:T(1,128)S(1)}) custom-call(s32[8,64]{1,0:T(8,128)S(1)} %get-tuple-element.21.off_ref.refs_0_, s32[4,1,512]{2,1,0:T(1,128)S(1)} %places.1.refs_5_.refs_2_.refs_1_, s32[4096,128]{1,0:T(8,128)S(1)} %get-tuple-element.31.refs_2_, ...), custom_call_target="tpu_custom_call" | custom-call | flops 4294967296 | bytes 33554432 | tf_op jit(solution)/shard_map/update/pallas_call | solution.py:596
  81.3 0.0 copy-start
  81.3 0.0 collective-permute-done.14
  81.3 0.2 fusion.5
  81.5 0.1 collective-permute-start.17
  81.6 0.1 collective-permute-start.16
  81.7 2.6 %collective-permute-start.15 = (bf16[128,512]{1,0:T(8,128)(2,1)S(1)}, bf16[128,512]{1,0:T(8,128)(2,1)S(1)}, u32[]{:S(2)}, u32[]{:S(2)}) collective-permute-start(bf16[128,512]{1,0:T(8,128)(2,1)S(1)} %get-tuple-element.41), channel_id=1, source_target_pairs={{0,2},{1,3},{2,0},{3,1},{4,6},{5,7},{6,4},{7,5},{8,10},{9,11},{10,... | collective-permute-start | bytes 393224 | tf_op jit(solution)/shard_map/ppermute | solution.py:30
  84.2 3.1 %collective-permute-done.17 = bf16[128,512]{1,0:T(8,128)(2,1)S(1)} collective-permute-done((bf16[128,512]{1,0:T(8,128)(2,1)S(1)}, bf16[128,512]{1,0:T(8,128)(2,1)S(1)}, u32[]{:S(2)}, u32[]{:S(2)}) %collective-permute-start.17) | collective-permute-done | bytes 131104 | tf_op jit(solution)/shard_map/ppermute | solution.py:30
  87.3 2.2 %collective-permute-done.16 = bf16[128,512]{1,0:T(8,128)(2,1)S(1)} collective-permute-done((bf16[128,512]{1,0:T(8,128)(2,1)S(1)}, bf16[128,512]{1,0:T(8,128)(2,1)S(1)}, u32[]{:S(2)}, u32[]{:S(2)}) %collective-permute-start.16) | collective-permute-done | bytes 131104 | tf_op jit(solution)/shard_map/ppermute | solution.py:30
  89.5 0.0 collective-permute-done.15
  89.6 0.1 fusion.2
  89.6 0.0 copy-done
  89.6 0.2 multiply_reduce_fusion
  89.8 0.8 subtract_divide_fusion
  (9 shorter events, 0.1 us)
Async XLA Ops:
  1.6 6.9 %collective-permute-start.2 = (bf16[80,512]{1,0:T(8,128)(2,1)S(1)}, bf16[80,512]{1,0:T(8,128)(2,1)S(1)}, u32[]{:S(2)}, u32[]{:S(2)}) collective-permute-start(bf16[80,512]{1,0:T(8,128)(2,1)S(1)} %tell.1.refs_3_), channel_id=1, source_target_pairs={{0,6},{1,7},{2,4},{3,5},{4,2},{5,3},{6,0},{7,1},{8,14},{9,15},{10,... | collective-permute-start | bytes 245768 | tf_op jit(solution)/shard_map/ppermute | solution.py:30
  4.7 4.3 %collective-permute-start.1 = (bf16[80,512]{1,0:T(8,128)(2,1)S(1)}, bf16[80,512]{1,0:T(8,128)(2,1)S(1)}, u32[]{:S(2)}, u32[]{:S(2)}) collective-permute-start(bf16[80,512]{1,0:T(8,128)(2,1)S(1)} %tell.1.refs_3_), channel_id=1, source_target_pairs={{0,4},{1,5},{2,6},{3,7},{4,0},{5,1},{6,2},{7,3},{8,12},{9,13},{10,... | collective-permute-start | bytes 245768 | tf_op jit(solution)/shard_map/ppermute | solution.py:30
  4.9 4.2 %collective-permute-start = (bf16[80,512]{1,0:T(8,128)(2,1)S(1)}, bf16[80,512]{1,0:T(8,128)(2,1)S(1)}, u32[]{:S(2)}, u32[]{:S(2)}) collective-permute-start(bf16[80,512]{1,0:T(8,128)(2,1)S(1)} %tell.1.refs_3_), channel_id=1, source_target_pairs={{0,2},{1,3},{2,0},{3,1},{4,6},{5,7},{6,4},{7,5},{8,10},{9,11},{10,... | collective-permute-start | bytes 245768 | tf_op jit(solution)/shard_map/ppermute | solution.py:30
  5.0 10.7 %collective-permute-start.4 = (bf16[80,512]{1,0:T(8,128)(2,1)S(1)}, bf16[80,512]{1,0:T(8,128)(2,1)S(1)}, u32[]{:S(2)}, u32[]{:S(2)}) collective-permute-start(bf16[80,512]{1,0:T(8,128)(2,1)S(1)} %tell.1.refs_3_), channel_id=1, source_target_pairs={{0,8},{8,16},{16,24},{24,0},{1,9},{9,17},{17,25},{25,1},{2,10},{10... | collective-permute-start | bytes 245768 | tf_op jit(solution)/shard_map/ppermute | solution.py:35
  6.5 9.2 %collective-permute-start.5 = (bf16[80,512]{1,0:T(8,128)(2,1)S(1)}, bf16[80,512]{1,0:T(8,128)(2,1)S(1)}, u32[]{:S(2)}, u32[]{:S(2)}) collective-permute-start(bf16[80,512]{1,0:T(8,128)(2,1)S(1)} %tell.1.refs_3_), channel_id=1, source_target_pairs={{0,24},{8,0},{16,8},{24,16},{1,25},{9,1},{17,9},{25,17},{2,26},{10... | collective-permute-start | bytes 245768 | tf_op jit(solution)/shard_map/ppermute | solution.py:35
  8.5 7.2 %collective-permute-start.6 = (bf16[80,512]{1,0:T(8,128)(2,1)S(1)}, bf16[80,512]{1,0:T(8,128)(2,1)S(1)}, u32[]{:S(2)}, u32[]{:S(2)}) collective-permute-start(bf16[80,512]{1,0:T(8,128)(2,1)S(1)} %tell.1.refs_3_), channel_id=1, source_target_pairs={{0,16},{8,24},{16,0},{24,8},{1,17},{9,25},{17,1},{25,9},{2,18},{10... | collective-permute-start | bytes 245768 | tf_op jit(solution)/shard_map/ppermute | solution.py:35
  9.1 20.7 %collective-permute-start.3 = (bf16[4,80,512]{2,1,0:T(8,128)(2,1)S(1)}, bf16[4,80,512]{2,1,0:T(8,128)(2,1)S(1)}, u32[]{:S(2)}, u32[]{:S(2)}) collective-permute-start(bf16[4,80,512]{2,1,0:T(8,128)(2,1)S(1)} %pad_maximum_fusion.refs_1_), channel_id=1, source_target_pairs={{0,1},{1,0},{2,3},{3,2},{4,5},{5,4},{6,7},{7,6},{8,9},{9,8},{10,11... | collective-permute-start | bytes 983048 | tf_op jit(solution)/shard_map/ppermute | solution.py:30
  15.8 5.3 %collective-permute-start.7 = (bf16[3,64,512]{2,1,0:T(8,128)(2,1)S(1)}, bf16[3,64,512]{2,1,0:T(8,128)(2,1)S(1)}, u32[]{:S(2)}, u32[]{:S(2)}) collective-permute-start(bf16[3,64,512]{2,1,0:T(8,128)(2,1)S(1)} %pad_maximum_fusion.1.refs_6_), channel_id=1, source_target_pairs={{0,2},{1,3},{2,0},{3,1},{4,6},{5,7},{6,4},{7,5},{8,10},{9,11},{10,... | collective-permute-start | bytes 589832 | tf_op jit(solution)/shard_map/ppermute | solution.py:30
  17.2 7.9 %collective-permute-start.8 = (bf16[3,64,512]{2,1,0:T(8,128)(2,1)S(1)}, bf16[3,64,512]{2,1,0:T(8,128)(2,1)S(1)}, u32[]{:S(2)}, u32[]{:S(2)}) collective-permute-start(bf16[3,64,512]{2,1,0:T(8,128)(2,1)S(1)} %pad_maximum_fusion.1.refs_6_), channel_id=1, source_target_pairs={{0,4},{1,5},{2,6},{3,7},{4,0},{5,1},{6,2},{7,3},{8,12},{9,13},{10,... | collective-permute-start | bytes 589832 | tf_op jit(solution)/shard_map/ppermute | solution.py:30
  18.4 10.5 %collective-permute-start.9 = (bf16[3,64,512]{2,1,0:T(8,128)(2,1)S(1)}, bf16[3,64,512]{2,1,0:T(8,128)(2,1)S(1)}, u32[]{:S(2)}, u32[]{:S(2)}) collective-permute-start(bf16[3,64,512]{2,1,0:T(8,128)(2,1)S(1)} %pad_maximum_fusion.1.refs_6_), channel_id=1, source_target_pairs={{0,6},{1,7},{2,4},{3,5},{4,2},{5,3},{6,0},{7,1},{8,14},{9,15},{10,... | collective-permute-start | bytes 589832 | tf_op jit(solution)/shard_map/ppermute | solution.py:30
  18.5 21.7 %collective-permute-start.10 = (bf16[3,64,512]{2,1,0:T(8,128)(2,1)S(1)}, bf16[3,64,512]{2,1,0:T(8,128)(2,1)S(1)}, u32[]{:S(2)}, u32[]{:S(2)}) collective-permute-start(bf16[3,64,512]{2,1,0:T(8,128)(2,1)S(1)} %pad_maximum_fusion.1.refs_6_), channel_id=1, source_target_pairs={{0,1},{1,0},{2,3},{3,2},{4,5},{5,4},{6,7},{7,6},{8,9},{9,8},{10,11... | collective-permute-start | bytes 589832 | tf_op jit(solution)/shard_map/ppermute | solution.py:30
  21.1 19.1 %collective-permute-start.11 = (bf16[3,64,512]{2,1,0:T(8,128)(2,1)S(1)}, bf16[3,64,512]{2,1,0:T(8,128)(2,1)S(1)}, u32[]{:S(2)}, u32[]{:S(2)}) collective-permute-start(bf16[3,64,512]{2,1,0:T(8,128)(2,1)S(1)} %collective-permute-done.7.refs_7_), channel_id=1, source_target_pairs={{0,1},{1,0},{2,3},{3,2},{4,5},{5,4},{6,7},{7,6},{8,9},{9,8},{10,11... | collective-permute-start | bytes 589832 | tf_op jit(solution)/shard_map/ppermute | solution.py:30
  25.0 15.2 %collective-permute-start.12 = (bf16[3,64,512]{2,1,0:T(8,128)(2,1)S(1)}, bf16[3,64,512]{2,1,0:T(8,128)(2,1)S(1)}, u32[]{:S(2)}, u32[]{:S(2)}) collective-permute-start(bf16[3,64,512]{2,1,0:T(8,128)(2,1)S(1)} %collective-permute-done.8.refs_8_), channel_id=1, source_target_pairs={{0,1},{1,0},{2,3},{3,2},{4,5},{5,4},{6,7},{7,6},{8,9},{9,8},{10,11... | collective-permute-start | bytes 589832 | tf_op jit(solution)/shard_map/ppermute | solution.py:30
  28.9 11.3 %collective-permute-start.13 = (bf16[3,64,512]{2,1,0:T(8,128)(2,1)S(1)}, bf16[3,64,512]{2,1,0:T(8,128)(2,1)S(1)}, u32[]{:S(2)}, u32[]{:S(2)}) collective-permute-start(bf16[3,64,512]{2,1,0:T(8,128)(2,1)S(1)} %collective-permute-done.9.refs_9_), channel_id=1, source_target_pairs={{0,1},{1,0},{2,3},{3,2},{4,5},{5,4},{6,7},{7,6},{8,9},{9,8},{10,11... | collective-permute-start | bytes 589832 | tf_op jit(solution)/shard_map/ppermute | solution.py:30
  50.5 7.4 %collective-permute-start.18 = (f32[4,1,512]{2,1,0:T(1,128)S(1)}, f32[4,1,512]{2,1,0:T(1,128)S(1)}, u32[]{:S(2)}, u32[]{:S(2)}) collective-permute-start(f32[4,1,512]{2,1,0:T(1,128)S(1)} %get-tuple-element.35), channel_id=1, source_target_pairs={{0,1},{1,0},{2,3},{3,2},{4,5},{5,4},{6,7},{7,6},{8,9},{9,8},{10,11... | collective-permute-start | bytes 24584 | tf_op jit(solution)/shard_map/ppermute | solution.py:30
  57.8 23.5 %collective-permute-start.14 = (bf16[4,128,512]{2,1,0:T(8,128)(2,1)S(1)}, bf16[4,128,512]{2,1,0:T(8,128)(2,1)S(1)}, u32[]{:S(2)}, u32[]{:S(2)}) collective-permute-start(bf16[4,128,512]{2,1,0:T(8,128)(2,1)S(1)} %get-tuple-element.30), channel_id=1, source_target_pairs={{0,1},{1,0},{2,3},{3,2},{4,5},{5,4},{6,7},{7,6},{8,9},{9,8},{10,11... | collective-permute-start | bytes 1572872 | tf_op jit(solution)/shard_map/ppermute | solution.py:30
  57.9 2.7 %collective-permute-start.19 = (f32[4,1,512]{2,1,0:T(1,128)S(1)}, f32[4,1,512]{2,1,0:T(1,128)S(1)}, u32[]{:S(2)}, u32[]{:S(2)}) collective-permute-start(f32[4,1,512]{2,1,0:T(1,128)S(1)} %add.30.refs_8_), channel_id=1, source_target_pairs={{0,2},{1,3},{2,0},{3,1},{4,6},{5,7},{6,4},{7,5},{8,10},{9,11},{10,... | collective-permute-start | bytes 24584 | tf_op jit(solution)/shard_map/ppermute | solution.py:30
  58.0 2.6 %collective-permute-start.20 = (f32[4,1,512]{2,1,0:T(1,128)S(1)}, f32[4,1,512]{2,1,0:T(1,128)S(1)}, u32[]{:S(2)}, u32[]{:S(2)}) collective-permute-start(f32[4,1,512]{2,1,0:T(1,128)S(1)} %add.30.refs_8_), channel_id=1, source_target_pairs={{0,4},{1,5},{2,6},{3,7},{4,0},{5,1},{6,2},{7,3},{8,12},{9,13},{10,... | collective-permute-start | bytes 24584 | tf_op jit(solution)/shard_map/ppermute | solution.py:30
  58.1 3.6 %collective-permute-start.21 = (f32[4,1,512]{2,1,0:T(1,128)S(1)}, f32[4,1,512]{2,1,0:T(1,128)S(1)}, u32[]{:S(2)}, u32[]{:S(2)}) collective-permute-start(f32[4,1,512]{2,1,0:T(1,128)S(1)} %add.30.refs_8_), channel_id=1, source_target_pairs={{0,6},{1,7},{2,4},{3,5},{4,2},{5,3},{6,0},{7,1},{8,14},{9,15},{10,... | collective-permute-start | bytes 24584 | tf_op jit(solution)/shard_map/ppermute | solution.py:30
  81.3 8.3 %copy-start = (bf16[64,512]{1,0:T(8,128)(2,1)S(1)}, bf16[64,512]{1,0:T(8,128)(2,1)}, u32[]{:S(2)}) copy-start(bf16[64,512]{1,0:T(8,128)(2,1)} %refs_0_.1) | copy-start | bytes 196612
  81.5 5.8 %collective-permute-start.17 = (bf16[128,512]{1,0:T(8,128)(2,1)S(1)}, bf16[128,512]{1,0:T(8,128)(2,1)S(1)}, u32[]{:S(2)}, u32[]{:S(2)}) collective-permute-start(bf16[128,512]{1,0:T(8,128)(2,1)S(1)} %get-tuple-element.42), channel_id=1, source_target_pairs={{0,6},{1,7},{2,4},{3,5},{4,2},{5,3},{6,0},{7,1},{8,14},{9,15},{10,... | collective-permute-start | bytes 393224 | tf_op jit(solution)/shard_map/ppermute | solution.py:30
  81.6 7.9 %collective-permute-start.16 = (bf16[128,512]{1,0:T(8,128)(2,1)S(1)}, bf16[128,512]{1,0:T(8,128)(2,1)S(1)}, u32[]{:S(2)}, u32[]{:S(2)}) collective-permute-start(bf16[128,512]{1,0:T(8,128)(2,1)S(1)} %get-tuple-element.43), channel_id=1, source_target_pairs={{0,4},{1,5},{2,6},{3,7},{4,0},{5,1},{6,2},{7,3},{8,12},{9,13},{10,... | collective-permute-start | bytes 393224 | tf_op jit(solution)/shard_map/ppermute | solution.py:30
  81.7 7.9 %collective-permute-start.15 = (bf16[128,512]{1,0:T(8,128)(2,1)S(1)}, bf16[128,512]{1,0:T(8,128)(2,1)S(1)}, u32[]{:S(2)}, u32[]{:S(2)}) collective-permute-start(bf16[128,512]{1,0:T(8,128)(2,1)S(1)} %get-tuple-element.41), channel_id=1, source_target_pairs={{0,2},{1,3},{2,0},{3,1},{4,6},{5,7},{6,4},{7,5},{8,10},{9,11},{10,... | collective-permute-start | bytes 393224 | tf_op jit(solution)/shard_map/ppermute | solution.py:30

commit v4 on v3

--- a/solution.py
+++ b/solution.py
@@ -15,6 +15,7 @@
 weight_decay = 0.0005
 
 LANES = 128
+OUT = 4
 sharpness = logit_scale * math.log2(math.e)
 HBM = pl.BlockSpec(memory_space=pltpu.HBM)
 bf16 = jnp.bfloat16
@@ -485,7 +486,7 @@
         )
 
     def outs(g):
-        at, slot = span(g), lax.bitwise_and(g, 1)
+        at, slot = span(g), lax.bitwise_and(g, OUT - 1)
         return (
             pltpu.make_async_copy(c_new.at[slot], co_hbm.at[at], co_sem.at[slot]),
             pltpu.make_async_copy(m_new.at[slot], mo_hbm.at[at], mo_sem.at[slot]),
@@ -496,9 +497,11 @@
         at = pl.ds(pl.multiple_of(start, step), step)
         return slot, pltpu.make_async_copy(w_hbm.at[at], buf.at[slot], w_sem.at[slot])
 
-    @pl.when(used > 0)
-    def _():
-        fetch(0)[1].start()
+    for first in (0, step):
+
+        @pl.when(used > first)
+        def _():
+            fetch(first)[1].start()
 
     for g in range(groups):
         for copy in ins(g):
@@ -534,10 +537,6 @@
         dw_ref[pl.ds(pl.multiple_of(done + size, size), 2 * LANES), :] = jnp.zeros((2 * LANES, width), bf16)
 
     def one(done):
-        @pl.when(done + step < used)
-        def _():
-            fetch(done + step)[1].start()
-
         fetch(done)[1].wait()
 
         @pl.when(used - done > step // 2)
@@ -547,6 +546,10 @@
         @pl.when(used - done <= step // 2)
         def _():
             work(done, step // 2)
+
+        @pl.when(done + 2 * step < used)
+        def _():
+            fetch(done + 2 * step)[1].start()
 
         return done + step
 
@@ -554,11 +557,11 @@
         done = lax.while_loop(lambda d: d < off_ref[0, blocks + (g + 1) * per - 1], one, done)
         for copy in ins(g):
             copy.wait()
-        slot = lax.bitwise_and(g, 1)
-
-        @pl.when(g >= 2)
+        slot = lax.bitwise_and(g, OUT - 1)
+
+        @pl.when(g >= OUT)
         def _():
-            for copy in outs(g - 2):
+            for copy in outs(g - OUT):
                 copy.wait()
 
         lane = iota((LANES, LANES), 1)
@@ -582,7 +585,7 @@
         dw_ref[: 2 * LANES, :] = jnp.zeros((2 * LANES, width), bf16)
 
     lax.fori_loop(0, groups, group, 0)
-    for g in range(max(0, groups - 2), groups):
+    for g in range(max(0, groups - OUT), groups):
         for copy in outs(g):
             copy.wait()
 
@@ -607,14 +610,14 @@
             pltpu.VMEM((classes + 2 * LANES + step, width), bf16),
             pltpu.VMEM((classes, width), bf16),
             pltpu.VMEM((classes, width), f32),
-            pltpu.VMEM((2, tile, width), bf16),
-            pltpu.VMEM((2, tile, width), f32),
+            pltpu.VMEM((OUT, tile, width), bf16),
+            pltpu.VMEM((OUT, tile, width), f32),
             pltpu.VMEM((2, step, chunks * rows), bf16),
             pltpu.SemaphoreType.DMA((2,)),
             sems,
             sems,
-            pltpu.SemaphoreType.DMA((2,)),
-            pltpu.SemaphoreType.DMA((2,)),
+            pltpu.SemaphoreType.DMA((OUT,)),
+            pltpu.SemaphoreType.DMA((OUT,)),
         ],
         compiler_params=params(22 + 3 * chunks),
         cost_estimate=pl.CostEstimate(
@@ -639,11 +642,15 @@
     dims = (home_rows, rows_here, here, classes, sampled)
     told = tell(embeddings, sample_home, sample_row, labels, dims)
 
-    from_z = [shift(told, "dp", m) for m in (1, group - 1)] + [shift(told, "dp", m) for m in range(2, group - 1)]
+    from_z = []
+    for m in [1, group - 1] + list(range(2, group - 1)):
+        from_z.append(shift(told, "dp", m))
     early = jnp.stack([told] + [swap(told, "cls", 2 * q) for q in range(1, chips)])
     early_away = swap(early, "cls", 1)
     late0 = jnp.stack([z[:rows_here] for z in from_z])
-    late = [late0] + [swap(late0, "cls", 2 * q) for q in range(1, chips)]
+    late = [late0]
+    for q in range(1, chips):
+        late.append(swap(late0, "cls", 2 * q))
     late_away = []
     for x in late:
         late_away.append(swap(x, "cls", 1))

time: 91.9 us -> 91 us (level)
  transfers between devices with their start and end apart: 22 -> 22, of which waited for: 5 -> 5; matrix products, arithmetic and copies ran while one was open for 1% -> 1% of each run, Pallas kernels for 41% -> 40%
where the time goes in v4:
time: 91 us; the launch traced here: 89.9 us
  Pallas kernels  47.5 us (52%)
  starting transfers between devices  28.3 us (31%)
  waiting for transfers between devices  10.9 us (12%)
  other arithmetic  2.24 us (2%)
    ppermute x19, starting transfers between devices, swap(): return lax.ppermute(x, axis_name, [(i, i ^ m) for i in range(n)])  24.4 us
    pallas_call x1, Pallas kernels, update(): pl.pallas_call(lambda *refs: update_kernel(chunks, step, tile, *refs), in...  18.7 us
    pallas_call x1, Pallas kernels, logits(): pl.pallas_call(lambda *refs: logits_kernel(chunks, tile, *refs), in_specs...  10.3 us
    pallas_call x1, Pallas kernels, row_parts(): pl.pallas_call(lambda *refs: rows_kernel(chunks, *refs), grid_spec=pltpu....  7.24 us
    ppermute x19, waiting for transfers between devices, swap(): return lax.ppermute(x, axis_name, [(i, i ^ m) for i in range(n)])  6.59 us
    pallas_call x1, Pallas kernels, pack(): pl.pallas_call(pack_kernel, grid=(classes // tile,), in_specs=[pl.BlockSp...  5.89 us
    ppermute x3, waiting for transfers between devices, shift(): return lax.ppermute(x, axis_name, [(i, (i + m) % n) for i in range(n)])  4.27 us
    ppermute x3, starting transfers between devices, shift(): return lax.ppermute(x, axis_name, [(i, (i + m) % n) for i in range(n)])  3.97 us
  transfers between devices with their start and end apart: 22, of which 5 were waited for; matrix products, arithmetic and copies ran while one was open for 1% of the time, Pallas kernels for 40%

profile of v4, /device:TPU:1, one launch (start us, length us, event | category | flops | bytes accessed | tf_op | source)
XLA Modules:
  0.0 89.9 jit_solution(12439221273130904192)
XLA Ops:
  0.6 1.0 %tell.1.refs_3_ = bf16[80,512]{1,0:T(8,128)(2,1)S(1)} custom-call(bf16[64,512]{1,0:T(8,128)(2,1)} %refs_0_.1, s32[16,128]{1,0:T(8,128)} %bitcast.34, s32[16,128]{1,0:T(8,128)} %bitcast.35, s32[4,128]{1,0:T(4,128)} %bitcast.36), custom_call_target="tpu_custom_call" | custom-call | tf_op jit(solution)/shard_map/tell/pallas_call | solution.py:89
  1.6 3.0 %collective-permute-start.2 = (bf16[80,512]{1,0:T(8,128)(2,1)S(1)}, bf16[80,512]{1,0:T(8,128)(2,1)S(1)}, u32[]{:S(2)}, u32[]{:S(2)}) collective-permute-start(bf16[80,512]{1,0:T(8,128)(2,1)S(1)} %tell.1.refs_3_), channel_id=1, source_target_pairs={{0,6},{1,7},{2,4},{3,5},{4,2},{5,3},{6,0},{7,1},{8,14},{9,15},{10,... | collective-permute-start | bytes 245768 | tf_op jit(solution)/shard_map/ppermute | solution.py:31
  4.7 0.2 collective-permute-start.1
  4.9 0.1 collective-permute-start
  5.0 1.4 %collective-permute-start.4 = (bf16[80,512]{1,0:T(8,128)(2,1)S(1)}, bf16[80,512]{1,0:T(8,128)(2,1)S(1)}, u32[]{:S(2)}, u32[]{:S(2)}) collective-permute-start(bf16[80,512]{1,0:T(8,128)(2,1)S(1)} %tell.1.refs_3_), channel_id=1, source_target_pairs={{0,8},{8,16},{16,24},{24,0},{1,9},{9,17},{17,25},{25,1},{2,10},{10... | collective-permute-start | bytes 245768 | tf_op jit(solution)/shard_map/ppermute | solution.py:36
  6.5 2.0 %collective-permute-start.5 = (bf16[80,512]{1,0:T(8,128)(2,1)S(1)}, bf16[80,512]{1,0:T(8,128)(2,1)S(1)}, u32[]{:S(2)}, u32[]{:S(2)}) collective-permute-start(bf16[80,512]{1,0:T(8,128)(2,1)S(1)} %tell.1.refs_3_), channel_id=1, source_target_pairs={{0,24},{8,0},{16,8},{24,16},{1,25},{9,1},{17,9},{25,17},{2,26},{10... | collective-permute-start | bytes 245768 | tf_op jit(solution)/shard_map/ppermute | solution.py:36
  8.5 0.0 collective-permute-done.2
  8.5 0.5 collective-permute-start.6
  9.0 0.0 collective-permute-done.1
  9.0 0.1 collective-permute-done
  9.1 2.3 %collective-permute-start.3 = (bf16[4,80,512]{2,1,0:T(8,128)(2,1)S(1)}, bf16[4,80,512]{2,1,0:T(8,128)(2,1)S(1)}, u32[]{:S(2)}, u32[]{:S(2)}) collective-permute-start(bf16[4,80,512]{2,1,0:T(8,128)(2,1)S(1)} %pad_maximum_fusion.refs_1_), channel_id=1, source_target_pairs={{0,1},{1,0},{2,3},{3,2},{4,5},{5,4},{6,7},{7,6},{8,9},{9,8},{10,11... | collective-permute-start | bytes 983048 | tf_op jit(solution)/shard_map/ppermute | solution.py:31
  11.4 4.3 %collective-permute-done.6.refs_6_ = bf16[80,512]{1,0:T(8,128)(2,1)S(1)} collective-permute-done((bf16[80,512]{1,0:T(8,128)(2,1)S(1)}, bf16[80,512]{1,0:T(8,128)(2,1)S(1)}, u32[]{:S(2)}, u32[]{:S(2)}) %collective-permute-start.6) | collective-permute-done | bytes 81952 | tf_op jit(solution)/shard_map/ppermute | solution.py:36
  15.7 0.0 collective-permute-done.5.refs_5_
  15.7 0.0 collective-permute-done.4.refs_4_
  15.8 1.4 %collective-permute-start.7 = (bf16[3,64,512]{2,1,0:T(8,128)(2,1)S(1)}, bf16[3,64,512]{2,1,0:T(8,128)(2,1)S(1)}, u32[]{:S(2)}, u32[]{:S(2)}) collective-permute-start(bf16[3,64,512]{2,1,0:T(8,128)(2,1)S(1)} %pad_maximum_fusion.1.refs_6_), channel_id=1, source_target_pairs={{0,2},{1,3},{2,0},{3,1},{4,6},{5,7},{6,4},{7,5},{8,10},{9,11},{10,... | collective-permute-start | bytes 589832 | tf_op jit(solution)/shard_map/ppermute | solution.py:31
  17.2 1.2 %collective-permute-start.8 = (bf16[3,64,512]{2,1,0:T(8,128)(2,1)S(1)}, bf16[3,64,512]{2,1,0:T(8,128)(2,1)S(1)}, u32[]{:S(2)}, u32[]{:S(2)}) collective-permute-start(bf16[3,64,512]{2,1,0:T(8,128)(2,1)S(1)} %pad_maximum_fusion.1.refs_6_), channel_id=1, source_target_pairs={{0,4},{1,5},{2,6},{3,7},{4,0},{5,1},{6,2},{7,3},{8,12},{9,13},{10,... | collective-permute-start | bytes 589832 | tf_op jit(solution)/shard_map/ppermute | solution.py:31
  18.4 0.1 collective-permute-start.9
  18.5 2.6 %collective-permute-start.10 = (bf16[3,64,512]{2,1,0:T(8,128)(2,1)S(1)}, bf16[3,64,512]{2,1,0:T(8,128)(2,1)S(1)}, u32[]{:S(2)}, u32[]{:S(2)}) collective-permute-start(bf16[3,64,512]{2,1,0:T(8,128)(2,1)S(1)} %pad_maximum_fusion.1.refs_6_), channel_id=1, source_target_pairs={{0,1},{1,0},{2,3},{3,2},{4,5},{5,4},{6,7},{7,6},{8,9},{9,8},{10,11... | collective-permute-start | bytes 589832 | tf_op jit(solution)/shard_map/ppermute | solution.py:31
  21.1 0.0 collective-permute-done.7.refs_7_
  21.1 4.0 %collective-permute-start.11 = (bf16[3,64,512]{2,1,0:T(8,128)(2,1)S(1)}, bf16[3,64,512]{2,1,0:T(8,128)(2,1)S(1)}, u32[]{:S(2)}, u32[]{:S(2)}) collective-permute-start(bf16[3,64,512]{2,1,0:T(8,128)(2,1)S(1)} %collective-permute-done.7.refs_7_), channel_id=1, source_target_pairs={{0,1},{1,0},{2,3},{3,2},{4,5},{5,4},{6,7},{7,6},{8,9},{9,8},{10,11... | collective-permute-start | bytes 589832 | tf_op jit(solution)/shard_map/ppermute | solution.py:31
  25.0 0.0 collective-permute-done.8.refs_8_
  25.0 3.8 %collective-permute-start.12 = (bf16[3,64,512]{2,1,0:T(8,128)(2,1)S(1)}, bf16[3,64,512]{2,1,0:T(8,128)(2,1)S(1)}, u32[]{:S(2)}, u32[]{:S(2)}) collective-permute-start(bf16[3,64,512]{2,1,0:T(8,128)(2,1)S(1)} %collective-permute-done.8.refs_8_), channel_id=1, source_target_pairs={{0,1},{1,0},{2,3},{3,2},{4,5},{5,4},{6,7},{7,6},{8,9},{9,8},{10,11... | collective-permute-start | bytes 589832 | tf_op jit(solution)/shard_map/ppermute | solution.py:31
  28.9 0.0 collective-permute-done.9.refs_9_
  28.9 0.0 collective-permute-start.13
  28.9 1.0 %fusion.3 = f32[64]{0:T(128)S(1)} fusion(bf16[64,512]{1,0:T(8,128)(2,1)} %refs_0_.1), kind=kLoop, calls=%fused_computation.9 | loop fusion | flops 98240 | bytes 65792 | tf_op jit(solution)/shard_map/reduce_sum | solution.py:681
  29.9 0.0 collective-permute-done.3.refs_2_
  29.9 3.0 %prep.1 = (s32[32,1,128]{2,1,0:T(1,128)S(1)}, s32[4096,128]{1,0:T(8,128)S(1)}, f32[4096,128]{1,0:T(8,128)S(1)}, s32[8,64]{1,0:T(8,128)S(1)}, s32[32,128]{1,0:T(8,128)S(1)}, /*index=5*/s32[128,128]{1,0:T(8,128)S(1)}) custom-call(s32[1]{0:T(128)} %bitcast.refs_0_, bf16[4,80,512]{2,1,0:T(8,128)(2,1)S(1)} %pad_maximum_fusion.refs_1_, ...), custom_call_target="tpu_custom_call" | custom-call | flops 268435456 | bytes 4194304 | tf_op jit(solution)/shard_map/prep/pallas_call | solution.py:186
  32.8 1.5 %places.1.refs_5_.refs_2_.refs_1_ = s32[4,1,512]{2,1,0:T(1,128)S(1)} custom-call(s32[1]{0:T(128)} %bitcast.refs_0_, s32[32,128]{1,0:T(8,128)S(1)} %get-tuple-element.25.refs_1_, s32[128,128]{1,0:T(8,128)S(1)} %get-tuple-element.26.refs_2_, bf16[80,512]{1,0:T(8,128)(2,1)S(1)} %tell.1.refs_3_, bf16[80,512]{1,0:T(8,128)(2,1)S(1)} %collective-permute-done.4.refs_4_, ...), custom_call_target="tpu_custom_call" | custom-call | flops 268435456 | bytes 131072 | tf_op jit(solution)/shard_map/places/pallas_call | solution.py:207
  34.3 5.9 %pack.1 = (bf16[4864,512]{1,0:T(8,128)(2,1)S(1)}, bf16[4864,512]{1,0:T(8,128)(2,1)S(1)}, f32[4864,128]{1,0:T(8,128)S(1)}) custom-call(s32[8,64]{1,0:T(8,128)S(1)} %get-tuple-element.21.off_ref.refs_0_, s32[32,1,128]{2,1,0:T(1,128)S(1)} %get-tuple-element.22.row_ref, f32[4096,128]{1,0:T(8,128)S(1)} %get-tuple-element.23.cnt_ref, bf16[4096,512]{1,0:T(8,128)(2,1)} %refs_4_.1), custom_call_target="tpu_custom_call" | custom-call | flops 1342177280 | bytes 8388608 | tf_op jit(solution)/shard_map/pack/pallas_call | solution.py:263
  40.2 0.0 collective-permute-done.10.refs_10_
  40.2 0.0 collective-permute-done.11.refs_11_
  40.2 0.0 collective-permute-done.12.refs_12_
  40.2 0.0 collective-permute-done.13.refs_13_
  40.2 10.3 %logits.1 = (bf16[4096,2048]{1,0:T(8,128)(2,1)}, f32[4,1,512]{2,1,0:T(1,128)S(1)}, f32[4,1,512]{2,1,0:T(1,128)S(1)}, bf16[2048,512]{1,0:T(8,128)(2,1)S(1)}) custom-call(s32[8,64]{1,0:T(8,128)S(1)} %get-tuple-element.21.off_ref.refs_0_, bf16[4,80,512]{2,1,0:T(8,128)(2,1)S(1)} %pad_maximum_fusion.refs_1_, ...), custom_call_target="tpu_custom_call" | custom-call | flops 4294967296 | bytes 10485760 | tf_op jit(solution)/shard_map/logits/pallas_call | solution.py:377
  50.5 0.1 collective-permute-start.18
  50.6 7.2 %rows.1 = (bf16[4,128,512]{2,1,0:T(8,128)(2,1)S(1)}, bf16[4,128,512]{2,1,0:T(8,128)(2,1)S(1)}) custom-call(s32[8,64]{1,0:T(8,128)S(1)} %get-tuple-element.21.off_ref.refs_0_, bf16[4864,512]{1,0:T(8,128)(2,1)S(1)} %get-tuple-element.24.refs_3_.refs_1_, s32[4,1,512]{2,1,0:T(1,128)S(1)} %places.1.refs_5_.refs_2_.refs_1_, ...), custom_call_target="tpu_custom_call" | custom-call | flops 2147483648 | bytes 4980736 | tf_op jit(solution)/shard_map/rows/pallas_call | solution.py:446
  57.8 0.1 collective-permute-start.14
  57.9 0.0 collective-permute-done.18
  57.9 0.1 collective-permute-start.19
  58.0 0.1 collective-permute-start.20
  58.1 2.6 %collective-permute-start.21 = (f32[4,1,512]{2,1,0:T(1,128)S(1)}, f32[4,1,512]{2,1,0:T(1,128)S(1)}, u32[]{:S(2)}, u32[]{:S(2)}) collective-permute-start(f32[4,1,512]{2,1,0:T(1,128)S(1)} %add.30.refs_8_), channel_id=1, source_target_pairs={{0,6},{1,7},{2,4},{3,5},{4,2},{5,3},{6,0},{7,1},{8,14},{9,15},{10,... | collective-permute-start | bytes 24584 | tf_op jit(solution)/shard_map/ppermute | solution.py:31
  60.7 0.0 collective-permute-done.19.refs_9_
  60.7 0.0 collective-permute-done.20.refs_10_
  60.7 1.0 %collective-permute-done.21.refs_11_ = f32[4,1,512]{2,1,0:T(1,128)S(1)} collective-permute-done((f32[4,1,512]{2,1,0:T(1,128)S(1)}, f32[4,1,512]{2,1,0:T(1,128)S(1)}, u32[]{:S(2)}, u32[]{:S(2)}) %collective-permute-start.21) | collective-permute-done | bytes 8224 | tf_op jit(solution)/shard_map/ppermute | solution.py:31
  61.7 18.7 %update.1 = (f32[4096,512]{1,0:T(8,128)}, bf16[4096,512]{1,0:T(8,128)(2,1)}, f32[1,512]{1,0:T(1,128)S(1)}) custom-call(s32[8,64]{1,0:T(8,128)S(1)} %get-tuple-element.21.off_ref.refs_0_, s32[4,1,512]{2,1,0:T(1,128)S(1)} %places.1.refs_5_.refs_2_.refs_1_, s32[4096,128]{1,0:T(8,128)S(1)} %get-tuple-element.31.refs_2_, ...), custom_call_target="tpu_custom_call" | custom-call | flops 4294967296 | bytes 33554432 | tf_op jit(solution)/shard_map/update/pallas_call | solution.py:599
  80.4 0.0 copy-start
  80.4 0.0 collective-permute-done.14
  80.4 0.2 fusion.5
  80.6 0.1 collective-permute-start.17
  80.7 0.1 collective-permute-start.16
  80.8 2.6 %collective-permute-start.15 = (bf16[128,512]{1,0:T(8,128)(2,1)S(1)}, bf16[128,512]{1,0:T(8,128)(2,1)S(1)}, u32[]{:S(2)}, u32[]{:S(2)}) collective-permute-start(bf16[128,512]{1,0:T(8,128)(2,1)S(1)} %get-tuple-element.41), channel_id=1, source_target_pairs={{0,2},{1,3},{2,0},{3,1},{4,6},{5,7},{6,4},{7,5},{8,10},{9,11},{10,... | collective-permute-start | bytes 393224 | tf_op jit(solution)/shard_map/ppermute | solution.py:31
  83.4 2.9 %collective-permute-done.17 = bf16[128,512]{1,0:T(8,128)(2,1)S(1)} collective-permute-done((bf16[128,512]{1,0:T(8,128)(2,1)S(1)}, bf16[128,512]{1,0:T(8,128)(2,1)S(1)}, u32[]{:S(2)}, u32[]{:S(2)}) %collective-permute-start.17) | collective-permute-done | bytes 131104 | tf_op jit(solution)/shard_map/ppermute | solution.py:31
  86.3 2.6 %collective-permute-done.16 = bf16[128,512]{1,0:T(8,128)(2,1)S(1)} collective-permute-done((bf16[128,512]{1,0:T(8,128)(2,1)S(1)}, bf16[128,512]{1,0:T(8,128)(2,1)S(1)}, u32[]{:S(2)}, u32[]{:S(2)}) %collective-permute-start.16) | collective-permute-done | bytes 131104 | tf_op jit(solution)/shard_map/ppermute | solution.py:31
  88.8 0.0 collective-permute-done.15
  88.8 0.1 fusion.2
  88.9 0.0 copy-done
  88.9 0.2 multiply_reduce_fusion
  89.1 0.8 subtract_divide_fusion
  (9 shorter events, 0.1 us)
Async XLA Ops:
  1.6 6.9 %collective-permute-start.2 = (bf16[80,512]{1,0:T(8,128)(2,1)S(1)}, bf16[80,512]{1,0:T(8,128)(2,1)S(1)}, u32[]{:S(2)}, u32[]{:S(2)}) collective-permute-start(bf16[80,512]{1,0:T(8,128)(2,1)S(1)} %tell.1.refs_3_), channel_id=1, source_target_pairs={{0,6},{1,7},{2,4},{3,5},{4,2},{5,3},{6,0},{7,1},{8,14},{9,15},{10,... | collective-permute-start | bytes 245768 | tf_op jit(solution)/shard_map/ppermute | solution.py:31
  4.7 4.3 %collective-permute-start.1 = (bf16[80,512]{1,0:T(8,128)(2,1)S(1)}, bf16[80,512]{1,0:T(8,128)(2,1)S(1)}, u32[]{:S(2)}, u32[]{:S(2)}) collective-permute-start(bf16[80,512]{1,0:T(8,128)(2,1)S(1)} %tell.1.refs_3_), channel_id=1, source_target_pairs={{0,4},{1,5},{2,6},{3,7},{4,0},{5,1},{6,2},{7,3},{8,12},{9,13},{10,... | collective-permute-start | bytes 245768 | tf_op jit(solution)/shard_map/ppermute | solution.py:31
  4.9 4.2 %collective-permute-start = (bf16[80,512]{1,0:T(8,128)(2,1)S(1)}, bf16[80,512]{1,0:T(8,128)(2,1)S(1)}, u32[]{:S(2)}, u32[]{:S(2)}) collective-permute-start(bf16[80,512]{1,0:T(8,128)(2,1)S(1)} %tell.1.refs_3_), channel_id=1, source_target_pairs={{0,2},{1,3},{2,0},{3,1},{4,6},{5,7},{6,4},{7,5},{8,10},{9,11},{10,... | collective-permute-start | bytes 245768 | tf_op jit(solution)/shard_map/ppermute | solution.py:31
  5.0 10.7 %collective-permute-start.4 = (bf16[80,512]{1,0:T(8,128)(2,1)S(1)}, bf16[80,512]{1,0:T(8,128)(2,1)S(1)}, u32[]{:S(2)}, u32[]{:S(2)}) collective-permute-start(bf16[80,512]{1,0:T(8,128)(2,1)S(1)} %tell.1.refs_3_), channel_id=1, source_target_pairs={{0,8},{8,16},{16,24},{24,0},{1,9},{9,17},{17,25},{25,1},{2,10},{10... | collective-permute-start | bytes 245768 | tf_op jit(solution)/shard_map/ppermute | solution.py:36
  6.5 9.2 %collective-permute-start.5 = (bf16[80,512]{1,0:T(8,128)(2,1)S(1)}, bf16[80,512]{1,0:T(8,128)(2,1)S(1)}, u32[]{:S(2)}, u32[]{:S(2)}) collective-permute-start(bf16[80,512]{1,0:T(8,128)(2,1)S(1)} %tell.1.refs_3_), channel_id=1, source_target_pairs={{0,24},{8,0},{16,8},{24,16},{1,25},{9,1},{17,9},{25,17},{2,26},{10... | collective-permute-start | bytes 245768 | tf_op jit(solution)/shard_map/ppermute | solution.py:36
  8.5 7.2 %collective-permute-start.6 = (bf16[80,512]{1,0:T(8,128)(2,1)S(1)}, bf16[80,512]{1,0:T(8,128)(2,1)S(1)}, u32[]{:S(2)}, u32[]{:S(2)}) collective-permute-start(bf16[80,512]{1,0:T(8,128)(2,1)S(1)} %tell.1.refs_3_), channel_id=1, source_target_pairs={{0,16},{8,24},{16,0},{24,8},{1,17},{9,25},{17,1},{25,9},{2,18},{10... | collective-permute-start | bytes 245768 | tf_op jit(solution)/shard_map/ppermute | solution.py:36
  9.1 20.7 %collective-permute-start.3 = (bf16[4,80,512]{2,1,0:T(8,128)(2,1)S(1)}, bf16[4,80,512]{2,1,0:T(8,128)(2,1)S(1)}, u32[]{:S(2)}, u32[]{:S(2)}) collective-permute-start(bf16[4,80,512]{2,1,0:T(8,128)(2,1)S(1)} %pad_maximum_fusion.refs_1_), channel_id=1, source_target_pairs={{0,1},{1,0},{2,3},{3,2},{4,5},{5,4},{6,7},{7,6},{8,9},{9,8},{10,11... | collective-permute-start | bytes 983048 | tf_op jit(solution)/shard_map/ppermute | solution.py:31
  15.8 5.3 %collective-permute-start.7 = (bf16[3,64,512]{2,1,0:T(8,128)(2,1)S(1)}, bf16[3,64,512]{2,1,0:T(8,128)(2,1)S(1)}, u32[]{:S(2)}, u32[]{:S(2)}) collective-permute-start(bf16[3,64,512]{2,1,0:T(8,128)(2,1)S(1)} %pad_maximum_fusion.1.refs_6_), channel_id=1, source_target_pairs={{0,2},{1,3},{2,0},{3,1},{4,6},{5,7},{6,4},{7,5},{8,10},{9,11},{10,... | collective-permute-start | bytes 589832 | tf_op jit(solution)/shard_map/ppermute | solution.py:31
  17.2 7.9 %collective-permute-start.8 = (bf16[3,64,512]{2,1,0:T(8,128)(2,1)S(1)}, bf16[3,64,512]{2,1,0:T(8,128)(2,1)S(1)}, u32[]{:S(2)}, u32[]{:S(2)}) collective-permute-start(bf16[3,64,512]{2,1,0:T(8,128)(2,1)S(1)} %pad_maximum_fusion.1.refs_6_), channel_id=1, source_target_pairs={{0,4},{1,5},{2,6},{3,7},{4,0},{5,1},{6,2},{7,3},{8,12},{9,13},{10,... | collective-permute-start | bytes 589832 | tf_op jit(solution)/shard_map/ppermute | solution.py:31
  18.4 10.5 %collective-permute-start.9 = (bf16[3,64,512]{2,1,0:T(8,128)(2,1)S(1)}, bf16[3,64,512]{2,1,0:T(8,128)(2,1)S(1)}, u32[]{:S(2)}, u32[]{:S(2)}) collective-permute-start(bf16[3,64,512]{2,1,0:T(8,128)(2,1)S(1)} %pad_maximum_fusion.1.refs_6_), channel_id=1, source_target_pairs={{0,6},{1,7},{2,4},{3,5},{4,2},{5,3},{6,0},{7,1},{8,14},{9,15},{10,... | collective-permute-start | bytes 589832 | tf_op jit(solution)/shard_map/ppermute | solution.py:31
  18.5 21.7 %collective-permute-start.10 = (bf16[3,64,512]{2,1,0:T(8,128)(2,1)S(1)}, bf16[3,64,512]{2,1,0:T(8,128)(2,1)S(1)}, u32[]{:S(2)}, u32[]{:S(2)}) collective-permute-start(bf16[3,64,512]{2,1,0:T(8,128)(2,1)S(1)} %pad_maximum_fusion.1.refs_6_), channel_id=1, source_target_pairs={{0,1},{1,0},{2,3},{3,2},{4,5},{5,4},{6,7},{7,6},{8,9},{9,8},{10,11... | collective-permute-start | bytes 589832 | tf_op jit(solution)/shard_map/ppermute | solution.py:31
  21.1 19.1 %collective-permute-start.11 = (bf16[3,64,512]{2,1,0:T(8,128)(2,1)S(1)}, bf16[3,64,512]{2,1,0:T(8,128)(2,1)S(1)}, u32[]{:S(2)}, u32[]{:S(2)}) collective-permute-start(bf16[3,64,512]{2,1,0:T(8,128)(2,1)S(1)} %collective-permute-done.7.refs_7_), channel_id=1, source_target_pairs={{0,1},{1,0},{2,3},{3,2},{4,5},{5,4},{6,7},{7,6},{8,9},{9,8},{10,11... | collective-permute-start | bytes 589832 | tf_op jit(solution)/shard_map/ppermute | solution.py:31
  25.0 15.2 %collective-permute-start.12 = (bf16[3,64,512]{2,1,0:T(8,128)(2,1)S(1)}, bf16[3,64,512]{2,1,0:T(8,128)(2,1)S(1)}, u32[]{:S(2)}, u32[]{:S(2)}) collective-permute-start(bf16[3,64,512]{2,1,0:T(8,128)(2,1)S(1)} %collective-permute-done.8.refs_8_), channel_id=1, source_target_pairs={{0,1},{1,0},{2,3},{3,2},{4,5},{5,4},{6,7},{7,6},{8,9},{9,8},{10,11... | collective-permute-start | bytes 589832 | tf_op jit(solution)/shard_map/ppermute | solution.py:31
  28.9 11.3 %collective-permute-start.13 = (bf16[3,64,512]{2,1,0:T(8,128)(2,1)S(1)}, bf16[3,64,512]{2,1,0:T(8,128)(2,1)S(1)}, u32[]{:S(2)}, u32[]{:S(2)}) collective-permute-start(bf16[3,64,512]{2,1,0:T(8,128)(2,1)S(1)} %collective-permute-done.9.refs_9_), channel_id=1, source_target_pairs={{0,1},{1,0},{2,3},{3,2},{4,5},{5,4},{6,7},{7,6},{8,9},{9,8},{10,11... | collective-permute-start | bytes 589832 | tf_op jit(solution)/shard_map/ppermute | solution.py:31
  50.5 7.4 %collective-permute-start.18 = (f32[4,1,512]{2,1,0:T(1,128)S(1)}, f32[4,1,512]{2,1,0:T(1,128)S(1)}, u32[]{:S(2)}, u32[]{:S(2)}) collective-permute-start(f32[4,1,512]{2,1,0:T(1,128)S(1)} %get-tuple-element.35), channel_id=1, source_target_pairs={{0,1},{1,0},{2,3},{3,2},{4,5},{5,4},{6,7},{7,6},{8,9},{9,8},{10,11... | collective-permute-start | bytes 24584 | tf_op jit(solution)/shard_map/ppermute | solution.py:31
  57.8 22.6 %collective-permute-start.14 = (bf16[4,128,512]{2,1,0:T(8,128)(2,1)S(1)}, bf16[4,128,512]{2,1,0:T(8,128)(2,1)S(1)}, u32[]{:S(2)}, u32[]{:S(2)}) collective-permute-start(bf16[4,128,512]{2,1,0:T(8,128)(2,1)S(1)} %get-tuple-element.30), channel_id=1, source_target_pairs={{0,1},{1,0},{2,3},{3,2},{4,5},{5,4},{6,7},{7,6},{8,9},{9,8},{10,11... | collective-permute-start | bytes 1572872 | tf_op jit(solution)/shard_map/ppermute | solution.py:31
  57.9 2.7 %collective-permute-start.19 = (f32[4,1,512]{2,1,0:T(1,128)S(1)}, f32[4,1,512]{2,1,0:T(1,128)S(1)}, u32[]{:S(2)}, u32[]{:S(2)}) collective-permute-start(f32[4,1,512]{2,1,0:T(1,128)S(1)} %add.30.refs_8_), channel_id=1, source_target_pairs={{0,2},{1,3},{2,0},{3,1},{4,6},{5,7},{6,4},{7,5},{8,10},{9,11},{10,... | collective-permute-start | bytes 24584 | tf_op jit(solution)/shard_map/ppermute | solution.py:31
  58.0 2.6 %collective-permute-start.20 = (f32[4,1,512]{2,1,0:T(1,128)S(1)}, f32[4,1,512]{2,1,0:T(1,128)S(1)}, u32[]{:S(2)}, u32[]{:S(2)}) collective-permute-start(f32[4,1,512]{2,1,0:T(1,128)S(1)} %add.30.refs_8_), channel_id=1, source_target_pairs={{0,4},{1,5},{2,6},{3,7},{4,0},{5,1},{6,2},{7,3},{8,12},{9,13},{10,... | collective-permute-start | bytes 24584 | tf_op jit(solution)/shard_map/ppermute | solution.py:31
  58.1 3.6 %collective-permute-start.21 = (f32[4,1,512]{2,1,0:T(1,128)S(1)}, f32[4,1,512]{2,1,0:T(1,128)S(1)}, u32[]{:S(2)}, u32[]{:S(2)}) collective-permute-start(f32[4,1,512]{2,1,0:T(1,128)S(1)} %add.30.refs_8_), channel_id=1, source_target_pairs={{0,6},{1,7},{2,4},{3,5},{4,2},{5,3},{6,0},{7,1},{8,14},{9,15},{10,... | collective-permute-start | bytes 24584 | tf_op jit(solution)/shard_map/ppermute | solution.py:31
  80.4 8.5 %copy-start = (bf16[64,512]{1,0:T(8,128)(2,1)S(1)}, bf16[64,512]{1,0:T(8,128)(2,1)}, u32[]{:S(2)}) copy-start(bf16[64,512]{1,0:T(8,128)(2,1)} %refs_0_.1) | copy-start | bytes 196612
  80.6 5.6 %collective-permute-start.17 = (bf16[128,512]{1,0:T(8,128)(2,1)S(1)}, bf16[128,512]{1,0:T(8,128)(2,1)S(1)}, u32[]{:S(2)}, u32[]{:S(2)}) collective-permute-start(bf16[128,512]{1,0:T(8,128)(2,1)S(1)} %get-tuple-element.42), channel_id=1, source_target_pairs={{0,6},{1,7},{2,4},{3,5},{4,2},{5,3},{6,0},{7,1},{8,14},{9,15},{10,... | collective-permute-start | bytes 393224 | tf_op jit(solution)/shard_map/ppermute | solution.py:31
  80.7 8.1 %collective-permute-start.16 = (bf16[128,512]{1,0:T(8,128)(2,1)S(1)}, bf16[128,512]{1,0:T(8,128)(2,1)S(1)}, u32[]{:S(2)}, u32[]{:S(2)}) collective-permute-start(bf16[128,512]{1,0:T(8,128)(2,1)S(1)} %get-tuple-element.43), channel_id=1, source_target_pairs={{0,4},{1,5},{2,6},{3,7},{4,0},{5,1},{6,2},{7,3},{8,12},{9,13},{10,... | collective-permute-start | bytes 393224 | tf_op jit(solution)/shard_map/ppermute | solution.py:31
  80.8 8.0 %collective-permute-start.15 = (bf16[128,512]{1,0:T(8,128)(2,1)S(1)}, bf16[128,512]{1,0:T(8,128)(2,1)S(1)}, u32[]{:S(2)}, u32[]{:S(2)}) collective-permute-start(bf16[128,512]{1,0:T(8,128)(2,1)S(1)} %get-tuple-element.41), channel_id=1, source_target_pairs={{0,2},{1,3},{2,0},{3,1},{4,6},{5,7},{6,4},{7,5},{8,10},{9,11},{10,... | collective-permute-start | bytes 393224 | tf_op jit(solution)/shard_map/ppermute | solution.py:31

commit v5 on v4

--- a/solution.py
+++ b/solution.py
@@ -421,13 +421,13 @@
         a = [w[:size, :] for w in w_refs] + [ones_where(ids == at_ref[j][:, :own]) for j in range(chunks)]
         acc[...] += dot(jnp.concatenate(a, axis=1), what_ref[:size, :], 0, 0)
 
-    @pl.when(left > tile // 2)
-    def _():
-        add(tile)
-
-    @pl.when((left > 0) & (left <= tile // 2))
-    def _():
-        add(tile // 2)
+    quarter = tile // 4
+    for size in range(quarter, tile + 1, quarter):
+        fits = left > size - quarter if size == tile else (left > size - quarter) & (left <= size)
+
+        @pl.when(fits)
+        def _():
+            add(size)
 
     @pl.when(i == pl.num_programs(0) - 1)
     def _():
@@ -667,7 +667,7 @@
     den = own_den + swap(turned, "cls", 1)
     dens = [den] + [swap(den, "cls", 2 * q) for q in range(1, chips)]
 
-    self_part, away_part = row_parts(off, what, at, w, 2 * rows_here, tile)
+    self_part, away_part = row_parts(off, what, at, w, 2 * rows_here, min(1024, home_rows))
     pair = self_part.astype(f32) + swap(away_part, "cls", 1).astype(f32)
     sums = [swap(pair[q].astype(bf16), "cls", 2 * q) for q in range(1, chips)]
 

time: 91 us -> 89.7 us (0.986)
  Pallas kernels: 47.5 us -> 46.3 us
    pallas_call x1, Pallas kernels: 7.24 us -> 5.99 us  [row_parts(): pl.pallas_call(lambda *refs: rows_kernel(chunks, *refs), grid_spec=pltpu....]
where the time goes in v5:
time: 89.7 us; the launch traced here: 88.6 us
  Pallas kernels  46.3 us (52%)
  starting transfers between devices  28.3 us (32%)
  waiting for transfers between devices  10.9 us (12%)
  other arithmetic  2.24 us (2%)
  between operations  0.9 us (1%)
    ppermute x19, starting transfers between devices, swap(): return lax.ppermute(x, axis_name, [(i, i ^ m) for i in range(n)])  24.4 us
    pallas_call x1, Pallas kernels, update(): pl.pallas_call(lambda *refs: update_kernel(chunks, step, tile, *refs), in...  18.7 us
    pallas_call x1, Pallas kernels, logits(): pl.pallas_call(lambda *refs: logits_kernel(chunks, tile, *refs), in_specs...  10.3 us
    ppermute x19, waiting for transfers between devices, swap(): return lax.ppermute(x, axis_name, [(i, i ^ m) for i in range(n)])  6.59 us
    pallas_call x1, Pallas kernels, row_parts(): pl.pallas_call(lambda *refs: rows_kernel(chunks, *refs), grid_spec=pltpu....  5.99 us
    pallas_call x1, Pallas kernels, pack(): pl.pallas_call(pack_kernel, grid=(classes // tile,), in_specs=[pl.BlockSp...  5.89 us
    ppermute x3, waiting for transfers between devices, shift(): return lax.ppermute(x, axis_name, [(i, (i + m) % n) for i in range(n)])  4.27 us
    ppermute x3, starting transfers between devices, shift(): return lax.ppermute(x, axis_name, [(i, (i + m) % n) for i in range(n)])  3.97 us
  transfers between devices with their start and end apart: 22, of which 5 were waited for; matrix products, arithmetic and copies ran while one was open for 1% of the time, Pallas kernels for 40%

profile of v5, /device:TPU:1, one launch (start us, length us, event | category | flops | bytes accessed | tf_op | source)
XLA Modules:
  0.0 88.6 jit_solution(18326522010431262241)
XLA Ops:
  0.6 1.0 %tell.1.refs_3_ = bf16[80,512]{1,0:T(8,128)(2,1)S(1)} custom-call(bf16[64,512]{1,0:T(8,128)(2,1)} %refs_0_.1, s32[16,128]{1,0:T(8,128)} %bitcast.34, s32[16,128]{1,0:T(8,128)} %bitcast.35, s32[4,128]{1,0:T(4,128)} %bitcast.36), custom_call_target="tpu_custom_call" | custom-call | tf_op jit(solution)/shard_map/tell/pallas_call | solution.py:89
  1.6 3.0 %collective-permute-start.2 = (bf16[80,512]{1,0:T(8,128)(2,1)S(1)}, bf16[80,512]{1,0:T(8,128)(2,1)S(1)}, u32[]{:S(2)}, u32[]{:S(2)}) collective-permute-start(bf16[80,512]{1,0:T(8,128)(2,1)S(1)} %tell.1.refs_3_), channel_id=1, source_target_pairs={{0,6},{1,7},{2,4},{3,5},{4,2},{5,3},{6,0},{7,1},{8,14},{9,15},{10,... | collective-permute-start | bytes 245768 | tf_op jit(solution)/shard_map/ppermute | solution.py:31
  4.7 0.2 collective-permute-start.1
  4.9 0.1 collective-permute-start
  5.0 1.4 %collective-permute-start.4 = (bf16[80,512]{1,0:T(8,128)(2,1)S(1)}, bf16[80,512]{1,0:T(8,128)(2,1)S(1)}, u32[]{:S(2)}, u32[]{:S(2)}) collective-permute-start(bf16[80,512]{1,0:T(8,128)(2,1)S(1)} %tell.1.refs_3_), channel_id=1, source_target_pairs={{0,8},{8,16},{16,24},{24,0},{1,9},{9,17},{17,25},{25,1},{2,10},{10... | collective-permute-start | bytes 245768 | tf_op jit(solution)/shard_map/ppermute | solution.py:36
  6.5 2.0 %collective-permute-start.5 = (bf16[80,512]{1,0:T(8,128)(2,1)S(1)}, bf16[80,512]{1,0:T(8,128)(2,1)S(1)}, u32[]{:S(2)}, u32[]{:S(2)}) collective-permute-start(bf16[80,512]{1,0:T(8,128)(2,1)S(1)} %tell.1.refs_3_), channel_id=1, source_target_pairs={{0,24},{8,0},{16,8},{24,16},{1,25},{9,1},{17,9},{25,17},{2,26},{10... | collective-permute-start | bytes 245768 | tf_op jit(solution)/shard_map/ppermute | solution.py:36
  8.5 0.0 collective-permute-done.2
  8.5 0.5 collective-permute-start.6
  9.0 0.0 collective-permute-done.1
  9.0 0.1 collective-permute-done
  9.1 2.3 %collective-permute-start.3 = (bf16[4,80,512]{2,1,0:T(8,128)(2,1)S(1)}, bf16[4,80,512]{2,1,0:T(8,128)(2,1)S(1)}, u32[]{:S(2)}, u32[]{:S(2)}) collective-permute-start(bf16[4,80,512]{2,1,0:T(8,128)(2,1)S(1)} %pad_maximum_fusion.refs_1_), channel_id=1, source_target_pairs={{0,1},{1,0},{2,3},{3,2},{4,5},{5,4},{6,7},{7,6},{8,9},{9,8},{10,11... | collective-permute-start | bytes 983048 | tf_op jit(solution)/shard_map/ppermute | solution.py:31
  11.4 4.3 %collective-permute-done.6.refs_6_ = bf16[80,512]{1,0:T(8,128)(2,1)S(1)} collective-permute-done((bf16[80,512]{1,0:T(8,128)(2,1)S(1)}, bf16[80,512]{1,0:T(8,128)(2,1)S(1)}, u32[]{:S(2)}, u32[]{:S(2)}) %collective-permute-start.6) | collective-permute-done | bytes 81952 | tf_op jit(solution)/shard_map/ppermute | solution.py:36
  15.7 0.0 collective-permute-done.5.refs_5_
  15.7 0.0 collective-permute-done.4.refs_4_
  15.8 1.4 %collective-permute-start.7 = (bf16[3,64,512]{2,1,0:T(8,128)(2,1)S(1)}, bf16[3,64,512]{2,1,0:T(8,128)(2,1)S(1)}, u32[]{:S(2)}, u32[]{:S(2)}) collective-permute-start(bf16[3,64,512]{2,1,0:T(8,128)(2,1)S(1)} %pad_maximum_fusion.1.refs_6_), channel_id=1, source_target_pairs={{0,2},{1,3},{2,0},{3,1},{4,6},{5,7},{6,4},{7,5},{8,10},{9,11},{10,... | collective-permute-start | bytes 589832 | tf_op jit(solution)/shard_map/ppermute | solution.py:31
  17.2 1.2 %collective-permute-start.8 = (bf16[3,64,512]{2,1,0:T(8,128)(2,1)S(1)}, bf16[3,64,512]{2,1,0:T(8,128)(2,1)S(1)}, u32[]{:S(2)}, u32[]{:S(2)}) collective-permute-start(bf16[3,64,512]{2,1,0:T(8,128)(2,1)S(1)} %pad_maximum_fusion.1.refs_6_), channel_id=1, source_target_pairs={{0,4},{1,5},{2,6},{3,7},{4,0},{5,1},{6,2},{7,3},{8,12},{9,13},{10,... | collective-permute-start | bytes 589832 | tf_op jit(solution)/shard_map/ppermute | solution.py:31
  18.4 0.1 collective-permute-start.9
  18.5 2.6 %collective-permute-start.10 = (bf16[3,64,512]{2,1,0:T(8,128)(2,1)S(1)}, bf16[3,64,512]{2,1,0:T(8,128)(2,1)S(1)}, u32[]{:S(2)}, u32[]{:S(2)}) collective-permute-start(bf16[3,64,512]{2,1,0:T(8,128)(2,1)S(1)} %pad_maximum_fusion.1.refs_6_), channel_id=1, source_target_pairs={{0,1},{1,0},{2,3},{3,2},{4,5},{5,4},{6,7},{7,6},{8,9},{9,8},{10,11... | collective-permute-start | bytes 589832 | tf_op jit(solution)/shard_map/ppermute | solution.py:31
  21.1 0.0 collective-permute-done.7.refs_7_
  21.1 4.0 %collective-permute-start.11 = (bf16[3,64,512]{2,1,0:T(8,128)(2,1)S(1)}, bf16[3,64,512]{2,1,0:T(8,128)(2,1)S(1)}, u32[]{:S(2)}, u32[]{:S(2)}) collective-permute-start(bf16[3,64,512]{2,1,0:T(8,128)(2,1)S(1)} %collective-permute-done.7.refs_7_), channel_id=1, source_target_pairs={{0,1},{1,0},{2,3},{3,2},{4,5},{5,4},{6,7},{7,6},{8,9},{9,8},{10,11... | collective-permute-start | bytes 589832 | tf_op jit(solution)/shard_map/ppermute | solution.py:31
  25.0 0.0 collective-permute-done.8.refs_8_
  25.0 3.8 %collective-permute-start.12 = (bf16[3,64,512]{2,1,0:T(8,128)(2,1)S(1)}, bf16[3,64,512]{2,1,0:T(8,128)(2,1)S(1)}, u32[]{:S(2)}, u32[]{:S(2)}) collective-permute-start(bf16[3,64,512]{2,1,0:T(8,128)(2,1)S(1)} %collective-permute-done.8.refs_8_), channel_id=1, source_target_pairs={{0,1},{1,0},{2,3},{3,2},{4,5},{5,4},{6,7},{7,6},{8,9},{9,8},{10,11... | collective-permute-start | bytes 589832 | tf_op jit(solution)/shard_map/ppermute | solution.py:31
  28.9 0.0 collective-permute-done.9.refs_9_
  28.9 0.0 collective-permute-start.13
  28.9 1.0 %fusion.3 = f32[64]{0:T(128)S(1)} fusion(bf16[64,512]{1,0:T(8,128)(2,1)} %refs_0_.1), kind=kLoop, calls=%fused_computation.9 | loop fusion | flops 98240 | bytes 65792 | tf_op jit(solution)/shard_map/reduce_sum | solution.py:681
  29.9 0.0 collective-permute-done.3.refs_2_
  29.9 3.0 %prep.1 = (s32[32,1,128]{2,1,0:T(1,128)S(1)}, s32[4096,128]{1,0:T(8,128)S(1)}, f32[4096,128]{1,0:T(8,128)S(1)}, s32[8,64]{1,0:T(8,128)S(1)}, s32[32,128]{1,0:T(8,128)S(1)}, /*index=5*/s32[128,128]{1,0:T(8,128)S(1)}) custom-call(s32[1]{0:T(128)} %bitcast.refs_0_, bf16[4,80,512]{2,1,0:T(8,128)(2,1)S(1)} %pad_maximum_fusion.refs_1_, ...), custom_call_target="tpu_custom_call" | custom-call | flops 268435456 | bytes 4194304 | tf_op jit(solution)/shard_map/prep/pallas_call | solution.py:186
  32.8 1.5 %places.1.refs_5_.refs_2_.refs_1_ = s32[4,1,512]{2,1,0:T(1,128)S(1)} custom-call(s32[1]{0:T(128)} %bitcast.refs_0_, s32[32,128]{1,0:T(8,128)S(1)} %get-tuple-element.25.refs_1_, s32[128,128]{1,0:T(8,128)S(1)} %get-tuple-element.26.refs_2_, bf16[80,512]{1,0:T(8,128)(2,1)S(1)} %tell.1.refs_3_, bf16[80,512]{1,0:T(8,128)(2,1)S(1)} %collective-permute-done.4.refs_4_, ...), custom_call_target="tpu_custom_call" | custom-call | flops 268435456 | bytes 131072 | tf_op jit(solution)/shard_map/places/pallas_call | solution.py:207
  34.3 5.9 %pack.1 = (bf16[4864,512]{1,0:T(8,128)(2,1)S(1)}, bf16[4864,512]{1,0:T(8,128)(2,1)S(1)}, f32[4864,128]{1,0:T(8,128)S(1)}) custom-call(s32[8,64]{1,0:T(8,128)S(1)} %get-tuple-element.21.off_ref.refs_0_, s32[32,1,128]{2,1,0:T(1,128)S(1)} %get-tuple-element.22.row_ref, f32[4096,128]{1,0:T(8,128)S(1)} %get-tuple-element.23.cnt_ref, bf16[4096,512]{1,0:T(8,128)(2,1)} %refs_4_.1), custom_call_target="tpu_custom_call" | custom-call | flops 1342177280 | bytes 8388608 | tf_op jit(solution)/shard_map/pack/pallas_call | solution.py:263
  40.2 0.0 collective-permute-done.10.refs_10_
  40.2 0.0 collective-permute-done.11.refs_11_
  40.2 0.0 collective-permute-done.12.refs_12_
  40.2 0.0 collective-permute-done.13.refs_13_
  40.2 10.3 %logits.1 = (bf16[4096,2048]{1,0:T(8,128)(2,1)}, f32[4,1,512]{2,1,0:T(1,128)S(1)}, f32[4,1,512]{2,1,0:T(1,128)S(1)}, bf16[2048,512]{1,0:T(8,128)(2,1)S(1)}) custom-call(s32[8,64]{1,0:T(8,128)S(1)} %get-tuple-element.21.off_ref.refs_0_, bf16[4,80,512]{2,1,0:T(8,128)(2,1)S(1)} %pad_maximum_fusion.refs_1_, ...), custom_call_target="tpu_custom_call" | custom-call | flops 4294967296 | bytes 10485760 | tf_op jit(solution)/shard_map/logits/pallas_call | solution.py:377
  50.5 0.1 collective-permute-start.18
  50.6 6.0 %rows.1 = (bf16[4,128,512]{2,1,0:T(8,128)(2,1)S(1)}, bf16[4,128,512]{2,1,0:T(8,128)(2,1)S(1)}) custom-call(s32[8,64]{1,0:T(8,128)S(1)} %get-tuple-element.21.off_ref.refs_0_, bf16[4864,512]{1,0:T(8,128)(2,1)S(1)} %get-tuple-element.24.refs_3_.refs_1_, s32[4,1,512]{2,1,0:T(1,128)S(1)} %places.1.refs_5_.refs_2_.refs_1_, ...), custom_call_target="tpu_custom_call" | custom-call | flops 2147483648 | bytes 4980736 | tf_op jit(solution)/shard_map/rows/pallas_call | solution.py:446
  56.6 0.1 collective-permute-start.14
  56.7 0.0 collective-permute-done.18
  56.7 0.1 collective-permute-start.19
  56.8 0.1 collective-permute-start.20
  56.8 2.6 %collective-permute-start.21 = (f32[4,1,512]{2,1,0:T(1,128)S(1)}, f32[4,1,512]{2,1,0:T(1,128)S(1)}, u32[]{:S(2)}, u32[]{:S(2)}) collective-permute-start(f32[4,1,512]{2,1,0:T(1,128)S(1)} %add.30.refs_8_), channel_id=1, source_target_pairs={{0,6},{1,7},{2,4},{3,5},{4,2},{5,3},{6,0},{7,1},{8,14},{9,15},{10,... | collective-permute-start | bytes 24584 | tf_op jit(solution)/shard_map/ppermute | solution.py:31
  59.4 0.0 collective-permute-done.19.refs_9_
  59.4 0.0 collective-permute-done.20.refs_10_
  59.4 1.0 %collective-permute-done.21.refs_11_ = f32[4,1,512]{2,1,0:T(1,128)S(1)} collective-permute-done((f32[4,1,512]{2,1,0:T(1,128)S(1)}, f32[4,1,512]{2,1,0:T(1,128)S(1)}, u32[]{:S(2)}, u32[]{:S(2)}) %collective-permute-start.21) | collective-permute-done | bytes 8224 | tf_op jit(solution)/shard_map/ppermute | solution.py:31
  60.4 18.7 %update.1 = (f32[4096,512]{1,0:T(8,128)}, bf16[4096,512]{1,0:T(8,128)(2,1)}, f32[1,512]{1,0:T(1,128)S(1)}) custom-call(s32[8,64]{1,0:T(8,128)S(1)} %get-tuple-element.21.off_ref.refs_0_, s32[4,1,512]{2,1,0:T(1,128)S(1)} %places.1.refs_5_.refs_2_.refs_1_, s32[4096,128]{1,0:T(8,128)S(1)} %get-tuple-element.31.refs_2_, ...), custom_call_target="tpu_custom_call" | custom-call | flops 4294967296 | bytes 33554432 | tf_op jit(solution)/shard_map/update/pallas_call | solution.py:599
  79.2 0.0 copy-start
  79.2 0.0 collective-permute-done.14
  79.2 0.2 fusion.5
  79.4 0.1 collective-permute-start.17
  79.5 0.1 collective-permute-start.16
  79.6 2.6 %collective-permute-start.15 = (bf16[128,512]{1,0:T(8,128)(2,1)S(1)}, bf16[128,512]{1,0:T(8,128)(2,1)S(1)}, u32[]{:S(2)}, u32[]{:S(2)}) collective-permute-start(bf16[128,512]{1,0:T(8,128)(2,1)S(1)} %get-tuple-element.41), channel_id=1, source_target_pairs={{0,2},{1,3},{2,0},{3,1},{4,6},{5,7},{6,4},{7,5},{8,10},{9,11},{10,... | collective-permute-start | bytes 393224 | tf_op jit(solution)/shard_map/ppermute | solution.py:31
  82.1 2.9 %collective-permute-done.17 = bf16[128,512]{1,0:T(8,128)(2,1)S(1)} collective-permute-done((bf16[128,512]{1,0:T(8,128)(2,1)S(1)}, bf16[128,512]{1,0:T(8,128)(2,1)S(1)}, u32[]{:S(2)}, u32[]{:S(2)}) %collective-permute-start.17) | collective-permute-done | bytes 131104 | tf_op jit(solution)/shard_map/ppermute | solution.py:31
  85.0 2.6 %collective-permute-done.16 = bf16[128,512]{1,0:T(8,128)(2,1)S(1)} collective-permute-done((bf16[128,512]{1,0:T(8,128)(2,1)S(1)}, bf16[128,512]{1,0:T(8,128)(2,1)S(1)}, u32[]{:S(2)}, u32[]{:S(2)}) %collective-permute-start.16) | collective-permute-done | bytes 131104 | tf_op jit(solution)/shard_map/ppermute | solution.py:31
  87.6 0.0 collective-permute-done.15
  87.6 0.1 fusion.2
  87.7 0.0 copy-done
  87.7 0.2 multiply_reduce_fusion
  87.9 0.8 subtract_divide_fusion
  (9 shorter events, 0.1 us)
Async XLA Ops:
  1.6 6.9 %collective-permute-start.2 = (bf16[80,512]{1,0:T(8,128)(2,1)S(1)}, bf16[80,512]{1,0:T(8,128)(2,1)S(1)}, u32[]{:S(2)}, u32[]{:S(2)}) collective-permute-start(bf16[80,512]{1,0:T(8,128)(2,1)S(1)} %tell.1.refs_3_), channel_id=1, source_target_pairs={{0,6},{1,7},{2,4},{3,5},{4,2},{5,3},{6,0},{7,1},{8,14},{9,15},{10,... | collective-permute-start | bytes 245768 | tf_op jit(solution)/shard_map/ppermute | solution.py:31
  4.7 4.3 %collective-permute-start.1 = (bf16[80,512]{1,0:T(8,128)(2,1)S(1)}, bf16[80,512]{1,0:T(8,128)(2,1)S(1)}, u32[]{:S(2)}, u32[]{:S(2)}) collective-permute-start(bf16[80,512]{1,0:T(8,128)(2,1)S(1)} %tell.1.refs_3_), channel_id=1, source_target_pairs={{0,4},{1,5},{2,6},{3,7},{4,0},{5,1},{6,2},{7,3},{8,12},{9,13},{10,... | collective-permute-start | bytes 245768 | tf_op jit(solution)/shard_map/ppermute | solution.py:31
  4.9 4.2 %collective-permute-start = (bf16[80,512]{1,0:T(8,128)(2,1)S(1)}, bf16[80,512]{1,0:T(8,128)(2,1)S(1)}, u32[]{:S(2)}, u32[]{:S(2)}) collective-permute-start(bf16[80,512]{1,0:T(8,128)(2,1)S(1)} %tell.1.refs_3_), channel_id=1, source_target_pairs={{0,2},{1,3},{2,0},{3,1},{4,6},{5,7},{6,4},{7,5},{8,10},{9,11},{10,... | collective-permute-start | bytes 245768 | tf_op jit(solution)/shard_map/ppermute | solution.py:31
  5.0 10.7 %collective-permute-start.4 = (bf16[80,512]{1,0:T(8,128)(2,1)S(1)}, bf16[80,512]{1,0:T(8,128)(2,1)S(1)}, u32[]{:S(2)}, u32[]{:S(2)}) collective-permute-start(bf16[80,512]{1,0:T(8,128)(2,1)S(1)} %tell.1.refs_3_), channel_id=1, source_target_pairs={{0,8},{8,16},{16,24},{24,0},{1,9},{9,17},{17,25},{25,1},{2,10},{10... | collective-permute-start | bytes 245768 | tf_op jit(solution)/shard_map/ppermute | solution.py:36
  6.5 9.2 %collective-permute-start.5 = (bf16[80,512]{1,0:T(8,128)(2,1)S(1)}, bf16[80,512]{1,0:T(8,128)(2,1)S(1)}, u32[]{:S(2)}, u32[]{:S(2)}) collective-permute-start(bf16[80,512]{1,0:T(8,128)(2,1)S(1)} %tell.1.refs_3_), channel_id=1, source_target_pairs={{0,24},{8,0},{16,8},{24,16},{1,25},{9,1},{17,9},{25,17},{2,26},{10... | collective-permute-start | bytes 245768 | tf_op jit(solution)/shard_map/ppermute | solution.py:36
  8.5 7.2 %collective-permute-start.6 = (bf16[80,512]{1,0:T(8,128)(2,1)S(1)}, bf16[80,512]{1,0:T(8,128)(2,1)S(1)}, u32[]{:S(2)}, u32[]{:S(2)}) collective-permute-start(bf16[80,512]{1,0:T(8,128)(2,1)S(1)} %tell.1.refs_3_), channel_id=1, source_target_pairs={{0,16},{8,24},{16,0},{24,8},{1,17},{9,25},{17,1},{25,9},{2,18},{10... | collective-permute-start | bytes 245768 | tf_op jit(solution)/shard_map/ppermute | solution.py:36
  9.1 20.7 %collective-permute-start.3 = (bf16[4,80,512]{2,1,0:T(8,128)(2,1)S(1)}, bf16[4,80,512]{2,1,0:T(8,128)(2,1)S(1)}, u32[]{:S(2)}, u32[]{:S(2)}) collective-permute-start(bf16[4,80,512]{2,1,0:T(8,128)(2,1)S(1)} %pad_maximum_fusion.refs_1_), channel_id=1, source_target_pairs={{0,1},{1,0},{2,3},{3,2},{4,5},{5,4},{6,7},{7,6},{8,9},{9,8},{10,11... | collective-permute-start | bytes 983048 | tf_op jit(solution)/shard_map/ppermute | solution.py:31
  15.8 5.3 %collective-permute-start.7 = (bf16[3,64,512]{2,1,0:T(8,128)(2,1)S(1)}, bf16[3,64,512]{2,1,0:T(8,128)(2,1)S(1)}, u32[]{:S(2)}, u32[]{:S(2)}) collective-permute-start(bf16[3,64,512]{2,1,0:T(8,128)(2,1)S(1)} %pad_maximum_fusion.1.refs_6_), channel_id=1, source_target_pairs={{0,2},{1,3},{2,0},{3,1},{4,6},{5,7},{6,4},{7,5},{8,10},{9,11},{10,... | collective-permute-start | bytes 589832 | tf_op jit(solution)/shard_map/ppermute | solution.py:31
  17.2 7.9 %collective-permute-start.8 = (bf16[3,64,512]{2,1,0:T(8,128)(2,1)S(1)}, bf16[3,64,512]{2,1,0:T(8,128)(2,1)S(1)}, u32[]{:S(2)}, u32[]{:S(2)}) collective-permute-start(bf16[3,64,512]{2,1,0:T(8,128)(2,1)S(1)} %pad_maximum_fusion.1.refs_6_), channel_id=1, source_target_pairs={{0,4},{1,5},{2,6},{3,7},{4,0},{5,1},{6,2},{7,3},{8,12},{9,13},{10,... | collective-permute-start | bytes 589832 | tf_op jit(solution)/shard_map/ppermute | solution.py:31
  18.4 10.5 %collective-permute-start.9 = (bf16[3,64,512]{2,1,0:T(8,128)(2,1)S(1)}, bf16[3,64,512]{2,1,0:T(8,128)(2,1)S(1)}, u32[]{:S(2)}, u32[]{:S(2)}) collective-permute-start(bf16[3,64,512]{2,1,0:T(8,128)(2,1)S(1)} %pad_maximum_fusion.1.refs_6_), channel_id=1, source_target_pairs={{0,6},{1,7},{2,4},{3,5},{4,2},{5,3},{6,0},{7,1},{8,14},{9,15},{10,... | collective-permute-start | bytes 589832 | tf_op jit(solution)/shard_map/ppermute | solution.py:31
  18.5 21.7 %collective-permute-start.10 = (bf16[3,64,512]{2,1,0:T(8,128)(2,1)S(1)}, bf16[3,64,512]{2,1,0:T(8,128)(2,1)S(1)}, u32[]{:S(2)}, u32[]{:S(2)}) collective-permute-start(bf16[3,64,512]{2,1,0:T(8,128)(2,1)S(1)} %pad_maximum_fusion.1.refs_6_), channel_id=1, source_target_pairs={{0,1},{1,0},{2,3},{3,2},{4,5},{5,4},{6,7},{7,6},{8,9},{9,8},{10,11... | collective-permute-start | bytes 589832 | tf_op jit(solution)/shard_map/ppermute | solution.py:31
  21.1 19.1 %collective-permute-start.11 = (bf16[3,64,512]{2,1,0:T(8,128)(2,1)S(1)}, bf16[3,64,512]{2,1,0:T(8,128)(2,1)S(1)}, u32[]{:S(2)}, u32[]{:S(2)}) collective-permute-start(bf16[3,64,512]{2,1,0:T(8,128)(2,1)S(1)} %collective-permute-done.7.refs_7_), channel_id=1, source_target_pairs={{0,1},{1,0},{2,3},{3,2},{4,5},{5,4},{6,7},{7,6},{8,9},{9,8},{10,11... | collective-permute-start | bytes 589832 | tf_op jit(solution)/shard_map/ppermute | solution.py:31
  25.0 15.2 %collective-permute-start.12 = (bf16[3,64,512]{2,1,0:T(8,128)(2,1)S(1)}, bf16[3,64,512]{2,1,0:T(8,128)(2,1)S(1)}, u32[]{:S(2)}, u32[]{:S(2)}) collective-permute-start(bf16[3,64,512]{2,1,0:T(8,128)(2,1)S(1)} %collective-permute-done.8.refs_8_), channel_id=1, source_target_pairs={{0,1},{1,0},{2,3},{3,2},{4,5},{5,4},{6,7},{7,6},{8,9},{9,8},{10,11... | collective-permute-start | bytes 589832 | tf_op jit(solution)/shard_map/ppermute | solution.py:31
  28.9 11.3 %collective-permute-start.13 = (bf16[3,64,512]{2,1,0:T(8,128)(2,1)S(1)}, bf16[3,64,512]{2,1,0:T(8,128)(2,1)S(1)}, u32[]{:S(2)}, u32[]{:S(2)}) collective-permute-start(bf16[3,64,512]{2,1,0:T(8,128)(2,1)S(1)} %collective-permute-done.9.refs_9_), channel_id=1, source_target_pairs={{0,1},{1,0},{2,3},{3,2},{4,5},{5,4},{6,7},{7,6},{8,9},{9,8},{10,11... | collective-permute-start | bytes 589832 | tf_op jit(solution)/shard_map/ppermute | solution.py:31
  50.5 6.2 %collective-permute-start.18 = (f32[4,1,512]{2,1,0:T(1,128)S(1)}, f32[4,1,512]{2,1,0:T(1,128)S(1)}, u32[]{:S(2)}, u32[]{:S(2)}) collective-permute-start(f32[4,1,512]{2,1,0:T(1,128)S(1)} %get-tuple-element.35), channel_id=1, source_target_pairs={{0,1},{1,0},{2,3},{3,2},{4,5},{5,4},{6,7},{7,6},{8,9},{9,8},{10,11... | collective-permute-start | bytes 24584 | tf_op jit(solution)/shard_map/ppermute | solution.py:31
  56.6 22.6 %collective-permute-start.14 = (bf16[4,128,512]{2,1,0:T(8,128)(2,1)S(1)}, bf16[4,128,512]{2,1,0:T(8,128)(2,1)S(1)}, u32[]{:S(2)}, u32[]{:S(2)}) collective-permute-start(bf16[4,128,512]{2,1,0:T(8,128)(2,1)S(1)} %get-tuple-element.30), channel_id=1, source_target_pairs={{0,1},{1,0},{2,3},{3,2},{4,5},{5,4},{6,7},{7,6},{8,9},{9,8},{10,11... | collective-permute-start | bytes 1572872 | tf_op jit(solution)/shard_map/ppermute | solution.py:31
  56.7 2.7 %collective-permute-start.19 = (f32[4,1,512]{2,1,0:T(1,128)S(1)}, f32[4,1,512]{2,1,0:T(1,128)S(1)}, u32[]{:S(2)}, u32[]{:S(2)}) collective-permute-start(f32[4,1,512]{2,1,0:T(1,128)S(1)} %add.30.refs_8_), channel_id=1, source_target_pairs={{0,2},{1,3},{2,0},{3,1},{4,6},{5,7},{6,4},{7,5},{8,10},{9,11},{10,... | collective-permute-start | bytes 24584 | tf_op jit(solution)/shard_map/ppermute | solution.py:31
  56.8 2.6 %collective-permute-start.20 = (f32[4,1,512]{2,1,0:T(1,128)S(1)}, f32[4,1,512]{2,1,0:T(1,128)S(1)}, u32[]{:S(2)}, u32[]{:S(2)}) collective-permute-start(f32[4,1,512]{2,1,0:T(1,128)S(1)} %add.30.refs_8_), channel_id=1, source_target_pairs={{0,4},{1,5},{2,6},{3,7},{4,0},{5,1},{6,2},{7,3},{8,12},{9,13},{10,... | collective-permute-start | bytes 24584 | tf_op jit(solution)/shard_map/ppermute | solution.py:31
  56.8 3.6 %collective-permute-start.21 = (f32[4,1,512]{2,1,0:T(1,128)S(1)}, f32[4,1,512]{2,1,0:T(1,128)S(1)}, u32[]{:S(2)}, u32[]{:S(2)}) collective-permute-start(f32[4,1,512]{2,1,0:T(1,128)S(1)} %add.30.refs_8_), channel_id=1, source_target_pairs={{0,6},{1,7},{2,4},{3,5},{4,2},{5,3},{6,0},{7,1},{8,14},{9,15},{10,... | collective-permute-start | bytes 24584 | tf_op jit(solution)/shard_map/ppermute | solution.py:31
  79.2 8.5 %copy-start = (bf16[64,512]{1,0:T(8,128)(2,1)S(1)}, bf16[64,512]{1,0:T(8,128)(2,1)}, u32[]{:S(2)}) copy-start(bf16[64,512]{1,0:T(8,128)(2,1)} %refs_0_.1) | copy-start | bytes 196612
  79.4 5.6 %collective-permute-start.17 = (bf16[128,512]{1,0:T(8,128)(2,1)S(1)}, bf16[128,512]{1,0:T(8,128)(2,1)S(1)}, u32[]{:S(2)}, u32[]{:S(2)}) collective-permute-start(bf16[128,512]{1,0:T(8,128)(2,1)S(1)} %get-tuple-element.42), channel_id=1, source_target_pairs={{0,6},{1,7},{2,4},{3,5},{4,2},{5,3},{6,0},{7,1},{8,14},{9,15},{10,... | collective-permute-start | bytes 393224 | tf_op jit(solution)/shard_map/ppermute | solution.py:31
  79.5 8.1 %collective-permute-start.16 = (bf16[128,512]{1,0:T(8,128)(2,1)S(1)}, bf16[128,512]{1,0:T(8,128)(2,1)S(1)}, u32[]{:S(2)}, u32[]{:S(2)}) collective-permute-start(bf16[128,512]{1,0:T(8,128)(2,1)S(1)} %get-tuple-element.43), channel_id=1, source_target_pairs={{0,4},{1,5},{2,6},{3,7},{4,0},{5,1},{6,2},{7,3},{8,12},{9,13},{10,... | collective-permute-start | bytes 393224 | tf_op jit(solution)/shard_map/ppermute | solution.py:31
  79.6 8.0 %collective-permute-start.15 = (bf16[128,512]{1,0:T(8,128)(2,1)S(1)}, bf16[128,512]{1,0:T(8,128)(2,1)S(1)}, u32[]{:S(2)}, u32[]{:S(2)}) collective-permute-start(bf16[128,512]{1,0:T(8,128)(2,1)S(1)} %get-tuple-element.41), channel_id=1, source_target_pairs={{0,2},{1,3},{2,0},{3,1},{4,6},{5,7},{6,4},{7,5},{8,10},{9,11},{10,... | collective-permute-start | bytes 393224 | tf_op jit(solution)/shard_map/ppermute | solution.py:31

commit v6 on v5

--- a/solution.py
+++ b/solution.py
@@ -536,34 +536,8 @@
         dw_ref[at, :] = ((dw - c * along) * (inv * (1.0 / sharpness))).astype(bf16)
         dw_ref[pl.ds(pl.multiple_of(done + size, size), 2 * LANES), :] = jnp.zeros((2 * LANES, width), bf16)
 
-    def one(done):
-        fetch(done)[1].wait()
-
-        @pl.when(used - done > step // 2)
-        def _():
-            work(done, step)
-
-        @pl.when(used - done <= step // 2)
-        def _():
-            work(done, step // 2)
-
-        @pl.when(done + 2 * step < used)
-        def _():
-            fetch(done + 2 * step)[1].start()
-
-        return done + step
-
-    def group(g, done):
-        done = lax.while_loop(lambda d: d < off_ref[0, blocks + (g + 1) * per - 1], one, done)
-        for copy in ins(g):
-            copy.wait()
+    def apply(g):
         slot = lax.bitwise_and(g, OUT - 1)
-
-        @pl.when(g >= OUT)
-        def _():
-            for copy in outs(g - OUT):
-                copy.wait()
-
         lane = iota((LANES, LANES), 1)
         for k in range(per):
             base = pl.multiple_of(lax.shift_left(lax.shift_right_logical(off_ref[0, g * per + k], 4), 4), 16)
@@ -576,15 +550,68 @@
             m = momentum_rate * m_buf[mine, :] + dw + weight_decay * c
             m_new[slot, to, :] = m
             c_new[slot, to, :] = (c - learn_rate * m).astype(bf16)
+
+    def ready(g):
+        for copy in ins(g):
+            copy.wait()
+
+        @pl.when(g >= OUT)
+        def _():
+            for copy in outs(g - OUT):
+                copy.wait()
+
+    def send(g):
         for copy in outs(g):
             copy.start()
-        return done
+
+    def ahead(done):
+        @pl.when(done + 2 * step < used)
+        def _():
+            fetch(done + 2 * step)[1].start()
 
     @pl.when(used == 0)
     def _():
         dw_ref[: 2 * LANES, :] = jnp.zeros((2 * LANES, width), bf16)
 
-    lax.fori_loop(0, groups, group, 0)
+    def turn(state):
+        done, g = state
+        can = off_ref[0, blocks + (g + 1) * per - 1] <= done
+        full = used - done > step // 2
+        both = can & full
+
+        @pl.when(both)
+        def _():
+            ready(g)
+            fetch(done)[1].wait()
+            apply(g)
+            work(done, step)
+            send(g)
+            ahead(done)
+
+        @pl.when(can & jnp.logical_not(full))
+        def _():
+            ready(g)
+            apply(g)
+            send(g)
+
+        @pl.when(jnp.logical_not(can))
+        def _():
+            fetch(done)[1].wait()
+
+            @pl.when(full)
+            def _():
+                work(done, step)
+
+            @pl.when(jnp.logical_not(full))
+            def _():
+                work(done, step // 2)
+
+            ahead(done)
+
+        tile_done = both | jnp.logical_not(can)
+        return done + jnp.where(tile_done, step, 0), g + jnp.where(can, 1, 0)
+
+    lax.while_loop(lambda state: state[1] < groups, turn, (jnp.int32(0), jnp.int32(0)))
     for g in range(max(0, groups - OUT), groups):
         for copy in outs(g):
             copy.wait()
@@ -658,7 +685,7 @@
     me = shard.astype(jnp.int32).reshape(1)
     in_hbm = lambda x: pltpu.with_memory_space_constraint(x, pltpu.HBM)
     row, rep, cnt, off, known, table = prepare(me, early, early_away, dims)
-    what, raw, num = pack(off, row, cnt, in_hbm(centres), min(1024, home_rows))
+    what, raw, num = pack(off, row, cnt, in_hbm(centres), min(2048, home_rows))
     at = label_places(me, known, table, [told] + from_z, chips, dims)
     tile = min(512, home_rows)
     w, own_den, turned, x = logits(off, early, early_away, late, late_away, what, num, at, tile, home_rows)

time: 89.7 us -> 89.1 us (level)
  transfers between devices with their start and end apart: 22 -> 22, of which waited for: 5 -> 5; matrix products, arithmetic and copies ran while one was open for 1% -> 1% of each run, Pallas kernels for 40% -> 39%
where the time goes in v6:
time: 89.1 us; the launch traced here: 87.9 us
  Pallas kernels  45.7 us (51%)
  starting transfers between devices  28.3 us (32%)
  waiting for transfers between devices  10.7 us (12%)
  other arithmetic  2.24 us (3%)
  between operations  0.9 us (1%)
    ppermute x19, starting transfers between devices, swap(): return lax.ppermute(x, axis_name, [(i, i ^ m) for i in range(n)])  24.4 us
    pallas_call x1, Pallas kernels, update(): pl.pallas_call(lambda *refs: update_kernel(chunks, step, tile, *refs), in...  18.4 us
    pallas_call x1, Pallas kernels, logits(): pl.pallas_call(lambda *refs: logits_kernel(chunks, tile, *refs), in_specs...  10.3 us
    ppermute x19, waiting for transfers between devices, swap(): return lax.ppermute(x, axis_name, [(i, i ^ m) for i in range(n)])  6.39 us
    pallas_call x1, Pallas kernels, row_parts(): pl.pallas_call(lambda *refs: rows_kernel(chunks, *refs), grid_spec=pltpu....  5.99 us
    pallas_call x1, Pallas kernels, pack(): pl.pallas_call(pack_kernel, grid=(classes // tile,), in_specs=[pl.BlockSp...  5.59 us
    ppermute x3, waiting for transfers between devices, shift(): return lax.ppermute(x, axis_name, [(i, (i + m) % n) for i in range(n)])  4.27 us
    ppermute x3, starting transfers between devices, shift(): return lax.ppermute(x, axis_name, [(i, (i + m) % n) for i in range(n)])  3.97 us
  transfers between devices with their start and end apart: 22, of which 5 were waited for; matrix products, arithmetic and copies ran while one was open for 1% of the time, Pallas kernels for 39%

profile of v6, /device:TPU:1, one launch (start us, length us, event | category | flops | bytes accessed | tf_op | source)
XLA Modules:
  0.0 87.9 jit_solution(13091513307968855780)
XLA Ops:
  0.6 1.0 %tell.1.refs_3_ = bf16[80,512]{1,0:T(8,128)(2,1)S(1)} custom-call(bf16[64,512]{1,0:T(8,128)(2,1)} %refs_0_.1, s32[16,128]{1,0:T(8,128)} %bitcast.34, s32[16,128]{1,0:T(8,128)} %bitcast.35, s32[4,128]{1,0:T(4,128)} %bitcast.36), custom_call_target="tpu_custom_call" | custom-call | tf_op jit(solution)/shard_map/tell/pallas_call | solution.py:89
  1.6 3.0 %collective-permute-start.2 = (bf16[80,512]{1,0:T(8,128)(2,1)S(1)}, bf16[80,512]{1,0:T(8,128)(2,1)S(1)}, u32[]{:S(2)}, u32[]{:S(2)}) collective-permute-start(bf16[80,512]{1,0:T(8,128)(2,1)S(1)} %tell.1.refs_3_), channel_id=1, source_target_pairs={{0,6},{1,7},{2,4},{3,5},{4,2},{5,3},{6,0},{7,1},{8,14},{9,15},{10,... | collective-permute-start | bytes 245768 | tf_op jit(solution)/shard_map/ppermute | solution.py:31
  4.7 0.2 collective-permute-start.1
  4.9 0.1 collective-permute-start
  5.0 1.4 %collective-permute-start.4 = (bf16[80,512]{1,0:T(8,128)(2,1)S(1)}, bf16[80,512]{1,0:T(8,128)(2,1)S(1)}, u32[]{:S(2)}, u32[]{:S(2)}) collective-permute-start(bf16[80,512]{1,0:T(8,128)(2,1)S(1)} %tell.1.refs_3_), channel_id=1, source_target_pairs={{0,8},{8,16},{16,24},{24,0},{1,9},{9,17},{17,25},{25,1},{2,10},{10... | collective-permute-start | bytes 245768 | tf_op jit(solution)/shard_map/ppermute | solution.py:36
  6.5 2.0 %collective-permute-start.5 = (bf16[80,512]{1,0:T(8,128)(2,1)S(1)}, bf16[80,512]{1,0:T(8,128)(2,1)S(1)}, u32[]{:S(2)}, u32[]{:S(2)}) collective-permute-start(bf16[80,512]{1,0:T(8,128)(2,1)S(1)} %tell.1.refs_3_), channel_id=1, source_target_pairs={{0,24},{8,0},{16,8},{24,16},{1,25},{9,1},{17,9},{25,17},{2,26},{10... | collective-permute-start | bytes 245768 | tf_op jit(solution)/shard_map/ppermute | solution.py:36
  8.5 0.0 collective-permute-done.2
  8.5 0.5 collective-permute-start.6
  9.0 0.0 collective-permute-done.1
  9.0 0.1 collective-permute-done
  9.1 2.3 %collective-permute-start.3 = (bf16[4,80,512]{2,1,0:T(8,128)(2,1)S(1)}, bf16[4,80,512]{2,1,0:T(8,128)(2,1)S(1)}, u32[]{:S(2)}, u32[]{:S(2)}) collective-permute-start(bf16[4,80,512]{2,1,0:T(8,128)(2,1)S(1)} %pad_maximum_fusion.refs_1_), channel_id=1, source_target_pairs={{0,1},{1,0},{2,3},{3,2},{4,5},{5,4},{6,7},{7,6},{8,9},{9,8},{10,11... | collective-permute-start | bytes 983048 | tf_op jit(solution)/shard_map/ppermute | solution.py:31
  11.4 4.3 %collective-permute-done.6.refs_6_ = bf16[80,512]{1,0:T(8,128)(2,1)S(1)} collective-permute-done((bf16[80,512]{1,0:T(8,128)(2,1)S(1)}, bf16[80,512]{1,0:T(8,128)(2,1)S(1)}, u32[]{:S(2)}, u32[]{:S(2)}) %collective-permute-start.6) | collective-permute-done | bytes 81952 | tf_op jit(solution)/shard_map/ppermute | solution.py:36
  15.7 0.0 collective-permute-done.5.refs_5_
  15.7 0.0 collective-permute-done.4.refs_4_
  15.8 1.4 %collective-permute-start.7 = (bf16[3,64,512]{2,1,0:T(8,128)(2,1)S(1)}, bf16[3,64,512]{2,1,0:T(8,128)(2,1)S(1)}, u32[]{:S(2)}, u32[]{:S(2)}) collective-permute-start(bf16[3,64,512]{2,1,0:T(8,128)(2,1)S(1)} %pad_maximum_fusion.1.refs_6_), channel_id=1, source_target_pairs={{0,2},{1,3},{2,0},{3,1},{4,6},{5,7},{6,4},{7,5},{8,10},{9,11},{10,... | collective-permute-start | bytes 589832 | tf_op jit(solution)/shard_map/ppermute | solution.py:31
  17.2 1.2 %collective-permute-start.8 = (bf16[3,64,512]{2,1,0:T(8,128)(2,1)S(1)}, bf16[3,64,512]{2,1,0:T(8,128)(2,1)S(1)}, u32[]{:S(2)}, u32[]{:S(2)}) collective-permute-start(bf16[3,64,512]{2,1,0:T(8,128)(2,1)S(1)} %pad_maximum_fusion.1.refs_6_), channel_id=1, source_target_pairs={{0,4},{1,5},{2,6},{3,7},{4,0},{5,1},{6,2},{7,3},{8,12},{9,13},{10,... | collective-permute-start | bytes 589832 | tf_op jit(solution)/shard_map/ppermute | solution.py:31
  18.4 0.1 collective-permute-start.9
  18.5 2.6 %collective-permute-start.10 = (bf16[3,64,512]{2,1,0:T(8,128)(2,1)S(1)}, bf16[3,64,512]{2,1,0:T(8,128)(2,1)S(1)}, u32[]{:S(2)}, u32[]{:S(2)}) collective-permute-start(bf16[3,64,512]{2,1,0:T(8,128)(2,1)S(1)} %pad_maximum_fusion.1.refs_6_), channel_id=1, source_target_pairs={{0,1},{1,0},{2,3},{3,2},{4,5},{5,4},{6,7},{7,6},{8,9},{9,8},{10,11... | collective-permute-start | bytes 589832 | tf_op jit(solution)/shard_map/ppermute | solution.py:31
  21.1 0.0 collective-permute-done.7.refs_7_
  21.1 4.0 %collective-permute-start.11 = (bf16[3,64,512]{2,1,0:T(8,128)(2,1)S(1)}, bf16[3,64,512]{2,1,0:T(8,128)(2,1)S(1)}, u32[]{:S(2)}, u32[]{:S(2)}) collective-permute-start(bf16[3,64,512]{2,1,0:T(8,128)(2,1)S(1)} %collective-permute-done.7.refs_7_), channel_id=1, source_target_pairs={{0,1},{1,0},{2,3},{3,2},{4,5},{5,4},{6,7},{7,6},{8,9},{9,8},{10,11... | collective-permute-start | bytes 589832 | tf_op jit(solution)/shard_map/ppermute | solution.py:31
  25.0 0.0 collective-permute-done.8.refs_8_
  25.0 3.8 %collective-permute-start.12 = (bf16[3,64,512]{2,1,0:T(8,128)(2,1)S(1)}, bf16[3,64,512]{2,1,0:T(8,128)(2,1)S(1)}, u32[]{:S(2)}, u32[]{:S(2)}) collective-permute-start(bf16[3,64,512]{2,1,0:T(8,128)(2,1)S(1)} %collective-permute-done.8.refs_8_), channel_id=1, source_target_pairs={{0,1},{1,0},{2,3},{3,2},{4,5},{5,4},{6,7},{7,6},{8,9},{9,8},{10,11... | collective-permute-start | bytes 589832 | tf_op jit(solution)/shard_map/ppermute | solution.py:31
  28.9 0.0 collective-permute-done.9.refs_9_
  28.9 0.0 collective-permute-start.13
  28.9 1.0 %fusion.3 = f32[64]{0:T(128)S(1)} fusion(bf16[64,512]{1,0:T(8,128)(2,1)} %refs_0_.1), kind=kLoop, calls=%fused_computation.9 | loop fusion | flops 98240 | bytes 65792 | tf_op jit(solution)/shard_map/reduce_sum | solution.py:708
  29.9 0.0 collective-permute-done.3.refs_2_
  29.9 3.0 %prep.1 = (s32[32,1,128]{2,1,0:T(1,128)S(1)}, s32[4096,128]{1,0:T(8,128)S(1)}, f32[4096,128]{1,0:T(8,128)S(1)}, s32[8,64]{1,0:T(8,128)S(1)}, s32[32,128]{1,0:T(8,128)S(1)}, /*index=5*/s32[128,128]{1,0:T(8,128)S(1)}) custom-call(s32[1]{0:T(128)} %bitcast.refs_0_, bf16[4,80,512]{2,1,0:T(8,128)(2,1)S(1)} %pad_maximum_fusion.refs_1_, ...), custom_call_target="tpu_custom_call" | custom-call | flops 268435456 | bytes 4194304 | tf_op jit(solution)/shard_map/prep/pallas_call | solution.py:186
  32.8 1.5 %places.1.refs_5_.refs_2_.refs_1_ = s32[4,1,512]{2,1,0:T(1,128)S(1)} custom-call(s32[1]{0:T(128)} %bitcast.refs_0_, s32[32,128]{1,0:T(8,128)S(1)} %get-tuple-element.25.refs_1_, s32[128,128]{1,0:T(8,128)S(1)} %get-tuple-element.26.refs_2_, bf16[80,512]{1,0:T(8,128)(2,1)S(1)} %tell.1.refs_3_, bf16[80,512]{1,0:T(8,128)(2,1)S(1)} %collective-permute-done.4.refs_4_, ...), custom_call_target="tpu_custom_call" | custom-call | flops 268435456 | bytes 131072 | tf_op jit(solution)/shard_map/places/pallas_call | solution.py:207
  34.3 5.6 %pack.1 = (bf16[4864,512]{1,0:T(8,128)(2,1)S(1)}, bf16[4864,512]{1,0:T(8,128)(2,1)S(1)}, f32[4864,128]{1,0:T(8,128)S(1)}) custom-call(s32[8,64]{1,0:T(8,128)S(1)} %get-tuple-element.21.off_ref.refs_0_, s32[32,1,128]{2,1,0:T(1,128)S(1)} %get-tuple-element.22.row_ref, f32[4096,128]{1,0:T(8,128)S(1)} %get-tuple-element.23.cnt_ref, bf16[4096,512]{1,0:T(8,128)(2,1)} %refs_4_.1), custom_call_target="tpu_custom_call" | custom-call | flops 1342177280 | bytes 8388608 | tf_op jit(solution)/shard_map/pack/pallas_call | solution.py:263
  39.9 0.0 collective-permute-done.10.refs_10_
  39.9 0.0 collective-permute-done.11.refs_11_
  39.9 0.0 collective-permute-done.12.refs_12_
  39.9 0.0 collective-permute-done.13.refs_13_
  39.9 10.3 %logits.1 = (bf16[4096,2048]{1,0:T(8,128)(2,1)}, f32[4,1,512]{2,1,0:T(1,128)S(1)}, f32[4,1,512]{2,1,0:T(1,128)S(1)}, bf16[2048,512]{1,0:T(8,128)(2,1)S(1)}) custom-call(s32[8,64]{1,0:T(8,128)S(1)} %get-tuple-element.21.off_ref.refs_0_, bf16[4,80,512]{2,1,0:T(8,128)(2,1)S(1)} %pad_maximum_fusion.refs_1_, ...), custom_call_target="tpu_custom_call" | custom-call | flops 4294967296 | bytes 10485760 | tf_op jit(solution)/shard_map/logits/pallas_call | solution.py:377
  50.2 0.1 collective-permute-start.18
  50.3 6.0 %rows.1 = (bf16[4,128,512]{2,1,0:T(8,128)(2,1)S(1)}, bf16[4,128,512]{2,1,0:T(8,128)(2,1)S(1)}) custom-call(s32[8,64]{1,0:T(8,128)S(1)} %get-tuple-element.21.off_ref.refs_0_, bf16[4864,512]{1,0:T(8,128)(2,1)S(1)} %get-tuple-element.24.refs_3_.refs_1_, s32[4,1,512]{2,1,0:T(1,128)S(1)} %places.1.refs_5_.refs_2_.refs_1_, ...), custom_call_target="tpu_custom_call" | custom-call | flops 2147483648 | bytes 4980736 | tf_op jit(solution)/shard_map/rows/pallas_call | solution.py:446
  56.3 0.1 collective-permute-start.14
  56.4 0.0 collective-permute-done.18
  56.4 0.1 collective-permute-start.19
  56.5 0.1 collective-permute-start.20
  56.5 2.6 %collective-permute-start.21 = (f32[4,1,512]{2,1,0:T(1,128)S(1)}, f32[4,1,512]{2,1,0:T(1,128)S(1)}, u32[]{:S(2)}, u32[]{:S(2)}) collective-permute-start(f32[4,1,512]{2,1,0:T(1,128)S(1)} %add.30.refs_8_), channel_id=1, source_target_pairs={{0,6},{1,7},{2,4},{3,5},{4,2},{5,3},{6,0},{7,1},{8,14},{9,15},{10,... | collective-permute-start | bytes 24584 | tf_op jit(solution)/shard_map/ppermute | solution.py:31
  59.1 0.0 collective-permute-done.19.refs_9_
  59.1 0.0 collective-permute-done.20.refs_10_
  59.1 1.0 %collective-permute-done.21.refs_11_ = f32[4,1,512]{2,1,0:T(1,128)S(1)} collective-permute-done((f32[4,1,512]{2,1,0:T(1,128)S(1)}, f32[4,1,512]{2,1,0:T(1,128)S(1)}, u32[]{:S(2)}, u32[]{:S(2)}) %collective-permute-start.21) | collective-permute-done | bytes 8224 | tf_op jit(solution)/shard_map/ppermute | solution.py:31
  60.1 18.4 %update.1 = (f32[4096,512]{1,0:T(8,128)}, bf16[4096,512]{1,0:T(8,128)(2,1)}, f32[1,512]{1,0:T(1,128)S(1)}) custom-call(s32[8,64]{1,0:T(8,128)S(1)} %get-tuple-element.21.off_ref.refs_0_, s32[4,1,512]{2,1,0:T(1,128)S(1)} %places.1.refs_5_.refs_2_.refs_1_, s32[4096,128]{1,0:T(8,128)S(1)} %get-tuple-element.31.refs_2_, ...), custom_call_target="tpu_custom_call" | custom-call | flops 4294967296 | bytes 33554432 | tf_op jit(solution)/shard_map/update/pallas_call | solution.py:626
  78.6 0.0 copy-start
  78.6 0.0 collective-permute-done.14
  78.6 0.2 fusion.5
  78.8 0.1 collective-permute-start.17
  78.9 0.1 collective-permute-start.16
  79.0 2.6 %collective-permute-start.15 = (bf16[128,512]{1,0:T(8,128)(2,1)S(1)}, bf16[128,512]{1,0:T(8,128)(2,1)S(1)}, u32[]{:S(2)}, u32[]{:S(2)}) collective-permute-start(bf16[128,512]{1,0:T(8,128)(2,1)S(1)} %get-tuple-element.41), channel_id=1, source_target_pairs={{0,2},{1,3},{2,0},{3,1},{4,6},{5,7},{6,4},{7,5},{8,10},{9,11},{10,... | collective-permute-start | bytes 393224 | tf_op jit(solution)/shard_map/ppermute | solution.py:31
  81.5 3.1 %collective-permute-done.17 = bf16[128,512]{1,0:T(8,128)(2,1)S(1)} collective-permute-done((bf16[128,512]{1,0:T(8,128)(2,1)S(1)}, bf16[128,512]{1,0:T(8,128)(2,1)S(1)}, u32[]{:S(2)}, u32[]{:S(2)}) %collective-permute-start.17) | collective-permute-done | bytes 131104 | tf_op jit(solution)/shard_map/ppermute | solution.py:31
  84.6 2.2 %collective-permute-done.16 = bf16[128,512]{1,0:T(8,128)(2,1)S(1)} collective-permute-done((bf16[128,512]{1,0:T(8,128)(2,1)S(1)}, bf16[128,512]{1,0:T(8,128)(2,1)S(1)}, u32[]{:S(2)}, u32[]{:S(2)}) %collective-permute-start.16) | collective-permute-done | bytes 131104 | tf_op jit(solution)/shard_map/ppermute | solution.py:31
  86.8 0.0 collective-permute-done.15
  86.8 0.1 fusion.2
  86.9 0.0 copy-done
  86.9 0.2 multiply_reduce_fusion
  87.1 0.8 subtract_divide_fusion
  (9 shorter events, 0.1 us)
Async XLA Ops:
  1.6 6.9 %collective-permute-start.2 = (bf16[80,512]{1,0:T(8,128)(2,1)S(1)}, bf16[80,512]{1,0:T(8,128)(2,1)S(1)}, u32[]{:S(2)}, u32[]{:S(2)}) collective-permute-start(bf16[80,512]{1,0:T(8,128)(2,1)S(1)} %tell.1.refs_3_), channel_id=1, source_target_pairs={{0,6},{1,7},{2,4},{3,5},{4,2},{5,3},{6,0},{7,1},{8,14},{9,15},{10,... | collective-permute-start | bytes 245768 | tf_op jit(solution)/shard_map/ppermute | solution.py:31
  4.7 4.3 %collective-permute-start.1 = (bf16[80,512]{1,0:T(8,128)(2,1)S(1)}, bf16[80,512]{1,0:T(8,128)(2,1)S(1)}, u32[]{:S(2)}, u32[]{:S(2)}) collective-permute-start(bf16[80,512]{1,0:T(8,128)(2,1)S(1)} %tell.1.refs_3_), channel_id=1, source_target_pairs={{0,4},{1,5},{2,6},{3,7},{4,0},{5,1},{6,2},{7,3},{8,12},{9,13},{10,... | collective-permute-start | bytes 245768 | tf_op jit(solution)/shard_map/ppermute | solution.py:31
  4.9 4.2 %collective-permute-start = (bf16[80,512]{1,0:T(8,128)(2,1)S(1)}, bf16[80,512]{1,0:T(8,128)(2,1)S(1)}, u32[]{:S(2)}, u32[]{:S(2)}) collective-permute-start(bf16[80,512]{1,0:T(8,128)(2,1)S(1)} %tell.1.refs_3_), channel_id=1, source_target_pairs={{0,2},{1,3},{2,0},{3,1},{4,6},{5,7},{6,4},{7,5},{8,10},{9,11},{10,... | collective-permute-start | bytes 245768 | tf_op jit(solution)/shard_map/ppermute | solution.py:31
  5.0 10.7 %collective-permute-start.4 = (bf16[80,512]{1,0:T(8,128)(2,1)S(1)}, bf16[80,512]{1,0:T(8,128)(2,1)S(1)}, u32[]{:S(2)}, u32[]{:S(2)}) collective-permute-start(bf16[80,512]{1,0:T(8,128)(2,1)S(1)} %tell.1.refs_3_), channel_id=1, source_target_pairs={{0,8},{8,16},{16,24},{24,0},{1,9},{9,17},{17,25},{25,1},{2,10},{10... | collective-permute-start | bytes 245768 | tf_op jit(solution)/shard_map/ppermute | solution.py:36
  6.5 9.2 %collective-permute-start.5 = (bf16[80,512]{1,0:T(8,128)(2,1)S(1)}, bf16[80,512]{1,0:T(8,128)(2,1)S(1)}, u32[]{:S(2)}, u32[]{:S(2)}) collective-permute-start(bf16[80,512]{1,0:T(8,128)(2,1)S(1)} %tell.1.refs_3_), channel_id=1, source_target_pairs={{0,24},{8,0},{16,8},{24,16},{1,25},{9,1},{17,9},{25,17},{2,26},{10... | collective-permute-start | bytes 245768 | tf_op jit(solution)/shard_map/ppermute | solution.py:36
  8.5 7.2 %collective-permute-start.6 = (bf16[80,512]{1,0:T(8,128)(2,1)S(1)}, bf16[80,512]{1,0:T(8,128)(2,1)S(1)}, u32[]{:S(2)}, u32[]{:S(2)}) collective-permute-start(bf16[80,512]{1,0:T(8,128)(2,1)S(1)} %tell.1.refs_3_), channel_id=1, source_target_pairs={{0,16},{8,24},{16,0},{24,8},{1,17},{9,25},{17,1},{25,9},{2,18},{10... | collective-permute-start | bytes 245768 | tf_op jit(solution)/shard_map/ppermute | solution.py:36
  9.1 20.7 %collective-permute-start.3 = (bf16[4,80,512]{2,1,0:T(8,128)(2,1)S(1)}, bf16[4,80,512]{2,1,0:T(8,128)(2,1)S(1)}, u32[]{:S(2)}, u32[]{:S(2)}) collective-permute-start(bf16[4,80,512]{2,1,0:T(8,128)(2,1)S(1)} %pad_maximum_fusion.refs_1_), channel_id=1, source_target_pairs={{0,1},{1,0},{2,3},{3,2},{4,5},{5,4},{6,7},{7,6},{8,9},{9,8},{10,11... | collective-permute-start | bytes 983048 | tf_op jit(solution)/shard_map/ppermute | solution.py:31
  15.8 5.3 %collective-permute-start.7 = (bf16[3,64,512]{2,1,0:T(8,128)(2,1)S(1)}, bf16[3,64,512]{2,1,0:T(8,128)(2,1)S(1)}, u32[]{:S(2)}, u32[]{:S(2)}) collective-permute-start(bf16[3,64,512]{2,1,0:T(8,128)(2,1)S(1)} %pad_maximum_fusion.1.refs_6_), channel_id=1, source_target_pairs={{0,2},{1,3},{2,0},{3,1},{4,6},{5,7},{6,4},{7,5},{8,10},{9,11},{10,... | collective-permute-start | bytes 589832 | tf_op jit(solution)/shard_map/ppermute | solution.py:31
  17.2 7.9 %collective-permute-start.8 = (bf16[3,64,512]{2,1,0:T(8,128)(2,1)S(1)}, bf16[3,64,512]{2,1,0:T(8,128)(2,1)S(1)}, u32[]{:S(2)}, u32[]{:S(2)}) collective-permute-start(bf16[3,64,512]{2,1,0:T(8,128)(2,1)S(1)} %pad_maximum_fusion.1.refs_6_), channel_id=1, source_target_pairs={{0,4},{1,5},{2,6},{3,7},{4,0},{5,1},{6,2},{7,3},{8,12},{9,13},{10,... | collective-permute-start | bytes 589832 | tf_op jit(solution)/shard_map/ppermute | solution.py:31
  18.4 10.5 %collective-permute-start.9 = (bf16[3,64,512]{2,1,0:T(8,128)(2,1)S(1)}, bf16[3,64,512]{2,1,0:T(8,128)(2,1)S(1)}, u32[]{:S(2)}, u32[]{:S(2)}) collective-permute-start(bf16[3,64,512]{2,1,0:T(8,128)(2,1)S(1)} %pad_maximum_fusion.1.refs_6_), channel_id=1, source_target_pairs={{0,6},{1,7},{2,4},{3,5},{4,2},{5,3},{6,0},{7,1},{8,14},{9,15},{10,... | collective-permute-start | bytes 589832 | tf_op jit(solution)/shard_map/ppermute | solution.py:31
  18.5 21.4 %collective-permute-start.10 = (bf16[3,64,512]{2,1,0:T(8,128)(2,1)S(1)}, bf16[3,64,512]{2,1,0:T(8,128)(2,1)S(1)}, u32[]{:S(2)}, u32[]{:S(2)}) collective-permute-start(bf16[3,64,512]{2,1,0:T(8,128)(2,1)S(1)} %pad_maximum_fusion.1.refs_6_), channel_id=1, source_target_pairs={{0,1},{1,0},{2,3},{3,2},{4,5},{5,4},{6,7},{7,6},{8,9},{9,8},{10,11... | collective-permute-start | bytes 589832 | tf_op jit(solution)/shard_map/ppermute | solution.py:31
  21.1 18.8 %collective-permute-start.11 = (bf16[3,64,512]{2,1,0:T(8,128)(2,1)S(1)}, bf16[3,64,512]{2,1,0:T(8,128)(2,1)S(1)}, u32[]{:S(2)}, u32[]{:S(2)}) collective-permute-start(bf16[3,64,512]{2,1,0:T(8,128)(2,1)S(1)} %collective-permute-done.7.refs_7_), channel_id=1, source_target_pairs={{0,1},{1,0},{2,3},{3,2},{4,5},{5,4},{6,7},{7,6},{8,9},{9,8},{10,11... | collective-permute-start | bytes 589832 | tf_op jit(solution)/shard_map/ppermute | solution.py:31
  25.0 14.9 %collective-permute-start.12 = (bf16[3,64,512]{2,1,0:T(8,128)(2,1)S(1)}, bf16[3,64,512]{2,1,0:T(8,128)(2,1)S(1)}, u32[]{:S(2)}, u32[]{:S(2)}) collective-permute-start(bf16[3,64,512]{2,1,0:T(8,128)(2,1)S(1)} %collective-permute-done.8.refs_8_), channel_id=1, source_target_pairs={{0,1},{1,0},{2,3},{3,2},{4,5},{5,4},{6,7},{7,6},{8,9},{9,8},{10,11... | collective-permute-start | bytes 589832 | tf_op jit(solution)/shard_map/ppermute | solution.py:31
  28.9 11.0 %collective-permute-start.13 = (bf16[3,64,512]{2,1,0:T(8,128)(2,1)S(1)}, bf16[3,64,512]{2,1,0:T(8,128)(2,1)S(1)}, u32[]{:S(2)}, u32[]{:S(2)}) collective-permute-start(bf16[3,64,512]{2,1,0:T(8,128)(2,1)S(1)} %collective-permute-done.9.refs_9_), channel_id=1, source_target_pairs={{0,1},{1,0},{2,3},{3,2},{4,5},{5,4},{6,7},{7,6},{8,9},{9,8},{10,11... | collective-permute-start | bytes 589832 | tf_op jit(solution)/shard_map/ppermute | solution.py:31
  50.2 6.2 %collective-permute-start.18 = (f32[4,1,512]{2,1,0:T(1,128)S(1)}, f32[4,1,512]{2,1,0:T(1,128)S(1)}, u32[]{:S(2)}, u32[]{:S(2)}) collective-permute-start(f32[4,1,512]{2,1,0:T(1,128)S(1)} %get-tuple-element.35), channel_id=1, source_target_pairs={{0,1},{1,0},{2,3},{3,2},{4,5},{5,4},{6,7},{7,6},{8,9},{9,8},{10,11... | collective-permute-start | bytes 24584 | tf_op jit(solution)/shard_map/ppermute | solution.py:31
  56.3 22.3 %collective-permute-start.14 = (bf16[4,128,512]{2,1,0:T(8,128)(2,1)S(1)}, bf16[4,128,512]{2,1,0:T(8,128)(2,1)S(1)}, u32[]{:S(2)}, u32[]{:S(2)}) collective-permute-start(bf16[4,128,512]{2,1,0:T(8,128)(2,1)S(1)} %get-tuple-element.30), channel_id=1, source_target_pairs={{0,1},{1,0},{2,3},{3,2},{4,5},{5,4},{6,7},{7,6},{8,9},{9,8},{10,11... | collective-permute-start | bytes 1572872 | tf_op jit(solution)/shard_map/ppermute | solution.py:31
  56.4 2.7 %collective-permute-start.19 = (f32[4,1,512]{2,1,0:T(1,128)S(1)}, f32[4,1,512]{2,1,0:T(1,128)S(1)}, u32[]{:S(2)}, u32[]{:S(2)}) collective-permute-start(f32[4,1,512]{2,1,0:T(1,128)S(1)} %add.30.refs_8_), channel_id=1, source_target_pairs={{0,2},{1,3},{2,0},{3,1},{4,6},{5,7},{6,4},{7,5},{8,10},{9,11},{10,... | collective-permute-start | bytes 24584 | tf_op jit(solution)/shard_map/ppermute | solution.py:31
  56.5 2.6 %collective-permute-start.20 = (f32[4,1,512]{2,1,0:T(1,128)S(1)}, f32[4,1,512]{2,1,0:T(1,128)S(1)}, u32[]{:S(2)}, u32[]{:S(2)}) collective-permute-start(f32[4,1,512]{2,1,0:T(1,128)S(1)} %add.30.refs_8_), channel_id=1, source_target_pairs={{0,4},{1,5},{2,6},{3,7},{4,0},{5,1},{6,2},{7,3},{8,12},{9,13},{10,... | collective-permute-start | bytes 24584 | tf_op jit(solution)/shard_map/ppermute | solution.py:31
  56.5 3.6 %collective-permute-start.21 = (f32[4,1,512]{2,1,0:T(1,128)S(1)}, f32[4,1,512]{2,1,0:T(1,128)S(1)}, u32[]{:S(2)}, u32[]{:S(2)}) collective-permute-start(f32[4,1,512]{2,1,0:T(1,128)S(1)} %add.30.refs_8_), channel_id=1, source_target_pairs={{0,6},{1,7},{2,4},{3,5},{4,2},{5,3},{6,0},{7,1},{8,14},{9,15},{10,... | collective-permute-start | bytes 24584 | tf_op jit(solution)/shard_map/ppermute | solution.py:31
  78.6 8.3 %copy-start = (bf16[64,512]{1,0:T(8,128)(2,1)S(1)}, bf16[64,512]{1,0:T(8,128)(2,1)}, u32[]{:S(2)}) copy-start(bf16[64,512]{1,0:T(8,128)(2,1)} %refs_0_.1) | copy-start | bytes 196612
  78.8 5.8 %collective-permute-start.17 = (bf16[128,512]{1,0:T(8,128)(2,1)S(1)}, bf16[128,512]{1,0:T(8,128)(2,1)S(1)}, u32[]{:S(2)}, u32[]{:S(2)}) collective-permute-start(bf16[128,512]{1,0:T(8,128)(2,1)S(1)} %get-tuple-element.42), channel_id=1, source_target_pairs={{0,6},{1,7},{2,4},{3,5},{4,2},{5,3},{6,0},{7,1},{8,14},{9,15},{10,... | collective-permute-start | bytes 393224 | tf_op jit(solution)/shard_map/ppermute | solution.py:31
  78.9 7.9 %collective-permute-start.16 = (bf16[128,512]{1,0:T(8,128)(2,1)S(1)}, bf16[128,512]{1,0:T(8,128)(2,1)S(1)}, u32[]{:S(2)}, u32[]{:S(2)}) collective-permute-start(bf16[128,512]{1,0:T(8,128)(2,1)S(1)} %get-tuple-element.43), channel_id=1, source_target_pairs={{0,4},{1,5},{2,6},{3,7},{4,0},{5,1},{6,2},{7,3},{8,12},{9,13},{10,... | collective-permute-start | bytes 393224 | tf_op jit(solution)/shard_map/ppermute | solution.py:31
  79.0 7.8 %collective-permute-start.15 = (bf16[128,512]{1,0:T(8,128)(2,1)S(1)}, bf16[128,512]{1,0:T(8,128)(2,1)S(1)}, u32[]{:S(2)}, u32[]{:S(2)}) collective-permute-start(bf16[128,512]{1,0:T(8,128)(2,1)S(1)} %get-tuple-element.41), channel_id=1, source_target_pairs={{0,2},{1,3},{2,0},{3,1},{4,6},{5,7},{6,4},{7,5},{8,10},{9,11},{10,... | collective-permute-start | bytes 393224 | tf_op jit(solution)/shard_map/ppermute | solution.py:31
